TPU v7x, 32 devices: a whole 2x2x4 slice. The times are simulated.
32 devices in a mesh: lat: 8 (over z, y), lon: 4 (over x, core).
Axes of the slice: x: 2, y: 2, z: 4, core: 2. Of those that a mesh axis runs over, the one named last changes fastest.
Arguments:
- features: bfloat16 [256, 16, 512], P(None, 'lat', 'lon'), may hold values from -6 to 6
- weight: bfloat16 [9, 65536], P(None, ('lat', 'lon')), may hold values from -0.125 to 0.125
- tap_values: bfloat16 [16, 5, 33], replicated, may hold values from -3 to 3
- basis_index: int32 [16, 5, 33], replicated, may hold values from 0 to 8
- half_width: int32 [16], replicated, may hold values from 1 to 16, as said below
- cotangent: bfloat16 [256, 16, 512], P(None, 'lat', 'lon'), may hold values from -6 to 6
Outputs:
- output: bfloat16 [256, 16, 512], P(None, 'lat', 'lon')
- input_grad: bfloat16 [256, 16, 512], P(None, 'lat', 'lon')
- weight_grad: float32 [9, 65536], P(None, ('lat', 'lon'))
Inputs may be any that keep to these rules, and one draw needn't show every extreme that they name: `half_width`: the widest half-width is 16.
All inputs are finite; a program needn't handle non-finite values.
Results may differ from a plain program's by a relative error of at most 0.005.
Values may be sent and summed in bfloat16 or wider, within the bound.
No kernel may reach another device: no remote copies, remote signals or barrier semaphores. Data moves between devices by JAX's collectives and lax.ppermute only.
A program may use at most 64 MiB of HBM per device.

v0:
```python
import jax
import jax.numpy as jnp
from jax import lax
from jax.experimental import pallas as pl
from jax.experimental.pallas import tpu as pltpu
from jax.sharding import PartitionSpec as P

TILE = 32
SLOT = 64
VMEM = 60 * 1024 * 1024
NT = (((1,), (1,)), ((), ()))
TN = (((0,), (0,)), ((), ()))


def dot(a, b, dims=(((1,), (0,)), ((), ()))):
    return lax.dot_general(a, b, dims, preferred_element_type=jnp.float32)


def in_vmem(count):
    return [pl.BlockSpec(memory_space=pltpu.VMEM) for _ in range(count)]


def call(body, outs, *args, scratch=()):
    return pl.pallas_call(
        body,
        out_shape=[jax.ShapeDtypeStruct(s, d) for s, d in outs],
        in_specs=in_vmem(len(args)),
        out_specs=in_vmem(len(outs)),
        scratch_shapes=list(scratch),
        compiler_params=pltpu.CompilerParams(vmem_limit_bytes=VMEM),
    )(*args)


def band_of(taps, index, basis_count):
    parts = []
    for basis in range(basis_count):
        line = jnp.where(index == basis, taps, 0.0)
        pieces = []
        for first in range(0, line.shape[1], 128):
            piece = jnp.broadcast_to(line[:, first : first + 128], (TILE, 128))
            pieces.append(pltpu.roll(piece, 0, 1, stride=1, stride_axis=0))
        parts.append(jnp.concatenate(pieces, axis=1).astype(jnp.bfloat16))
    return jnp.concatenate(parts, axis=0)


def convolve(source, taps_ref, index_ref, out_ref, rows, cols, offsets, basis_count):
    for row in range(rows):
        band = band_of(taps_ref[row], index_ref[row], basis_count)[:, : offsets * SLOT]
        for first in range(0, cols, TILE):
            lines = [source(row + a, first) for a in range(offsets)]
            moved = dot(band, jnp.concatenate(lines, axis=0)).astype(jnp.bfloat16)
            for basis in range(basis_count):
                start = row * cols + first
                out_ref[basis, start : start + TILE, :] = moved[basis * TILE : (basis + 1) * TILE]


def forward_body(ext_ref, perm_ref, taps_ref, index_ref, cot_ref, out_ref, send_ref, keep_ref, ext_scr):
    ext_rows, width, channels = ext_ref.shape
    basis_count = out_ref.shape[0]
    rows, cols = cot_ref.shape[0], cot_ref.shape[1]
    pick = (lax.broadcasted_iota(jnp.int32, (channels, channels), 0) == perm_ref[...]).astype(jnp.bfloat16)
    for row in range(ext_rows):
        ext_scr[row] = dot(ext_ref[row], pick).astype(jnp.bfloat16)
    convolve(
        lambda row, first: ext_scr[row, first : first + SLOT, :],
        taps_ref, index_ref, out_ref, rows, cols, ext_rows - rows + 1, basis_count,
    )
    cot = cot_ref[...].reshape(rows * cols, cot_ref.shape[2])
    half = channels // 2
    for basis in range(basis_count):
        terms = dot(out_ref[basis], cot, TN)
        send_ref[basis] = terms[half:].astype(send_ref.dtype)
        keep_ref[basis] = terms[:half]


def spread_body(ext_ref, taps_ref, index_ref, out_ref):
    ext_rows = ext_ref.shape[0]
    rows = taps_ref.shape[0]
    cols = out_ref.shape[1] // rows
    convolve(
        lambda row, first: ext_ref[row, first : first + SLOT, :],
        taps_ref, index_ref, out_ref, rows, cols, ext_rows - rows + 1, out_ref.shape[0],
    )


def mix_body(weight_ref, basis_ref, spread_ref, perm_ref, out_ref, grad_ref):
    basis_count, channels, _ = weight_ref.shape
    out = jnp.zeros(out_ref.shape[::-1], jnp.float32)
    grad = jnp.zeros(grad_ref.shape[::-1], jnp.float32)
    for basis in range(basis_count):
        out = out + dot(basis_ref[basis], weight_ref[basis])
        grad = grad + dot(spread_ref[basis], weight_ref[basis], NT)
    row = lax.broadcasted_iota(jnp.int32, (channels, channels), 0)
    col = lax.broadcasted_iota(jnp.int32, (channels, channels), 1)
    same = (row == col).astype(jnp.bfloat16)
    pick = (row == perm_ref[...]).astype(jnp.bfloat16)
    out_ref[...] = dot(same, out.astype(jnp.bfloat16), NT).astype(jnp.bfloat16)
    grad_ref[...] = dot(pick, grad.astype(jnp.bfloat16), NT).astype(jnp.bfloat16)


def swap(array, axis, stride):
    return lax.ppermute(array, axis, [(i, i ^ stride) for i in range(lax.axis_size(axis))])


def with_halo(array, axis, dim, width, wrap):
    devices, length = lax.axis_size(axis), array.shape[dim]
    up = [(i, (i + 1) % devices) for i in range(devices if wrap else devices - 1)]
    down = [(j, i) for i, j in up]
    before = lax.ppermute(lax.slice_in_dim(array, length - width, length, axis=dim), axis, up)
    after = lax.ppermute(lax.slice_in_dim(array, 0, width, axis=dim), axis, down)
    return jnp.concatenate([before, array, after], axis=dim)


def strides(axis):
    return [1 << b for b in range(lax.axis_size(axis).bit_length() - 1)]


def tap_lines(tap_values, basis_index, half_width, flip):
    lat_rows, offsets, window = tap_values.shape
    reach = (offsets - 1) // 2
    far = jnp.abs(jnp.arange(window) - (window - 1) // 2)
    index = jnp.where(far[None, None, :] <= half_width[:, None, None], basis_index, -1)
    taps = tap_values.astype(jnp.float32)
    if flip:
        pad = ((reach, reach), (0, 0), (0, 0))
        taps, index = jnp.pad(taps, pad), jnp.pad(index, pad, constant_values=-1)
        picked = [(a, offsets - 1 - a) for a in range(offsets)]
        taps = jnp.stack([taps[a : a + lat_rows, b, ::-1] for a, b in picked], axis=1)
        index = jnp.stack([index[a : a + lat_rows, b, ::-1] for a, b in picked], axis=1)
    slots = offsets + offsets % 2
    fill = ((0, 0), (0, slots - offsets), (0, SLOT - window))
    taps, index = jnp.pad(taps, fill), jnp.pad(index, fill, constant_values=-1)
    return taps.reshape(lat_rows, 1, slots * SLOT), index.reshape(lat_rows, 1, slots * SLOT)


def local(features, weight, tap_values, basis_index, half_width, cotangent):
    channels, lat_rows, lon_cols = features.shape
    basis_count = weight.shape[0]
    reach = (tap_values.shape[1] - 1) // 2
    rim = (tap_values.shape[2] - 1) // 2
    lats, lons = lax.axis_size("lat"), lax.axis_size("lon")
    devices = lats * lons
    parts = max(1, devices // channels)
    device = lax.axis_index("lat") * lons + lax.axis_index("lon")
    bf16 = jnp.bfloat16

    steps = [("lon", s, s) for s in strides("lon")] + [("lat", s, s * lons) for s in strides("lat")]
    split = [step for step in steps if step[2] < parts]
    steps = [step for step in steps if step[2] >= parts]
    own = channels * parts // devices
    place = jnp.arange(channels)
    perm = place % own + (device // parts) * own
    for rank, (_, _, bit) in enumerate(steps):
        size = channels >> (rank + 1)
        perm = perm ^ jnp.where(place & size, bit // parts * own, 0)
    perm = perm.astype(jnp.int32).reshape(1, channels)

    taps, index = tap_lines(tap_values, basis_index, half_width, False)
    flip_taps, flip_index = tap_lines(tap_values, basis_index, half_width, True)
    first = lax.axis_index("lat") * lat_rows
    taps, index, flip_taps, flip_index = (
        lax.dynamic_slice_in_dim(t, first, lat_rows, 0) for t in (taps, index, flip_taps, flip_index)
    )

    feat = jnp.transpose(features, (1, 2, 0))
    cot = jnp.transpose(cotangent, (1, 2, 0))
    feat_ext = with_halo(with_halo(feat, "lat", 0, reach, False), "lon", 1, rim, True)
    cot_ext = with_halo(with_halo(cot, "lat", 0, reach, False), "lon", 1, rim, True)

    full = weight.reshape(basis_count, own, channels // parts)
    for axis, stride, _ in split:
        other = swap(full, axis, stride)
        mine = (lax.axis_index(axis) // stride) % 2 == 0
        full = jnp.where(mine, jnp.concatenate([full, other], 2), jnp.concatenate([other, full], 2))
    for axis, stride, _ in reversed(steps):
        full = jnp.concatenate([full, swap(full, axis, stride)], axis=1)

    cells = lat_rows * lon_cols
    half = channels // 2
    basis_out, send, keep = call(
        forward_body,
        [((basis_count, cells, channels), bf16), ((basis_count, half, channels), jnp.float32),
         ((basis_count, half, channels), jnp.float32)],
        feat_ext, perm, taps, index, cot,
        scratch=[pltpu.VMEM(feat_ext.shape, bf16)],
    )
    for rank, (axis, stride, _) in enumerate(steps):
        terms = (keep, swap(send, axis, stride))
        if rank + 1 < len(steps):
            size = keep.shape[1] // 2
            send = terms[0][:, size:] + terms[1][:, size:]
            keep = terms[0][:, :size] + terms[1][:, :size]
    grad = terms[0] + terms[1]
    for axis, stride, _ in reversed(split):
        size = grad.shape[2] // 2
        mine = (lax.axis_index(axis) // stride) % 2
        other = swap(lax.dynamic_slice_in_dim(grad, (1 - mine) * size, size, 2), axis, stride)
        grad = lax.dynamic_slice_in_dim(grad, mine * size, size, 2) + other
    weight_grad = grad.reshape(basis_count, weight.shape[1])

    (spread,) = call(spread_body, [((basis_count, cells, channels), bf16)], cot_ext, flip_taps, flip_index)
    output, input_grad = call(
        mix_body, [((channels, cells), bf16), ((channels, cells), bf16)], full, basis_out, spread, perm
    )
    shape = (channels, lat_rows, lon_cols)
    return output.reshape(shape), input_grad.reshape(shape), weight_grad


def solution(mesh):
    field = P(None, "lat", "lon")
    flat = P(None, ("lat", "lon"))
    return jax.shard_map(
        local,
        mesh=mesh,
        in_specs=(field, flat, P(), P(), P(), field),
        out_specs=(field, field, flat),
        check_vma=False,
    )
```

profile of v0, /device:TPU:0, one launch (start us, length us, event | category | flops | bytes accessed | tf_op | source)
XLA Modules:
  0.0 77.3 jit_solution(7072814009193097423)
XLA Ops:
  1.7 4.9 %collective-permute-start.5 = (bf16[2,128,256]{2,1,0:T(8,128)(2,1)S(1)}, bf16[2,128,256]{2,1,0:T(8,128)(2,1)S(1)}, u32[]{:S(2)}, u32[]{:S(2)}) collective-permute-start(bf16[2,128,256]{2,1,0:T(8,128)(2,1)S(1)} %bitcast.13), channel_id=1, source_target_pairs={{0,4},{4,8},{8,12},{12,16},{16,20},{20,24},{24,28},{1,5},{5,9},{9,... | collective-permute-start | bytes 393224 | tf_op jit(solution)/shard_map/ppermute | solution.py:109
  8.9 1.3 %collective-permute-start.10 = (bf16[2,128,256]{2,1,0:T(8,128)(2,1)S(1)}, bf16[2,128,256]{2,1,0:T(8,128)(2,1)S(1)}, u32[]{:S(2)}, u32[]{:S(2)}) collective-permute-start(bf16[2,128,256]{2,1,0:T(8,128)(2,1)S(1)} %bitcast.8), channel_id=1, source_target_pairs={{4,0},{8,4},{12,8},{16,12},{20,16},{24,20},{28,24},{5,1},{9,5},{13... | collective-permute-start | bytes 393224 | tf_op jit(solution)/shard_map/ppermute | solution.py:110
  10.2 5.2 %collective-permute-start.9 = (bf16[2,128,256]{2,1,0:T(8,128)(2,1)S(1)}, bf16[2,128,256]{2,1,0:T(8,128)(2,1)S(1)}, u32[]{:S(2)}, u32[]{:S(2)}) collective-permute-start(bf16[2,128,256]{2,1,0:T(8,128)(2,1)S(1)} %bitcast.9), channel_id=1, source_target_pairs={{0,4},{4,8},{8,12},{12,16},{16,20},{20,24},{24,28},{1,5},{5,9},{9,... | collective-permute-start | bytes 393224 | tf_op jit(solution)/shard_map/ppermute | solution.py:109
  16.9 4.0 %collective-permute-start = (bf16[9,8,256]{2,1,0:T(8,128)(2,1)S(1)}, bf16[9,8,256]{2,1,0:T(8,128)(2,1)S(1)}, u32[]{:S(2)}, u32[]{:S(2)}) collective-permute-start(bf16[9,8,256]{2,1,0:T(8,128)(2,1)S(1)} %get-tuple-element.31), channel_id=1, source_target_pairs={{0,16},{4,20},{8,24},{12,28},{16,0},{20,4},{24,8},{28,12},{1,17},{... | collective-permute-start | bytes 110600 | tf_op jit(solution)/shard_map/ppermute | solution.py:102
  23.9 1.7 %collective-permute-start.8 = (bf16[6,16,256]{2,1,0:T(8,128)(2,1)S(1)}, bf16[6,16,256]{2,1,0:T(8,128)(2,1)S(1)}, u32[]{:S(2)}, u32[]{:S(2)}) collective-permute-start(bf16[6,16,256]{2,1,0:T(8,128)(2,1)S(1)} %get-tuple-element.22), channel_id=1, source_target_pairs={{1,0},{2,1},{3,2},{0,3},{5,4},{6,5},{7,6},{4,7},{9,8},{10,9},{11,1... | collective-permute-start | bytes 147464 | tf_op jit(solution)/shard_map/ppermute | solution.py:110
  28.3 3.9 %shard_map.85 = (bf16[9,256,256]{2,1,0:T(8,128)(2,1)}, f32[9,128,256]{2,1,0:T(8,128)}, f32[9,128,256]{2,1,0:T(8,128)}) custom-call(bf16[6,160,256]{2,1,0:T(8,128)(2,1)} %pad_maximum_fusion.ext_ref, s32[1,256]{1,0:T(1,128)} %fusion.6.perm_ref, f32[2,1,384]{2,1,0:T(1,128)} %constant_dynamic-slice_fusion.3.taps_ref, ...), custom_call_target="tpu_custom_call" | custom-call | tf_op jit(solution)/shard_map/pallas_call | solution.py:24
  32.2 1.6 %collective-permute-start.13 = (f32[9,128,256]{2,1,0:T(8,128)}, f32[9,128,256]{2,1,0:T(8,128)S(1)}, u32[]{:S(2)}, u32[]{:S(2)}) collective-permute-start(f32[9,128,256]{2,1,0:T(8,128)} %get-tuple-element.12), channel_id=1, source_target_pairs={{0,1},{1,0},{2,3},{3,2},{4,5},{5,4},{6,7},{7,6},{8,9},{9,8},{10,11... | collective-permute-start | bytes 3538952 | tf_op jit(solution)/shard_map/ppermute | solution.py:102
  34.8 1.7 %collective-permute-done.13 = f32[9,128,256]{2,1,0:T(8,128)S(1)} collective-permute-done((f32[9,128,256]{2,1,0:T(8,128)}, f32[9,128,256]{2,1,0:T(8,128)S(1)}, u32[]{:S(2)}, u32[]{:S(2)}) %collective-permute-start.13) | collective-permute-done | bytes 1179680 | tf_op jit(solution)/shard_map/ppermute | solution.py:102
  36.5 1.5 %slice_add_fusion.1 = (f32[9,64,256]{2,1,0:T(8,128)S(1)}, f32[9,64,256]{2,1,0:T(8,128)S(1)}) fusion(f32[9,128,256]{2,1,0:T(8,128)S(1)} %collective-permute-done.13, f32[9,128,256]{2,1,0:T(8,128)} %get-tuple-element.11), kind=kLoop, calls=%fused_computation.1 | loop fusion | flops 294912 | bytes 3538944 | tf_op jit(solution)/shard_map/add | solution.py:192
  38.6 1.6 %collective-permute-start.1 = (bf16[9,16,256]{2,1,0:T(8,128)(2,1)S(1)}, bf16[9,16,256]{2,1,0:T(8,128)(2,1)S(1)}, u32[]{:S(2)}, u32[]{:S(2)}) collective-permute-start(bf16[9,16,256]{2,1,0:T(8,128)(2,1)S(1)} %pad_maximum_fusion.4), channel_id=1, source_target_pairs={{0,8},{4,12},{8,0},{12,4},{16,24},{20,28},{24,16},{28,20},{1,9},{5... | collective-permute-start | bytes 221192 | tf_op jit(solution)/shard_map/ppermute | solution.py:102
  40.8 2.2 %collective-permute-done.1 = bf16[9,16,256]{2,1,0:T(8,128)(2,1)S(1)} collective-permute-done((bf16[9,16,256]{2,1,0:T(8,128)(2,1)S(1)}, bf16[9,16,256]{2,1,0:T(8,128)(2,1)S(1)}, u32[]{:S(2)}, u32[]{:S(2)}) %collective-permute-start.1) | collective-permute-done | bytes 73760 | tf_op jit(solution)/shard_map/ppermute | solution.py:102
  43.0 1.6 %collective-permute-start.2 = (bf16[9,32,256]{2,1,0:T(8,128)(2,1)S(1)}, bf16[9,32,256]{2,1,0:T(8,128)(2,1)S(1)}, u32[]{:S(2)}, u32[]{:S(2)}) collective-permute-start(bf16[9,32,256]{2,1,0:T(8,128)(2,1)S(1)} %pad_maximum_fusion.3), channel_id=1, source_target_pairs={{0,4},{4,0},{8,12},{12,8},{16,20},{20,16},{24,28},{28,24},{1,5},{5... | collective-permute-start | bytes 442376 | tf_op jit(solution)/shard_map/ppermute | solution.py:102
  44.6 3.6 %collective-permute-done.2 = bf16[9,32,256]{2,1,0:T(8,128)(2,1)S(1)} collective-permute-done((bf16[9,32,256]{2,1,0:T(8,128)(2,1)S(1)}, bf16[9,32,256]{2,1,0:T(8,128)(2,1)S(1)}, u32[]{:S(2)}, u32[]{:S(2)}) %collective-permute-start.2) | collective-permute-done | bytes 147488 | tf_op jit(solution)/shard_map/ppermute | solution.py:102
  48.3 1.5 %collective-permute-start.3 = (bf16[9,64,256]{2,1,0:T(8,128)(2,1)S(1)}, bf16[9,64,256]{2,1,0:T(8,128)(2,1)S(1)}, u32[]{:S(2)}, u32[]{:S(2)}) collective-permute-start(bf16[9,64,256]{2,1,0:T(8,128)(2,1)S(1)} %pad_maximum_fusion.2), channel_id=1, source_target_pairs={{0,2},{1,3},{2,0},{3,1},{4,6},{5,7},{6,4},{7,5},{8,10},{9,11},{10,... | collective-permute-start | bytes 884744 | tf_op jit(solution)/shard_map/ppermute | solution.py:102
  49.8 4.4 %collective-permute-done.14 = f32[9,64,256]{2,1,0:T(8,128)S(1)} collective-permute-done((f32[9,64,256]{2,1,0:T(8,128)S(1)}, f32[9,64,256]{2,1,0:T(8,128)S(1)}, u32[]{:S(2)}, u32[]{:S(2)}) %collective-permute-start.14) | collective-permute-done | bytes 589856 | tf_op jit(solution)/shard_map/ppermute | solution.py:102
  54.3 1.6 %collective-permute-start.15 = (f32[9,32,256]{2,1,0:T(8,128)S(1)}, f32[9,32,256]{2,1,0:T(8,128)S(1)}, u32[]{:S(2)}, u32[]{:S(2)}) collective-permute-start(f32[9,32,256]{2,1,0:T(8,128)S(1)} %get-tuple-element.16), channel_id=1, source_target_pairs={{0,4},{4,0},{8,12},{12,8},{16,20},{20,16},{24,28},{28,24},{1,5},{5... | collective-permute-start | bytes 884744 | tf_op jit(solution)/shard_map/ppermute | solution.py:102
  56.0 1.7 %collective-permute-start.12 = (bf16[6,16,256]{2,1,0:T(8,128)(2,1)S(1)}, bf16[6,16,256]{2,1,0:T(8,128)(2,1)S(1)}, u32[]{:S(2)}, u32[]{:S(2)}) collective-permute-start(bf16[6,16,256]{2,1,0:T(8,128)(2,1)S(1)} %get-tuple-element.20), channel_id=1, source_target_pairs={{1,0},{2,1},{3,2},{0,3},{5,4},{6,5},{7,6},{4,7},{9,8},{10,9},{11,1... | collective-permute-start | bytes 147464 | tf_op jit(solution)/shard_map/ppermute | solution.py:110
  57.7 2.8 %collective-permute-done.3 = bf16[9,64,256]{2,1,0:T(8,128)(2,1)S(1)} collective-permute-done((bf16[9,64,256]{2,1,0:T(8,128)(2,1)S(1)}, bf16[9,64,256]{2,1,0:T(8,128)(2,1)S(1)}, u32[]{:S(2)}, u32[]{:S(2)}) %collective-permute-start.3) | collective-permute-done | bytes 294944 | tf_op jit(solution)/shard_map/ppermute | solution.py:102
  60.6 1.6 %collective-permute-done.15 = f32[9,32,256]{2,1,0:T(8,128)S(1)} collective-permute-done((f32[9,32,256]{2,1,0:T(8,128)S(1)}, f32[9,32,256]{2,1,0:T(8,128)S(1)}, u32[]{:S(2)}, u32[]{:S(2)}) %collective-permute-start.15) | collective-permute-done | bytes 294944 | tf_op jit(solution)/shard_map/ppermute | solution.py:102
  62.3 1.6 %collective-permute-start.16 = (f32[9,16,256]{2,1,0:T(8,128)S(1)}, f32[9,16,256]{2,1,0:T(8,128)S(1)}, u32[]{:S(2)}, u32[]{:S(2)}) collective-permute-start(f32[9,16,256]{2,1,0:T(8,128)S(1)} %get-tuple-element.18), channel_id=1, source_target_pairs={{0,8},{4,12},{8,0},{12,4},{16,24},{20,28},{24,16},{28,20},{1,9},{5... | collective-permute-start | bytes 442376 | tf_op jit(solution)/shard_map/ppermute | solution.py:102
  65.4 2.9 %shard_map.86.spread_ref = bf16[9,256,256]{2,1,0:T(8,128)(2,1)} custom-call(bf16[6,160,256]{2,1,0:T(8,128)(2,1)} %pad_maximum_fusion.1.ext_ref, f32[2,1,384]{2,1,0:T(1,128)} %constant_dynamic-slice_fusion.1.taps_ref, s32[2,1,384]{2,1,0:T(1,128)} %constant_dynamic-slice_fusion.index_ref), custom_call_target="tpu_custom_call" | custom-call | tf_op jit(solution)/shard_map/pallas_call | solution.py:24
  69.7 3.6 %shard_map.87 = (bf16[256,256]{1,0:T(8,128)(2,1)}, bf16[256,256]{1,0:T(8,128)(2,1)}) custom-call(bf16[9,256,256]{2,1,0:T(8,128)(2,1)} %copy-done.2, bf16[9,256,256]{2,1,0:T(8,128)(2,1)} %get-tuple-element.8.basis_ref, bf16[9,256,256]{2,1,0:T(8,128)(2,1)} %shard_map.86.spread_ref, s32[1,256]{1,0:T(1,128)} %fusion.6.perm_ref), custom_call_target="tpu_custom_call" | custom-call | tf_op jit(solution)/shard_map/pallas_call | solution.py:24
  73.4 1.6 %reshape.170 = bf16[256,2,128]{2,1,0:T(2,128)(2,1)} reshape(bf16[256,256]{1,0:T(8,128)(2,1)} %get-tuple-element.9) | data formatting | bytes 262144 | tf_op jit(solution)/shard_map/reshape | solution.py:206
  75.0 1.6 %reshape.171 = bf16[256,2,128]{2,1,0:T(2,128)(2,1)} reshape(bf16[256,256]{1,0:T(8,128)(2,1)} %get-tuple-element.10) | data formatting | bytes 262144 | tf_op jit(solution)/shard_map/reshape | solution.py:206
  (94 shorter events, 16.6 us)
Async XLA Ops:
  0.6 22.5 %copy-start.3 = (bf16[16,5,33]{2,0,1:T(8,128)(2,1)S(1)}, bf16[16,5,33]{2,0,1:T(8,128)(2,1)}, u32[]{:S(2)}) copy-start(bf16[16,5,33]{2,0,1:T(8,128)(2,1)} %param.8) | copy-start | bytes 15844
  1.7 22.2 %collective-permute-start.5 = (bf16[2,128,256]{2,1,0:T(8,128)(2,1)S(1)}, bf16[2,128,256]{2,1,0:T(8,128)(2,1)S(1)}, u32[]{:S(2)}, u32[]{:S(2)}) collective-permute-start(bf16[2,128,256]{2,1,0:T(8,128)(2,1)S(1)} %bitcast.13), channel_id=1, source_target_pairs={{0,4},{4,8},{8,12},{12,16},{16,20},{20,24},{24,28},{1,5},{5,9},{9,... | collective-permute-start | bytes 393224 | tf_op jit(solution)/shard_map/ppermute | solution.py:109
  6.6 17.3 %collective-permute-start.6 = (bf16[2,128,256]{2,1,0:T(8,128)(2,1)S(1)}, bf16[2,128,256]{2,1,0:T(8,128)(2,1)S(1)}, u32[]{:S(2)}, u32[]{:S(2)}) collective-permute-start(bf16[2,128,256]{2,1,0:T(8,128)(2,1)S(1)} %bitcast.14), channel_id=1, source_target_pairs={{4,0},{8,4},{12,8},{16,12},{20,16},{24,20},{28,24},{5,1},{9,5},{13... | collective-permute-start | bytes 393224 | tf_op jit(solution)/shard_map/ppermute | solution.py:110
  8.9 19.4 %copy-start = (bf16[256,2,128]{0,2,1:T(8,128)(2,1)}, bf16[256,2,128]{0,2,1:T(8,128)(2,1)S(1)}, u32[]{:S(2)}) copy-start(bf16[256,2,128]{0,2,1:T(8,128)(2,1)S(1)} %copy.20) | copy-start | bytes 393220
  8.9 47.0 %collective-permute-start.10 = (bf16[2,128,256]{2,1,0:T(8,128)(2,1)S(1)}, bf16[2,128,256]{2,1,0:T(8,128)(2,1)S(1)}, u32[]{:S(2)}, u32[]{:S(2)}) collective-permute-start(bf16[2,128,256]{2,1,0:T(8,128)(2,1)S(1)} %bitcast.8), channel_id=1, source_target_pairs={{4,0},{8,4},{12,8},{16,12},{20,16},{24,20},{28,24},{5,1},{9,5},{13... | collective-permute-start | bytes 393224 | tf_op jit(solution)/shard_map/ppermute | solution.py:110
  10.2 45.7 %collective-permute-start.9 = (bf16[2,128,256]{2,1,0:T(8,128)(2,1)S(1)}, bf16[2,128,256]{2,1,0:T(8,128)(2,1)S(1)}, u32[]{:S(2)}, u32[]{:S(2)}) collective-permute-start(bf16[2,128,256]{2,1,0:T(8,128)(2,1)S(1)} %bitcast.9), channel_id=1, source_target_pairs={{0,4},{4,8},{8,12},{12,16},{16,20},{20,24},{24,28},{1,5},{5,9},{9,... | collective-permute-start | bytes 393224 | tf_op jit(solution)/shard_map/ppermute | solution.py:109
  16.9 21.7 %collective-permute-start = (bf16[9,8,256]{2,1,0:T(8,128)(2,1)S(1)}, bf16[9,8,256]{2,1,0:T(8,128)(2,1)S(1)}, u32[]{:S(2)}, u32[]{:S(2)}) collective-permute-start(bf16[9,8,256]{2,1,0:T(8,128)(2,1)S(1)} %get-tuple-element.31), channel_id=1, source_target_pairs={{0,16},{4,20},{8,24},{12,28},{16,0},{20,4},{24,8},{28,12},{1,17},{... | collective-permute-start | bytes 110600 | tf_op jit(solution)/shard_map/ppermute | solution.py:102
  23.9 3.6 %collective-permute-start.7 = (bf16[6,16,256]{2,1,0:T(8,128)(2,1)S(1)}, bf16[6,16,256]{2,1,0:T(8,128)(2,1)S(1)}, u32[]{:S(2)}, u32[]{:S(2)}) collective-permute-start(bf16[6,16,256]{2,1,0:T(8,128)(2,1)S(1)} %get-tuple-element.21), channel_id=1, source_target_pairs={{0,1},{1,2},{2,3},{3,0},{4,5},{5,6},{6,7},{7,4},{8,9},{9,10},{10,1... | collective-permute-start | bytes 147464 | tf_op jit(solution)/shard_map/ppermute | solution.py:109
  23.9 3.5 %collective-permute-start.8 = (bf16[6,16,256]{2,1,0:T(8,128)(2,1)S(1)}, bf16[6,16,256]{2,1,0:T(8,128)(2,1)S(1)}, u32[]{:S(2)}, u32[]{:S(2)}) collective-permute-start(bf16[6,16,256]{2,1,0:T(8,128)(2,1)S(1)} %get-tuple-element.22), channel_id=1, source_target_pairs={{1,0},{2,1},{3,2},{0,3},{5,4},{6,5},{7,6},{4,7},{9,8},{10,9},{11,1... | collective-permute-start | bytes 147464 | tf_op jit(solution)/shard_map/ppermute | solution.py:110
  32.2 4.3 %collective-permute-start.13 = (f32[9,128,256]{2,1,0:T(8,128)}, f32[9,128,256]{2,1,0:T(8,128)S(1)}, u32[]{:S(2)}, u32[]{:S(2)}) collective-permute-start(f32[9,128,256]{2,1,0:T(8,128)} %get-tuple-element.12), channel_id=1, source_target_pairs={{0,1},{1,0},{2,3},{3,2},{4,5},{5,4},{6,7},{7,6},{8,9},{9,8},{10,11... | collective-permute-start | bytes 3538952 | tf_op jit(solution)/shard_map/ppermute | solution.py:102
  36.5 8.1 %copy-start.4 = (bf16[9,128,256]{2,1,0:T(8,128)(2,1)S(1)}, bf16[9,128,256]{2,1,0:T(8,128)(2,1)}, u32[]{:S(2)}) copy-start(bf16[9,128,256]{2,1,0:T(8,128)(2,1)} %get-tuple-element.29) | copy-start | bytes 1769476
  38.0 16.2 %collective-permute-start.14 = (f32[9,64,256]{2,1,0:T(8,128)S(1)}, f32[9,64,256]{2,1,0:T(8,128)S(1)}, u32[]{:S(2)}, u32[]{:S(2)}) collective-permute-start(f32[9,64,256]{2,1,0:T(8,128)S(1)} %get-tuple-element.14), channel_id=1, source_target_pairs={{0,2},{1,3},{2,0},{3,1},{4,6},{5,7},{6,4},{7,5},{8,10},{9,11},{10,... | collective-permute-start | bytes 1769480 | tf_op jit(solution)/shard_map/ppermute | solution.py:102
  38.6 4.4 %collective-permute-start.1 = (bf16[9,16,256]{2,1,0:T(8,128)(2,1)S(1)}, bf16[9,16,256]{2,1,0:T(8,128)(2,1)S(1)}, u32[]{:S(2)}, u32[]{:S(2)}) collective-permute-start(bf16[9,16,256]{2,1,0:T(8,128)(2,1)S(1)} %pad_maximum_fusion.4), channel_id=1, source_target_pairs={{0,8},{4,12},{8,0},{12,4},{16,24},{20,28},{24,16},{28,20},{1,9},{5... | collective-permute-start | bytes 221192 | tf_op jit(solution)/shard_map/ppermute | solution.py:102
  43.0 5.2 %collective-permute-start.2 = (bf16[9,32,256]{2,1,0:T(8,128)(2,1)S(1)}, bf16[9,32,256]{2,1,0:T(8,128)(2,1)S(1)}, u32[]{:S(2)}, u32[]{:S(2)}) collective-permute-start(bf16[9,32,256]{2,1,0:T(8,128)(2,1)S(1)} %pad_maximum_fusion.3), channel_id=1, source_target_pairs={{0,4},{4,0},{8,12},{12,8},{16,20},{20,16},{24,28},{28,24},{1,5},{5... | collective-permute-start | bytes 442376 | tf_op jit(solution)/shard_map/ppermute | solution.py:102
  44.6 11.2 %copy-start.1 = (bf16[256,2,128]{0,2,1:T(8,128)(2,1)S(1)}, bf16[256,2,128]{0,2,1:T(8,128)(2,1)}, u32[]{:S(2)}) copy-start(bf16[256,2,128]{0,2,1:T(8,128)(2,1)} %copy-done) | copy-start | bytes 393220
  48.3 12.2 %collective-permute-start.3 = (bf16[9,64,256]{2,1,0:T(8,128)(2,1)S(1)}, bf16[9,64,256]{2,1,0:T(8,128)(2,1)S(1)}, u32[]{:S(2)}, u32[]{:S(2)}) collective-permute-start(bf16[9,64,256]{2,1,0:T(8,128)(2,1)S(1)} %pad_maximum_fusion.2), channel_id=1, source_target_pairs={{0,2},{1,3},{2,0},{3,1},{4,6},{5,7},{6,4},{7,5},{8,10},{9,11},{10,... | collective-permute-start | bytes 884744 | tf_op jit(solution)/shard_map/ppermute | solution.py:102
  54.3 8.0 %collective-permute-start.15 = (f32[9,32,256]{2,1,0:T(8,128)S(1)}, f32[9,32,256]{2,1,0:T(8,128)S(1)}, u32[]{:S(2)}, u32[]{:S(2)}) collective-permute-start(f32[9,32,256]{2,1,0:T(8,128)S(1)} %get-tuple-element.16), channel_id=1, source_target_pairs={{0,4},{4,0},{8,12},{12,8},{16,20},{20,16},{24,28},{28,24},{1,5},{5... | collective-permute-start | bytes 884744 | tf_op jit(solution)/shard_map/ppermute | solution.py:102
  55.9 8.6 %collective-permute-start.11 = (bf16[6,16,256]{2,1,0:T(8,128)(2,1)S(1)}, bf16[6,16,256]{2,1,0:T(8,128)(2,1)S(1)}, u32[]{:S(2)}, u32[]{:S(2)}) collective-permute-start(bf16[6,16,256]{2,1,0:T(8,128)(2,1)S(1)} %get-tuple-element.19), channel_id=1, source_target_pairs={{0,1},{1,2},{2,3},{3,0},{4,5},{5,6},{6,7},{7,4},{8,9},{9,10},{10,1... | collective-permute-start | bytes 147464 | tf_op jit(solution)/shard_map/ppermute | solution.py:109
  56.0 8.6 %collective-permute-start.12 = (bf16[6,16,256]{2,1,0:T(8,128)(2,1)S(1)}, bf16[6,16,256]{2,1,0:T(8,128)(2,1)S(1)}, u32[]{:S(2)}, u32[]{:S(2)}) collective-permute-start(bf16[6,16,256]{2,1,0:T(8,128)(2,1)S(1)} %get-tuple-element.20), channel_id=1, source_target_pairs={{1,0},{2,1},{3,2},{0,3},{5,4},{6,5},{7,6},{4,7},{9,8},{10,9},{11,1... | collective-permute-start | bytes 147464 | tf_op jit(solution)/shard_map/ppermute | solution.py:110
  60.5 8.1 %collective-permute-start.4 = (bf16[9,128,256]{2,1,0:T(8,128)(2,1)S(1)}, bf16[9,128,256]{2,1,0:T(8,128)(2,1)S(1)}, u32[]{:S(2)}, u32[]{:S(2)}) collective-permute-start(bf16[9,128,256]{2,1,0:T(8,128)(2,1)S(1)} %get-tuple-element.23), channel_id=1, source_target_pairs={{0,1},{1,0},{2,3},{3,2},{4,5},{5,4},{6,7},{7,6},{8,9},{9,8},{10,11... | collective-permute-start | bytes 1769480 | tf_op jit(solution)/shard_map/ppermute | solution.py:102
  62.3 6.0 %collective-permute-start.16 = (f32[9,16,256]{2,1,0:T(8,128)S(1)}, f32[9,16,256]{2,1,0:T(8,128)S(1)}, u32[]{:S(2)}, u32[]{:S(2)}) collective-permute-start(f32[9,16,256]{2,1,0:T(8,128)S(1)} %get-tuple-element.18), channel_id=1, source_target_pairs={{0,8},{4,12},{8,0},{12,4},{16,24},{20,28},{24,16},{28,20},{1,9},{5... | collective-permute-start | bytes 442376 | tf_op jit(solution)/shard_map/ppermute | solution.py:102
  68.3 8.3 %collective-permute-start.17 = (f32[9,8,256]{2,1,0:T(8,128)S(1)}, f32[9,8,256]{2,1,0:T(8,128)S(1)}, u32[]{:S(2)}, u32[]{:S(2)}) collective-permute-start(f32[9,8,256]{2,1,0:T(8,128)S(1)} %slice_add_fusion.6), channel_id=1, source_target_pairs={{0,16},{4,20},{8,24},{12,28},{16,0},{20,4},{24,8},{28,12},{1,17},{... | collective-permute-start | bytes 221192 | tf_op jit(solution)/shard_map/ppermute | solution.py:102
  68.7 1.0 %copy-start.2 = (bf16[9,256,256]{2,1,0:T(8,128)(2,1)}, bf16[9,256,256]{2,1,0:T(8,128)(2,1)S(1)}, u32[]{:S(2)}) copy-start(bf16[9,256,256]{2,1,0:T(8,128)(2,1)S(1)} %constant_dynamic-update-slice_fusion.5.weight_ref) | copy-start | bytes 3538948
where the time goes:
time: 77.8 us; the launch traced here: 77.3 us
  starting transfers between devices  30.9 us (40%)
  waiting for transfers between devices  17.4 us (22%)
  local copies, waits for them, and re-layouts  12.1 us (16%)
  Pallas kernels  10.5 us (13%)
  other arithmetic  5.44 us (7%)
  between operations  0.97 us (1%)
    ppermute x10, waiting for transfers between devices, swap(): lax.ppermute(array, axis, [(i, i ^ stride) for i in range(lax.axis_size(a...  16.3 us
    ppermute x10, starting transfers between devices, swap(): lax.ppermute(array, axis, [(i, i ^ stride) for i in range(lax.axis_size(a...  14.7 us
    pallas_call x3, Pallas kernels, call(): pl.pallas_call(body, out_shape=[jax.ShapeDtypeStruct(s, d) for s, d in ou...  10.5 us
    ppermute x4, starting transfers between devices, with_halo(): lax.ppermute(lax.slice_in_dim(array, length - width, length, axis=dim), a...  10.2 us
    ppermute x4, starting transfers between devices, with_halo(): lax.ppermute(lax.slice_in_dim(array, 0, width, axis=dim), axis, down)  6.05 us
    unnamed x31, local copies, waits for them, and re-layouts  5.38 us
    reshape x2, local copies, waits for them, and re-layouts, local(): return (output.reshape(shape), input_grad.reshape(shape), weight_grad)  3.19 us
    dynamic_slice x4, local copies, waits for them, and re-layouts, local(): lax.dynamic_slice_in_dim(t, first, lat_rows, 0)  2.33 us
  transfers between devices with their start and end apart: 18, of which 7 were waited for; matrix products, arithmetic and copies ran while one was open for 19% of the time, Pallas kernels for 14%

commit v1 on v0

v1 whole, which is shorter than its diff:
```python
import jax
import jax.numpy as jnp
from jax import lax
from jax.experimental import pallas as pl
from jax.experimental.pallas import tpu as pltpu
from jax.sharding import PartitionSpec as P

TILE = 32
SLOT = 64
VMEM = 60 * 1024 * 1024
NT = (((1,), (1,)), ((), ()))
TN = (((0,), (0,)), ((), ()))
bf16, f32 = jnp.bfloat16, jnp.float32


def dot(a, b, dims=(((1,), (0,)), ((), ()))):
    return lax.dot_general(a, b, dims, preferred_element_type=f32)


def call(body, name, outs, *args, scratch=()):
    in_vmem = pl.BlockSpec(memory_space=pltpu.VMEM)
    return pl.pallas_call(
        body,
        name=name,
        out_shape=[jax.ShapeDtypeStruct(s, d) for s, d in outs],
        in_specs=[in_vmem for _ in args],
        out_specs=[in_vmem for _ in outs],
        scratch_shapes=list(scratch),
        compiler_params=pltpu.CompilerParams(vmem_limit_bytes=VMEM),
    )(*args)


def log2(size):
    return size.bit_length() - 1


class Layout:
    def __init__(self, channels, lats, lons):
        self.channels, self.lons = channels, lons
        devices = lats * lons
        self.parts = max(1, devices // channels)
        self.own = channels * self.parts // devices

        def bits(axis, size, scale):
            return [(axis, 1 << b, scale << b) for b in range(size.bit_length() - 1)]

        steps = bits("lon", lons, 1) + [s for s in bits("lat", lats, lons) if s[1] > 1]
        self.split = [s for s in steps if s[2] < self.parts]
        self.steps = [s for s in steps if s[2] >= self.parts]
        self.pair = lons // self.parts * self.own

    def odd(self):
        return lax.axis_index("lat") & 1

    def places(self, shape, dim):
        place = lax.broadcasted_iota(jnp.int32, shape, dim)
        device = lax.axis_index("lat") * self.lons + lax.axis_index("lon")
        channel = place & (self.own - 1)
        for rank, (_, _, bit) in enumerate(self.steps):
            value = bit // self.parts * self.own
            value = value // 2 if value > self.pair else value
            size = self.channels >> (rank + 2)
            differs = ((place >> log2(size)) ^ (device >> log2(bit))) & 1
            channel = channel + (differs << log2(value))
        return channel

    def whole(self, channel, odd):
        low = log2(self.pair)
        return ((channel >> low) << (low + 1)) + (odd << low) + (channel & (self.pair - 1))


def bands(taps_ref, index_ref, row, basis_count):
    taps, index = taps_ref[row], index_ref[row]

    def paired(v):
        return [jnp.concatenate([v[s : s + 1], v[s + 1 : s + 2]], axis=1) for s in range(0, v.shape[0], 2)]

    taps, index = paired(taps), paired(index)
    parts = []
    for basis in range(basis_count):
        pieces = []
        for line, kind in zip(taps, index):
            piece = jnp.broadcast_to(jnp.where(kind == basis, line, 0.0), (TILE, 2 * SLOT))
            pieces.append(pltpu.roll(piece, 0, 1, stride=1, stride_axis=0))
        parts.append(jnp.concatenate(pieces, axis=1).astype(bf16))
    return jnp.concatenate(parts, axis=0)


def place_rows(scr, move, own_ref, pair_ref, near_ref, next_ref, core_ref, cross_ref):
    rows, cols = own_ref.shape[0], own_ref.shape[1]
    rim = core_ref.shape[1]
    odd, flip = lax.axis_index("lat") & 1, (lax.axis_index("lat") >> 1) & 1
    even_col = (lax.axis_index("lon") & 1) == 0
    slots = ((1 - flip) * 3 * rows, (1 + odd) * rows, (2 - odd) * rows, flip * 3 * rows)
    for rank, (slot, ref) in enumerate(zip(slots, (near_ref, own_ref, pair_ref, next_ref))):
        for row in range(rows):
            core, cross = core_ref[rank * rows + row], cross_ref[rank * rows + row]
            scr[slot + row, rim : rim + cols, :] = move(ref[row])
            scr[slot + row, :rim, :] = move(jnp.where(even_col, cross, core))
            scr[slot + row, rim + cols :, :] = move(jnp.where(even_col, core, cross))


def forward_body(lay, offsets, own_ref, pair_ref, near_ref, next_ref, core_ref, cross_ref, taps_ref, index_ref,
                 own_cot_ref, pair_cot_ref, out_ref, send_ref, keep_ref, ext_scr):
    rows, cols, channels = own_ref.shape
    basis_count = out_ref.shape[0]
    odd = lay.odd()
    shape = (channels, channels)
    pick = (lax.broadcasted_iota(jnp.int32, shape, 0) == lay.places(shape, 1)).astype(bf16)
    place_rows(ext_scr, lambda v: dot(v, pick).astype(bf16), own_ref, pair_ref, near_ref, next_ref, core_ref, cross_ref)
    first_row = (lax.axis_index("lat") - odd) * rows
    for line in range(2 * rows):
        low = (odd if line < rows else 1 - odd) * rows + line % rows
        band = bands(taps_ref, index_ref, first_row + low + rows, basis_count)[:, : offsets * SLOT]
        for first in range(0, cols, 2 * TILE):
            source = [
                jnp.concatenate([ext_scr[low + a, start : start + SLOT, :] for a in range(offsets)], axis=0)
                for start in (first, first + TILE)
            ]
            moved = dot(band, jnp.concatenate(source, axis=1)).astype(bf16)
            for basis in range(basis_count):
                for side in range(2):
                    start = line * cols + first + side * TILE
                    piece = moved[basis * TILE : (basis + 1) * TILE, side * channels : (side + 1) * channels]
                    out_ref[basis, start : start + TILE, :] = piece
    cot = jnp.concatenate([own_cot_ref[...], pair_cot_ref[...]], axis=0).reshape(2 * rows * cols, own_cot_ref.shape[2])
    half = channels // 2
    for basis in range(basis_count):
        terms = dot(out_ref[basis], cot, TN)
        send_ref[basis] = terms[half:].astype(send_ref.dtype)
        keep_ref[basis] = terms[:half]


def mix_body(weight_ref, basis_ref, own_ref, pair_ref):
    basis_count, channels, outs = weight_ref.shape
    cells = own_ref.shape[0]
    source = jnp.concatenate([basis_ref[basis] for basis in range(basis_count)], axis=1)
    total = dot(source, weight_ref[...].reshape(basis_count * channels, outs))
    own_ref[...] = total[:cells]
    pair_ref[...] = total[cells:]


def backward_body(lay, offsets, own_ref, pair_ref, near_ref, next_ref, core_ref, cross_ref, taps_ref, index_ref,
                  weight_ref, own_grad_ref, pair_grad_ref, ext_scr, basis_scr, sum_scr):
    rows, cols, _ = own_ref.shape
    basis_count, channels, outs = weight_ref.shape
    odd = lay.odd()
    place_rows(ext_scr, lambda v: v, own_ref, pair_ref, near_ref, next_ref, core_ref, cross_ref)
    weight = weight_ref[...].reshape(basis_count * channels, outs)
    first_row = (lax.axis_index("lat") - odd) * rows
    ext_rows, ext_cols, _ = ext_scr.shape
    reach, blocks = offsets // 2, ext_cols // TILE
    sum_scr[...] = jnp.zeros(sum_scr.shape, f32)
    for row in range(ext_rows):
        basis_grad = dot(ext_scr[row], weight, NT).astype(bf16)
        for basis in range(basis_count):
            for block in range(blocks):
                piece = basis_grad[block * TILE : (block + 1) * TILE, basis * channels : (basis + 1) * channels]
                side = block % 2 * channels
                basis_scr[block // 2, basis * TILE : (basis + 1) * TILE, side : side + channels] = piece
        wanted = [a for a in range(offsets) if rows <= row + a - reach < 3 * rows]
        low = wanted[0] // 2 * 2
        high = min(wanted[-1] // 2 * 2 + 2, offsets)
        band = bands(taps_ref, index_ref, first_row + row, basis_count)[:, low * SLOT : high * SLOT]
        for block in range(0, blocks, 2):
            sides = min(2, blocks - block)
            spread = dot(band, basis_scr[block // 2, :, : sides * channels], TN)
            for a in wanted:
                for side in range(sides):
                    target, start = row + a - reach - rows, (block + side) * TILE
                    piece = spread[(a - low) * SLOT : (a - low + 1) * SLOT, side * channels : (side + 1) * channels]
                    sum_scr[target, start : start + SLOT, :] = sum_scr[target, start : start + SLOT, :] + piece
    for row in range(rows):
        for ref, slot in ((own_grad_ref, odd * rows), (pair_grad_ref, (1 - odd) * rows)):
            ref[row * cols : (row + 1) * cols, :] = sum_scr[slot + row, TILE : TILE + cols, :].astype(bf16)


def finish_body(lay, own_ref, pair_ref, grad_ref):
    shape = (own_ref.shape[1], grad_ref.shape[1])
    place, column = lay.places(shape, 0), lax.broadcasted_iota(jnp.int32, shape, 1)
    odd = lay.odd()
    own = (column == lay.whole(place, odd)).astype(bf16)
    pair = (column == lay.whole(place, 1 - odd)).astype(bf16)
    grad_ref[...] = (dot(own_ref[...], own) + dot(pair_ref[...], pair)).astype(bf16)


def swap(array, axis, stride):
    return lax.ppermute(array, axis, [(i, i ^ stride) for i in range(lax.axis_size(axis))])


def swap_across(array, axis, stride, wrap):
    size = lax.axis_size(axis)
    pairs = [(i, i + stride if i // stride % 2 else i - stride) for i in range(size)]
    return lax.ppermute(array, axis, [(i, j % size) for i, j in pairs if wrap or 0 <= j < size])


def around(own, pair, rim):
    lat, lon = lax.axis_index("lat"), lax.axis_index("lon")
    own_first = (lat & 1) != ((lat >> 1) & 1)
    near = swap(jnp.where(own_first, own, pair), "lat", 2)
    far = swap_across(jnp.where(own_first, pair, own), "lat", 2, False)
    lines = (near, own, pair, far)
    first = jnp.concatenate([v[:, :rim] for v in lines], axis=0)
    last = jnp.concatenate([v[:, -rim:] for v in lines], axis=0)
    even = (lon & 1) == 0
    core = swap(jnp.where(even, last, first), "lon", 1)
    cross = swap_across(jnp.where(even, first, last), "lon", 1, True)
    return near, far, core, cross


def local(features, weight, tap_values, basis_index, half_width, cotangent):
    channels, rows, cols = features.shape
    basis_count = weight.shape[0]
    _, offsets, window = tap_values.shape
    rim = (window - 1) // 2
    lay = Layout(channels, lax.axis_size("lat"), lax.axis_size("lon"))
    odd = lay.odd()
    half = channels // 2

    split = features.reshape(half // lay.pair, 2, lay.pair, rows, cols)
    to_pair = lax.dynamic_index_in_dim(split, 1 - odd, 1, False).reshape(half, rows, cols)
    to_keep = lax.dynamic_index_in_dim(split, odd, 1, False).reshape(half, rows, cols)
    feat_pair = jnp.transpose(swap(to_pair, "lat", 1), (1, 2, 0))
    feat_own = jnp.transpose(to_keep, (1, 2, 0))
    cot_pair = jnp.transpose(swap(cotangent, "lat", 1), (1, 2, 0))
    cot_own = jnp.transpose(cotangent, (1, 2, 0))

    far = jnp.abs(jnp.arange(window) - rim)
    index = jnp.where(far[None, None, :] <= half_width[:, None, None], basis_index, -1)
    fill = ((rows, rows), (0, offsets % 2), (0, SLOT - window))
    index = jnp.pad(index, fill, constant_values=-1)
    taps = jnp.pad(tap_values.astype(f32), fill)

    feat_around = around(feat_own, feat_pair, rim)
    cot_around = around(cot_own, cot_pair, rim)

    full = weight.reshape(basis_count, lay.own, channels // lay.parts)
    for axis, stride, _ in lay.split:
        other = swap(full, axis, stride)
        low = (lax.axis_index(axis) // stride) % 2 == 0
        full = jnp.where(low, jnp.concatenate([full, other], 2), jnp.concatenate([other, full], 2))
    for axis, stride, _ in reversed(lay.steps):
        full = jnp.concatenate([full, swap(full, axis, stride)], axis=1)

    cells = rows * cols
    ext = (4 * rows, cols + 2 * rim)
    basis_out, send, keep = call(
        lambda *refs: forward_body(lay, offsets, *refs), "forward",
        [((basis_count, 2 * cells, half), bf16), ((basis_count, half // 2, channels), f32),
         ((basis_count, half // 2, channels), f32)],
        feat_own, feat_pair, *feat_around, taps, index, cot_own, cot_pair,
        scratch=[pltpu.VMEM((*ext, half), bf16)],
    )
    for rank, (axis, stride, _) in enumerate(lay.steps):
        terms = (keep, swap(send, axis, stride))
        if rank + 1 < len(lay.steps):
            size = keep.shape[1] // 2
            send = terms[0][:, size:] + terms[1][:, size:]
            keep = terms[0][:, :size] + terms[1][:, :size]
    grad = terms[0] + terms[1]
    for axis, stride, _ in reversed(lay.split):
        size = grad.shape[2] // 2
        mine = (lax.axis_index(axis) // stride) % 2
        other = swap(lax.dynamic_slice_in_dim(grad, (1 - mine) * size, size, 2), axis, stride)
        grad = lax.dynamic_slice_in_dim(grad, mine * size, size, 2) + other
    weight_grad = grad.reshape(basis_count, weight.shape[1])

    own_out, pair_out = call(mix_body, "mix", [((cells, channels), f32), ((cells, channels), f32)], full, basis_out)
    pair_out = swap(pair_out, "lat", 1)
    own_grad, pair_grad = call(
        lambda *refs: backward_body(lay, offsets, *refs), "backward",
        [((cells, half), bf16), ((cells, half), bf16)],
        cot_own, cot_pair, *cot_around, taps, index, full,
        scratch=[pltpu.VMEM((*ext, channels), bf16),
                 pltpu.VMEM((-(-ext[1] // (2 * TILE)), basis_count * TILE, 2 * half), bf16),
                 pltpu.VMEM((2 * rows, ext[1] + TILE, half), f32)],
    )
    pair_grad = swap(pair_grad, "lat", 1)
    output = (own_out + pair_out).astype(bf16)
    (input_grad,) = call(
        lambda *refs: finish_body(lay, *refs), "finish", [((cells, channels), bf16)], own_grad, pair_grad
    )

    def channels_first(v):
        return jnp.transpose(v.reshape(rows, cols, channels), (2, 0, 1))

    return channels_first(output), channels_first(input_grad), weight_grad


def solution(mesh):
    field = P(None, "lat", "lon")
    flat = P(None, ("lat", "lon"))
    return jax.shard_map(
        local,
        mesh=mesh,
        in_specs=(field, flat, P(), P(), P(), field),
        out_specs=(field, field, flat),
        check_vma=False,
    )
```

time: 77.8 us -> 67.2 us (0.86)
  waiting for transfers between devices: 17.4 us -> 9.98 us
  Pallas kernels: 10.5 us -> 14.2 us
  other arithmetic: 5.44 us -> 2 us
  starting transfers between devices: 30.9 us -> 29.1 us
  local copies, waits for them, and re-layouts: 12.1 us -> 10.4 us
    ppermute x8 -> x4, starting transfers between devices: 16.2 us -> 2.43 us  [swap_across(): lax.ppermute(array, axis, [(i, j % size) for i, j in pairs if wrap or 0 <...]
    ppermute x10 -> x16, starting transfers between devices: 14.7 us -> 26.7 us  [swap(): lax.ppermute(array, axis, [(i, i ^ stride) for i in range(lax.axis_size(a...]
    ppermute x10 -> x16, waiting for transfers between devices: 16.3 us -> 9.96 us  [swap(): lax.ppermute(array, axis, [(i, i ^ stride) for i in range(lax.axis_size(a...]
    pallas_call x3 -> x4, Pallas kernels: 10.5 us -> 14.2 us  [call(): pl.pallas_call(body, name=name, out_shape=[jax.ShapeDtypeStruct(s, d) for...]
    dynamic_slice x4 -> x1, local copies, waits for them, and re-layouts: 2.33 us -> 0.02 us  [local(): lax.dynamic_index_in_dim(split, 1 - odd, 1, False).reshape(half, rows, cols)]
    concatenate x2 -> x0, other arithmetic: 1.67 us -> none  [with_halo(): return jnp.concatenate([before, array, after], axis=dim)]
    add x3 -> x2, other arithmetic: 1.58 us -> 0.13 us  [local(): keep = terms[0][:, :size] + terms[1][:, :size]]
    ppermute x8 -> x4, waiting for transfers between devices: 1.13 us -> 0.01 us  [swap_across(): lax.ppermute(array, axis, [(i, j % size) for i, j in pairs if wrap or 0 <...]
  transfers between devices with their start and end apart: 18 -> 20, of which waited for: 7 -> 6; matrix products, arithmetic and copies ran while one was open for 19% -> 12% of each run, Pallas kernels for 14% -> 21%
where the time goes in v1:
time: 67.2 us; the launch traced here: 66.8 us
  starting transfers between devices  29.1 us (43%)
  Pallas kernels  14.2 us (21%)
  local copies, waits for them, and re-layouts  10.4 us (15%)
  waiting for transfers between devices  9.98 us (15%)
  other arithmetic  2 us (3%)
  between operations  1.05 us (2%)
    ppermute x16, starting transfers between devices, swap(): lax.ppermute(array, axis, [(i, i ^ stride) for i in range(lax.axis_size(a...  26.7 us
    pallas_call x4, Pallas kernels, call(): pl.pallas_call(body, name=name, out_shape=[jax.ShapeDtypeStruct(s, d) for...  14.2 us
    ppermute x16, waiting for transfers between devices, swap(): lax.ppermute(array, axis, [(i, i ^ stride) for i in range(lax.axis_size(a...  9.96 us
    unnamed x45, local copies, waits for them, and re-layouts  6.2 us
    reshape x2, local copies, waits for them, and re-layouts, channels_first(): return jnp.transpose(v.reshape(rows, cols, channels), (2, 0, 1))  2.46 us
    ppermute x4, starting transfers between devices, swap_across(): lax.ppermute(array, axis, [(i, j % size) for i, j in pairs if wrap or 0 <...  2.43 us
  transfers between devices with their start and end apart: 20, of which 6 were waited for; matrix products, arithmetic and copies ran while one was open for 12% of the time, Pallas kernels for 21%

profile of v1, /device:TPU:0, one launch (start us, length us, event | category | flops | bytes accessed | tf_op | source)
XLA Modules:
  0.0 66.8 jit_solution(7024109949417905445)
XLA Ops:
  0.7 0.9 %copy.25 = bf16[256,2,128]{2,0,1:T(8,128)(2,1)S(1)} copy(bf16[256,2,128]{2,1,0:T(2,128)(2,1)} %param.6) | data formatting | bytes 262144 | tf_op args[0]
  1.8 3.0 %collective-permute-start.4 = (bf16[128,2,128]{0,2,1:T(8,128)(2,1)S(1)}, bf16[128,2,128]{0,2,1:T(8,128)(2,1)S(1)}, u32[]{:S(2)}, u32[]{:S(2)}) collective-permute-start(bf16[128,2,128]{0,2,1:T(8,128)(2,1)S(1)} %copy.27), channel_id=1, source_target_pairs={{0,4},{4,0},{8,12},{12,8},{16,20},{20,16},{24,28},{28,24},{1,5},{5... | collective-permute-start | bytes 196616 | tf_op jit(solution)/shard_map/ppermute | solution.py:188
  4.8 1.0 %copy.30 = bf16[256,2,128]{0,2,1:T(8,128)(2,1)S(1)} copy(bf16[256,2,128]{2,1,0:T(2,128)(2,1)} %param.11) | data formatting | bytes 262144 | tf_op args[5]
  5.9 0.9 %copy.34 = bf16[2,8,8,256]{3,2,1,0:T(8,128)(2,1)S(1)} copy(bf16[2,8,8,256]{3,1,2,0:T(8,128)(2,1)} %bitcast.45) | data formatting | bytes 131072
  6.8 3.1 %collective-permute-start = (bf16[9,8,256]{2,1,0:T(8,128)(2,1)S(1)}, bf16[9,8,256]{2,1,0:T(8,128)(2,1)S(1)}, u32[]{:S(2)}, u32[]{:S(2)}) collective-permute-start(bf16[9,8,256]{2,1,0:T(8,128)(2,1)S(1)} %get-tuple-element.47), channel_id=1, source_target_pairs={{0,16},{4,20},{8,24},{12,28},{16,0},{20,4},{24,8},{28,12},{1,17},{... | collective-permute-start | bytes 110600 | tf_op jit(solution)/shard_map/ppermute | solution.py:188
  11.9 1.9 %collective-permute-start.1 = (bf16[9,16,256]{2,1,0:T(8,128)(2,1)S(1)}, bf16[9,16,256]{2,1,0:T(8,128)(2,1)S(1)}, u32[]{:S(2)}, u32[]{:S(2)}) collective-permute-start(bf16[9,16,256]{2,1,0:T(8,128)(2,1)S(1)} %pad_maximum_fusion.2), channel_id=1, source_target_pairs={{0,8},{4,12},{8,0},{12,4},{16,24},{20,28},{24,16},{28,20},{1,9},{5... | collective-permute-start | bytes 221192 | tf_op jit(solution)/shard_map/ppermute | solution.py:188
  14.5 4.7 %collective-permute-start.5 = (bf16[2,128,128]{2,1,0:T(8,128)(2,1)S(1)}, bf16[2,128,128]{2,1,0:T(8,128)(2,1)S(1)}, u32[]{:S(2)}, u32[]{:S(2)}) collective-permute-start(bf16[2,128,128]{2,1,0:T(8,128)(2,1)S(1)} %get-tuple-element.34), channel_id=1, source_target_pairs={{0,8},{4,12},{8,0},{12,4},{16,24},{20,28},{24,16},{28,20},{1,9},{5... | collective-permute-start | bytes 196616 | tf_op jit(solution)/shard_map/ppermute | solution.py:188
  19.3 1.6 %collective-permute-start.2 = (bf16[9,32,256]{2,1,0:T(8,128)(2,1)S(1)}, bf16[9,32,256]{2,1,0:T(8,128)(2,1)S(1)}, u32[]{:S(2)}, u32[]{:S(2)}) collective-permute-start(bf16[9,32,256]{2,1,0:T(8,128)(2,1)S(1)} %pad_maximum_fusion.1), channel_id=1, source_target_pairs={{0,2},{1,3},{2,0},{3,1},{4,6},{5,7},{6,4},{7,5},{8,10},{9,11},{10,... | collective-permute-start | bytes 442376 | tf_op jit(solution)/shard_map/ppermute | solution.py:188
  21.6 1.6 %collective-permute-start.7 = (bf16[8,16,128]{2,1,0:T(8,128)(2,1)S(1)}, bf16[8,16,128]{2,1,0:T(8,128)(2,1)S(1)}, u32[]{:S(2)}, u32[]{:S(2)}) collective-permute-start(bf16[8,16,128]{2,1,0:T(8,128)(2,1)S(1)} %get-tuple-element.38), channel_id=1, source_target_pairs={{0,1},{1,0},{2,3},{3,2},{4,5},{5,4},{6,7},{7,6},{8,9},{9,8},{10,11... | collective-permute-start | bytes 98312 | tf_op jit(solution)/shard_map/ppermute | solution.py:188
  23.9 3.3 %collective-permute-start.11 = (bf16[2,128,256]{2,1,0:T(8,128)(2,1)S(1)}, bf16[2,128,256]{2,1,0:T(8,128)(2,1)S(1)}, u32[]{:S(2)}, u32[]{:S(2)}) collective-permute-start(bf16[2,128,256]{2,1,0:T(8,128)(2,1)S(1)} %get-tuple-element.22), channel_id=1, source_target_pairs={{0,8},{4,12},{8,0},{12,4},{16,24},{20,28},{24,16},{28,20},{1,9},{5... | collective-permute-start | bytes 393224 | tf_op jit(solution)/shard_map/ppermute | solution.py:188
  27.9 3.8 %forward.1 = (bf16[9,512,128]{2,1,0:T(8,128)(2,1)}, f32[9,64,256]{2,1,0:T(8,128)}, f32[9,64,256]{2,1,0:T(8,128)}) custom-call(bf16[2,128,128]{2,1,0:T(8,128)(2,1)} %bitcast.32, bf16[2,128,128]{2,1,0:T(8,128)(2,1)} %bitcast.38, bf16[2,128,128]{2,1,0:T(8,128)(2,1)} %copy-done.9, bf16[2,128,128]{2,1,0:T(8,128)(2,1)} %copy-done.8, ...), custom_call_target="tpu_custom_call" | custom-call | tf_op jit(solution)/shard_map/forward/pallas_call | solution.py:22
  31.7 0.8 %fusion.3 = (bf16[2,16,256]{2,1,0:T(8,128)(2,1)S(1)}, bf16[2,16,256]{2,1,0:T(8,128)(2,1)S(1)}) fusion(bf16[2,128,256]{2,1,0:T(8,128)(2,1)} %bitcast.29), kind=kLoop, calls=%fused_computation.36 | loop fusion | bytes 65536 | tf_op jit(solution)/shard_map/slice | solution.py:204
  33.1 0.8 %collective-permute-done.16 = f32[9,64,256]{2,1,0:T(8,128)S(1)} collective-permute-done((f32[9,64,256]{2,1,0:T(8,128)}, f32[9,64,256]{2,1,0:T(8,128)S(1)}, u32[]{:S(2)}, u32[]{:S(2)}) %collective-permute-start.16) | collective-permute-done | bytes 589856 | tf_op jit(solution)/shard_map/ppermute | solution.py:188
  34.6 1.0 %collective-permute-start.14 = (bf16[8,16,256]{2,1,0:T(8,128)(2,1)S(1)}, bf16[8,16,256]{2,1,0:T(8,128)(2,1)S(1)}, u32[]{:S(2)}, u32[]{:S(2)}) collective-permute-start(bf16[8,16,256]{2,1,0:T(8,128)(2,1)S(1)} %get-tuple-element.23), channel_id=1, source_target_pairs={{0,3},{1,2},{2,1},{3,0},{4,7},{5,6},{6,5},{7,4},{8,11},{9,10},{10,... | collective-permute-start | bytes 196616 | tf_op jit(solution)/shard_map/ppermute | solution.py:194
  36.3 7.5 %collective-permute-done.17 = f32[9,32,256]{2,1,0:T(8,128)S(1)} collective-permute-done((f32[9,32,256]{2,1,0:T(8,128)S(1)}, f32[9,32,256]{2,1,0:T(8,128)S(1)}, u32[]{:S(2)}, u32[]{:S(2)}) %collective-permute-start.17) | collective-permute-done | bytes 294944 | tf_op jit(solution)/shard_map/ppermute | solution.py:188
  44.1 0.8 %copy-done = bf16[9,128,256]{2,1,0:T(8,128)(2,1)} copy-done((bf16[9,128,256]{2,1,0:T(8,128)(2,1)}, bf16[9,128,256]{2,1,0:T(8,128)(2,1)S(1)}, u32[]{:S(2)}) %copy-start) | copy-done | bytes 589848
  45.5 5.8 %backward.1 = (bf16[256,128]{1,0:T(8,128)(2,1)}, bf16[256,128]{1,0:T(8,128)(2,1)}) custom-call(bf16[2,128,256]{2,1,0:T(8,128)(2,1)} %bitcast.27, bf16[2,128,256]{2,1,0:T(8,128)(2,1)} %bitcast.30, bf16[2,128,256]{2,1,0:T(8,128)(2,1)} %copy-done.7, bf16[2,128,256]{2,1,0:T(8,128)(2,1)} %copy-done.6, bf16[8,16,256]{2,1,0:T(8,128)(2,1)} %copy-done.11, ...), custom_call_target="tpu_custom_call" | custom-call | tf_op jit(solution)/shard_map/backward/pallas_call | solution.py:22
  51.3 1.5 %collective-permute-start.15 = (bf16[256,128]{1,0:T(8,128)(2,1)}, bf16[256,128]{1,0:T(8,128)(2,1)S(1)}, u32[]{:S(2)}, u32[]{:S(2)}) collective-permute-start(bf16[256,128]{1,0:T(8,128)(2,1)} %get-tuple-element.14), channel_id=1, source_target_pairs={{0,4},{4,0},{8,12},{12,8},{16,20},{20,16},{24,28},{28,24},{1,5},{5... | collective-permute-start | bytes 196616 | tf_op jit(solution)/shard_map/ppermute | solution.py:188
  52.8 2.7 %mix.1 = (f32[256,256]{1,0:T(8,128)}, f32[256,256]{1,0:T(8,128)}) custom-call(bf16[9,128,256]{2,1,0:T(8,128)(2,1)} %copy-done, bf16[9,512,128]{2,1,0:T(8,128)(2,1)} %get-tuple-element.10.basis_ref), custom_call_target="tpu_custom_call" | custom-call | tf_op jit(solution)/shard_map/mix/pallas_call | solution.py:22
  56.7 1.8 %finish.1 = bf16[256,256]{1,0:T(8,128)(2,1)} custom-call(bf16[256,128]{1,0:T(8,128)(2,1)} %get-tuple-element.13.refs_0_, bf16[256,128]{1,0:T(8,128)(2,1)} %copy-done.12), custom_call_target="tpu_custom_call" | custom-call | tf_op jit(solution)/shard_map/finish/pallas_call | solution.py:22
  58.5 1.7 %copy.33 = bf16[2,128,256]{1,0,2:T(2,128)(2,1)} copy(bf16[2,128,256]{2,1,0:T(8,128)(2,1)} %bitcast.35) | data formatting | bytes 262144 | tf_op jit(solution)/shard_map/reshape | solution.py:285
  60.2 3.5 %collective-permute-start.19 = (f32[9,8,256]{2,1,0:T(8,128)S(1)}, f32[9,8,256]{2,1,0:T(8,128)S(1)}, u32[]{:S(2)}, u32[]{:S(2)}) collective-permute-start(f32[9,8,256]{2,1,0:T(8,128)S(1)} %slice_add_fusion.4), channel_id=1, source_target_pairs={{0,16},{4,20},{8,24},{12,28},{16,0},{20,4},{24,8},{28,12},{1,17},{... | collective-permute-start | bytes 221192 | tf_op jit(solution)/shard_map/ppermute | solution.py:188
  63.8 1.0 %add_convert_fusion = bf16[256,256]{1,0:T(8,128)(2,1)S(1)} fusion(f32[256,256]{1,0:T(8,128)} %get-tuple-element.11, f32[256,256]{1,0:T(8,128)S(1)} %collective-permute-done.10), kind=kLoop, calls=%fused_computation.3 | loop fusion | flops 131072 | bytes 655360 | tf_op jit(solution)/shard_map/convert_element_type | solution.py:279
  64.8 0.8 %copy.32 = bf16[2,128,256]{1,0,2:T(2,128)(2,1)} copy(bf16[2,128,256]{2,1,0:T(8,128)(2,1)S(1)} %bitcast.33) | data formatting | bytes 262144 | tf_op jit(solution)/shard_map/reshape | solution.py:285
  (97 shorter events, 10.1 us)
Async XLA Ops:
  1.8 12.0 %collective-permute-start.4 = (bf16[128,2,128]{0,2,1:T(8,128)(2,1)S(1)}, bf16[128,2,128]{0,2,1:T(8,128)(2,1)S(1)}, u32[]{:S(2)}, u32[]{:S(2)}) collective-permute-start(bf16[128,2,128]{0,2,1:T(8,128)(2,1)S(1)} %copy.27), channel_id=1, source_target_pairs={{0,4},{4,0},{8,12},{12,8},{16,20},{20,16},{24,28},{28,24},{1,5},{5... | collective-permute-start | bytes 196616 | tf_op jit(solution)/shard_map/ppermute | solution.py:188
  5.8 17.4 %copy-start.1 = (bf16[256,2,128]{0,2,1:T(8,128)(2,1)}, bf16[256,2,128]{0,2,1:T(8,128)(2,1)S(1)}, u32[]{:S(2)}) copy-start(bf16[256,2,128]{0,2,1:T(8,128)(2,1)S(1)} %copy.30) | copy-start | bytes 393220
  5.8 17.4 %collective-permute-start.9 = (bf16[256,2,128]{0,2,1:T(8,128)(2,1)S(1)}, bf16[256,2,128]{0,2,1:T(8,128)(2,1)S(1)}, u32[]{:S(2)}, u32[]{:S(2)}) collective-permute-start(bf16[256,2,128]{0,2,1:T(8,128)(2,1)S(1)} %copy.30), channel_id=1, source_target_pairs={{0,4},{4,0},{8,12},{12,8},{16,20},{20,16},{24,28},{28,24},{1,5},{5... | collective-permute-start | bytes 393224 | tf_op jit(solution)/shard_map/ppermute | solution.py:188
  6.8 5.1 %collective-permute-start = (bf16[9,8,256]{2,1,0:T(8,128)(2,1)S(1)}, bf16[9,8,256]{2,1,0:T(8,128)(2,1)S(1)}, u32[]{:S(2)}, u32[]{:S(2)}) collective-permute-start(bf16[9,8,256]{2,1,0:T(8,128)(2,1)S(1)} %get-tuple-element.47), channel_id=1, source_target_pairs={{0,16},{4,20},{8,24},{12,28},{16,0},{20,4},{24,8},{28,12},{1,17},{... | collective-permute-start | bytes 110600 | tf_op jit(solution)/shard_map/ppermute | solution.py:188
  10.1 17.2 %copy-start.3 = (bf16[128,2,128]{0,2,1:T(8,128)(2,1)}, bf16[128,2,128]{0,2,1:T(8,128)(2,1)S(1)}, u32[]{:S(2)}) copy-start(bf16[128,2,128]{0,2,1:T(8,128)(2,1)S(1)} %copy.26) | copy-start | bytes 196612
  11.9 7.3 %collective-permute-start.1 = (bf16[9,16,256]{2,1,0:T(8,128)(2,1)S(1)}, bf16[9,16,256]{2,1,0:T(8,128)(2,1)S(1)}, u32[]{:S(2)}, u32[]{:S(2)}) collective-permute-start(bf16[9,16,256]{2,1,0:T(8,128)(2,1)S(1)} %pad_maximum_fusion.2), channel_id=1, source_target_pairs={{0,8},{4,12},{8,0},{12,4},{16,24},{20,28},{24,16},{28,20},{1,9},{5... | collective-permute-start | bytes 221192 | tf_op jit(solution)/shard_map/ppermute | solution.py:188
  13.8 13.5 %copy-start.5 = (bf16[128,2,128]{0,2,1:T(8,128)(2,1)}, bf16[128,2,128]{0,2,1:T(8,128)(2,1)S(1)}, u32[]{:S(2)}) copy-start(bf16[128,2,128]{0,2,1:T(8,128)(2,1)S(1)} %collective-permute-done.4) | copy-start | bytes 196612
  13.8 7.0 %collective-permute-start.6 = (bf16[2,128,128]{2,1,0:T(8,128)(2,1)S(1)}, bf16[2,128,128]{2,1,0:T(8,128)(2,1)S(1)}, u32[]{:S(2)}, u32[]{:S(2)}) collective-permute-start(bf16[2,128,128]{2,1,0:T(8,128)(2,1)S(1)} %get-tuple-element.33), channel_id=1, source_target_pairs={{8,16},{12,20},{16,8},{20,12},{9,17},{13,21},{17,9},{21,13},{10,18... | collective-permute-start | bytes 196616 | tf_op jit(solution)/shard_map/ppermute | solution.py:194
  14.5 7.0 %collective-permute-start.5 = (bf16[2,128,128]{2,1,0:T(8,128)(2,1)S(1)}, bf16[2,128,128]{2,1,0:T(8,128)(2,1)S(1)}, u32[]{:S(2)}, u32[]{:S(2)}) collective-permute-start(bf16[2,128,128]{2,1,0:T(8,128)(2,1)S(1)} %get-tuple-element.34), channel_id=1, source_target_pairs={{0,8},{4,12},{8,0},{12,4},{16,24},{20,28},{24,16},{28,20},{1,9},{5... | collective-permute-start | bytes 196616 | tf_op jit(solution)/shard_map/ppermute | solution.py:188
  19.3 13.2 %collective-permute-start.2 = (bf16[9,32,256]{2,1,0:T(8,128)(2,1)S(1)}, bf16[9,32,256]{2,1,0:T(8,128)(2,1)S(1)}, u32[]{:S(2)}, u32[]{:S(2)}) collective-permute-start(bf16[9,32,256]{2,1,0:T(8,128)(2,1)S(1)} %pad_maximum_fusion.1), channel_id=1, source_target_pairs={{0,2},{1,3},{2,0},{3,1},{4,6},{5,7},{6,4},{7,5},{8,10},{9,11},{10,... | collective-permute-start | bytes 442376 | tf_op jit(solution)/shard_map/ppermute | solution.py:188
  21.5 5.7 %collective-permute-start.8 = (bf16[8,16,128]{2,1,0:T(8,128)(2,1)S(1)}, bf16[8,16,128]{2,1,0:T(8,128)(2,1)S(1)}, u32[]{:S(2)}, u32[]{:S(2)}) collective-permute-start(bf16[8,16,128]{2,1,0:T(8,128)(2,1)S(1)} %get-tuple-element.37), channel_id=1, source_target_pairs={{0,3},{1,2},{2,1},{3,0},{4,7},{5,6},{6,5},{7,4},{8,11},{9,10},{10,... | collective-permute-start | bytes 98312 | tf_op jit(solution)/shard_map/ppermute | solution.py:194
  21.6 5.7 %collective-permute-start.7 = (bf16[8,16,128]{2,1,0:T(8,128)(2,1)S(1)}, bf16[8,16,128]{2,1,0:T(8,128)(2,1)S(1)}, u32[]{:S(2)}, u32[]{:S(2)}) collective-permute-start(bf16[8,16,128]{2,1,0:T(8,128)(2,1)S(1)} %get-tuple-element.38), channel_id=1, source_target_pairs={{0,1},{1,0},{2,3},{3,2},{4,5},{5,4},{6,7},{7,6},{8,9},{9,8},{10,11... | collective-permute-start | bytes 98312 | tf_op jit(solution)/shard_map/ppermute | solution.py:188
  23.2 9.8 %collective-permute-start.12 = (bf16[2,128,256]{2,1,0:T(8,128)(2,1)S(1)}, bf16[2,128,256]{2,1,0:T(8,128)(2,1)S(1)}, u32[]{:S(2)}, u32[]{:S(2)}) collective-permute-start(bf16[2,128,256]{2,1,0:T(8,128)(2,1)S(1)} %get-tuple-element.21), channel_id=1, source_target_pairs={{8,16},{12,20},{16,8},{20,12},{9,17},{13,21},{17,9},{21,13},{10,18... | collective-permute-start | bytes 393224 | tf_op jit(solution)/shard_map/ppermute | solution.py:194
  23.9 10.7 %collective-permute-start.11 = (bf16[2,128,256]{2,1,0:T(8,128)(2,1)S(1)}, bf16[2,128,256]{2,1,0:T(8,128)(2,1)S(1)}, u32[]{:S(2)}, u32[]{:S(2)}) collective-permute-start(bf16[2,128,256]{2,1,0:T(8,128)(2,1)S(1)} %get-tuple-element.22), channel_id=1, source_target_pairs={{0,8},{4,12},{8,0},{12,4},{16,24},{20,28},{24,16},{28,20},{1,9},{5... | collective-permute-start | bytes 393224 | tf_op jit(solution)/shard_map/ppermute | solution.py:188
  31.7 2.2 %collective-permute-start.16 = (f32[9,64,256]{2,1,0:T(8,128)}, f32[9,64,256]{2,1,0:T(8,128)S(1)}, u32[]{:S(2)}, u32[]{:S(2)}) collective-permute-start(f32[9,64,256]{2,1,0:T(8,128)} %get-tuple-element.16), channel_id=1, source_target_pairs={{0,1},{1,0},{2,3},{3,2},{4,5},{5,4},{6,7},{7,6},{8,9},{9,8},{10,11... | collective-permute-start | bytes 1769480 | tf_op jit(solution)/shard_map/ppermute | solution.py:188
  32.5 11.4 %collective-permute-start.3 = (bf16[9,64,256]{2,1,0:T(8,128)(2,1)S(1)}, bf16[9,64,256]{2,1,0:T(8,128)(2,1)S(1)}, u32[]{:S(2)}, u32[]{:S(2)}) collective-permute-start(bf16[9,64,256]{2,1,0:T(8,128)(2,1)S(1)} %pad_maximum_fusion), channel_id=1, source_target_pairs={{0,1},{1,0},{2,3},{3,2},{4,5},{5,4},{6,7},{7,6},{8,9},{9,8},{10,11... | collective-permute-start | bytes 884744 | tf_op jit(solution)/shard_map/ppermute | solution.py:188
  33.1 10.8 %copy-start.6 = (bf16[2,128,256]{2,1,0:T(8,128)(2,1)}, bf16[2,128,256]{2,1,0:T(8,128)(2,1)S(1)}, u32[]{:S(2)}) copy-start(bf16[2,128,256]{2,1,0:T(8,128)(2,1)S(1)} %collective-permute-done.12.refs_3_) | copy-start | bytes 393220
  34.0 9.8 %collective-permute-start.17 = (f32[9,32,256]{2,1,0:T(8,128)S(1)}, f32[9,32,256]{2,1,0:T(8,128)S(1)}, u32[]{:S(2)}, u32[]{:S(2)}) collective-permute-start(f32[9,32,256]{2,1,0:T(8,128)S(1)} %get-tuple-element.18), channel_id=1, source_target_pairs={{0,2},{1,3},{2,0},{3,1},{4,6},{5,7},{6,4},{7,5},{8,10},{9,11},{10,... | collective-permute-start | bytes 884744 | tf_op jit(solution)/shard_map/ppermute | solution.py:188
  34.6 9.4 %collective-permute-start.14 = (bf16[8,16,256]{2,1,0:T(8,128)(2,1)S(1)}, bf16[8,16,256]{2,1,0:T(8,128)(2,1)S(1)}, u32[]{:S(2)}, u32[]{:S(2)}) collective-permute-start(bf16[8,16,256]{2,1,0:T(8,128)(2,1)S(1)} %get-tuple-element.23), channel_id=1, source_target_pairs={{0,3},{1,2},{2,1},{3,0},{4,7},{5,6},{6,5},{7,4},{8,11},{9,10},{10,... | collective-permute-start | bytes 196616 | tf_op jit(solution)/shard_map/ppermute | solution.py:194
  35.7 8.4 %collective-permute-start.13 = (bf16[8,16,256]{2,1,0:T(8,128)(2,1)S(1)}, bf16[8,16,256]{2,1,0:T(8,128)(2,1)S(1)}, u32[]{:S(2)}, u32[]{:S(2)}) collective-permute-start(bf16[8,16,256]{2,1,0:T(8,128)(2,1)S(1)} %get-tuple-element.24), channel_id=1, source_target_pairs={{0,1},{1,0},{2,3},{3,2},{4,5},{5,4},{6,7},{7,6},{8,9},{9,8},{10,11... | collective-permute-start | bytes 196616 | tf_op jit(solution)/shard_map/ppermute | solution.py:188
  43.9 16.3 %collective-permute-start.18 = (f32[9,16,256]{2,1,0:T(8,128)S(1)}, f32[9,16,256]{2,1,0:T(8,128)S(1)}, u32[]{:S(2)}, u32[]{:S(2)}) collective-permute-start(f32[9,16,256]{2,1,0:T(8,128)S(1)} %get-tuple-element.20), channel_id=1, source_target_pairs={{0,8},{4,12},{8,0},{12,4},{16,24},{20,28},{24,16},{28,20},{1,9},{5... | collective-permute-start | bytes 442376 | tf_op jit(solution)/shard_map/ppermute | solution.py:188
  51.3 4.7 %collective-permute-start.15 = (bf16[256,128]{1,0:T(8,128)(2,1)}, bf16[256,128]{1,0:T(8,128)(2,1)S(1)}, u32[]{:S(2)}, u32[]{:S(2)}) collective-permute-start(bf16[256,128]{1,0:T(8,128)(2,1)} %get-tuple-element.14), channel_id=1, source_target_pairs={{0,4},{4,0},{8,12},{12,8},{16,20},{20,16},{24,28},{28,24},{1,5},{5... | collective-permute-start | bytes 196616 | tf_op jit(solution)/shard_map/ppermute | solution.py:188
  55.5 8.3 %collective-permute-start.10 = (f32[256,256]{1,0:T(8,128)}, f32[256,256]{1,0:T(8,128)S(1)}, u32[]{:S(2)}, u32[]{:S(2)}) collective-permute-start(f32[256,256]{1,0:T(8,128)} %get-tuple-element.12), channel_id=1, source_target_pairs={{0,4},{4,0},{8,12},{12,8},{16,20},{20,16},{24,28},{28,24},{1,5},{5... | collective-permute-start | bytes 786440 | tf_op jit(solution)/shard_map/ppermute | solution.py:188
  60.2 5.8 %collective-permute-start.19 = (f32[9,8,256]{2,1,0:T(8,128)S(1)}, f32[9,8,256]{2,1,0:T(8,128)S(1)}, u32[]{:S(2)}, u32[]{:S(2)}) collective-permute-start(f32[9,8,256]{2,1,0:T(8,128)S(1)} %slice_add_fusion.4), channel_id=1, source_target_pairs={{0,16},{4,20},{8,24},{12,28},{16,0},{20,4},{24,8},{28,12},{1,17},{... | collective-permute-start | bytes 221192 | tf_op jit(solution)/shard_map/ppermute | solution.py:188
  (14 other events, 60.5 us)

commit v2 on v1

--- a/solution.py
+++ b/solution.py
@@ -7,7 +7,7 @@
 
 TILE = 32
 SLOT = 64
-VMEM = 60 * 1024 * 1024
+VMEM = 16 * 1024 * 1024
 NT = (((1,), (1,)), ((), ()))
 TN = (((0,), (0,)), ((), ()))
 bf16, f32 = jnp.bfloat16, jnp.float32
@@ -184,6 +184,10 @@
     grad_ref[...] = (dot(own_ref[...], own) + dot(pair_ref[...], pair)).astype(bf16)
 
 
+def after(array, *others):
+    return lax.optimization_barrier((array, *others))[0]
+
+
 def swap(array, axis, stride):
     return lax.ppermute(array, axis, [(i, i ^ stride) for i in range(lax.axis_size(axis))])
 
@@ -194,18 +198,23 @@
     return lax.ppermute(array, axis, [(i, j % size) for i, j in pairs if wrap or 0 <= j < size])
 
 
-def around(own, pair, rim):
-    lat, lon = lax.axis_index("lat"), lax.axis_index("lon")
+def row_halo(own, pair):
+    lat = lax.axis_index("lat")
     own_first = (lat & 1) != ((lat >> 1) & 1)
     near = swap(jnp.where(own_first, own, pair), "lat", 2)
     far = swap_across(jnp.where(own_first, pair, own), "lat", 2, False)
-    lines = (near, own, pair, far)
+    return near, far
+
+
+def edges(lines, rim):
     first = jnp.concatenate([v[:, :rim] for v in lines], axis=0)
     last = jnp.concatenate([v[:, -rim:] for v in lines], axis=0)
-    even = (lon & 1) == 0
-    core = swap(jnp.where(even, last, first), "lon", 1)
-    cross = swap_across(jnp.where(even, first, last), "lon", 1, True)
-    return near, far, core, cross
+    even = (lax.axis_index("lon") & 1) == 0
+    return jnp.where(even, last, first), jnp.where(even, first, last)
+
+
+def column_halo(to_core, to_cross):
+    return swap(to_core, "lon", 1), swap_across(to_cross, "lon", 1, True)
 
 
 def local(features, weight, tap_values, basis_index, half_width, cotangent):
@@ -231,16 +240,24 @@
     index = jnp.pad(index, fill, constant_values=-1)
     taps = jnp.pad(tap_values.astype(f32), fill)
 
-    feat_around = around(feat_own, feat_pair, rim)
-    cot_around = around(cot_own, cot_pair, rim)
-
+    near, far = row_halo(feat_own, feat_pair)
     full = weight.reshape(basis_count, lay.own, channels // lay.parts)
     for axis, stride, _ in lay.split:
         other = swap(full, axis, stride)
         low = (lax.axis_index(axis) // stride) % 2 == 0
         full = jnp.where(low, jnp.concatenate([full, other], 2), jnp.concatenate([other, full], 2))
-    for axis, stride, _ in reversed(lay.steps):
-        full = jnp.concatenate([full, swap(full, axis, stride)], axis=1)
+    gather = list(reversed(lay.steps))
+
+    def widen(full, step):
+        return jnp.concatenate([full, swap(full, step[0], step[1])], axis=1)
+
+    full = widen(full, gather[0])
+    full = widen(after(full, feat_pair), gather[1])
+    to_core, to_cross = edges((near, feat_own, feat_pair, far), rim)
+    feat_around = (near, far, *column_halo(to_core, to_cross))
+    full = after(full, to_core, to_cross)
+    for step in gather[2:-1]:
+        full = widen(full, step)
 
     cells = rows * cols
     ext = (4 * rows, cols + 2 * rim)
@@ -251,12 +268,16 @@
         feat_own, feat_pair, *feat_around, taps, index, cot_own, cot_pair,
         scratch=[pltpu.VMEM((*ext, half), bf16)],
     )
+    cot_near, cot_far = row_halo(after(cot_own, send), after(cot_pair, send))
+    full = widen(after(full, send), gather[-1])
+    sent = [send]
     for rank, (axis, stride, _) in enumerate(lay.steps):
         terms = (keep, swap(send, axis, stride))
         if rank + 1 < len(lay.steps):
             size = keep.shape[1] // 2
             send = terms[0][:, size:] + terms[1][:, size:]
             keep = terms[0][:, :size] + terms[1][:, :size]
+            sent.append(send)
     grad = terms[0] + terms[1]
     for axis, stride, _ in reversed(lay.split):
         size = grad.shape[2] // 2
@@ -265,16 +286,17 @@
         grad = lax.dynamic_slice_in_dim(grad, mine * size, size, 2) + other
     weight_grad = grad.reshape(basis_count, weight.shape[1])
 
+    cot_around = (cot_near, cot_far, *column_halo(*edges((cot_near, cot_own, cot_pair, cot_far), rim)))
     own_out, pair_out = call(mix_body, "mix", [((cells, channels), f32), ((cells, channels), f32)], full, basis_out)
-    pair_out = swap(pair_out, "lat", 1)
     own_grad, pair_grad = call(
         lambda *refs: backward_body(lay, offsets, *refs), "backward",
         [((cells, half), bf16), ((cells, half), bf16)],
-        cot_own, cot_pair, *cot_around, taps, index, full,
+        after(cot_own, pair_out, sent[-2]), cot_pair, *cot_around, taps, index, full,
         scratch=[pltpu.VMEM((*ext, channels), bf16),
                  pltpu.VMEM((-(-ext[1] // (2 * TILE)), basis_count * TILE, 2 * half), bf16),
                  pltpu.VMEM((2 * rows, ext[1] + TILE, half), f32)],
     )
+    pair_out = swap(pair_out, "lat", 1)
     pair_grad = swap(pair_grad, "lat", 1)
     output = (own_out + pair_out).astype(bf16)
     (input_grad,) = call(

time: 67.2 us -> 55.8 us (0.83)
  Pallas kernels: 14.2 us -> 6.08 us
  waiting for transfers between devices: 9.98 us -> 15.3 us
  local copies, waits for them, and re-layouts: 10.4 us -> 5.43 us
  starting transfers between devices: 29.1 us -> 27.4 us
  other arithmetic: 2 us -> 0.42 us
    pallas_call x4, Pallas kernels: 14.2 us -> 6.08 us  [call(): pl.pallas_call(body, name=name, out_shape=[jax.ShapeDtypeStruct(s, d) for...]
    ppermute x16, waiting for transfers between devices: 9.96 us -> 15.3 us  [swap(): lax.ppermute(array, axis, [(i, i ^ stride) for i in range(lax.axis_size(a...]
    ppermute x16, starting transfers between devices: 26.7 us -> 23.8 us  [swap(): lax.ppermute(array, axis, [(i, i ^ stride) for i in range(lax.axis_size(a...]
    unnamed x45 -> x13, local copies, waits for them, and re-layouts: 6.2 us -> 3.55 us
    ppermute x4, starting transfers between devices: 2.43 us -> 3.54 us  [swap_across(): lax.ppermute(array, axis, [(i, j % size) for i, j in pairs if wrap or 0 <...]
    convert_element_type x1, other arithmetic: 0.98 us -> 0.03 us  [local(): output = (own_out + pair_out).astype(bf16)]
    reshape x2, local copies, waits for them, and re-layouts: 2.46 us -> 1.56 us  [channels_first(): return jnp.transpose(v.reshape(rows, cols, channels), (2, 0, 1))]
    slice x8, local copies, waits for them, and re-layouts: 0.83 us -> 0.03 us  [edges(): last = jnp.concatenate([v[:, -rim:] for v in lines], axis=0)]
  transfers between devices with their start and end apart: 20 -> 20, of which waited for: 6 -> 6; matrix products, arithmetic and copies ran while one was open for 12% -> 7% of each run, Pallas kernels for 21% -> 11%
where the time goes in v2:
time: 55.8 us; the launch traced here: 55.6 us
  starting transfers between devices  27.4 us (49%)
  waiting for transfers between devices  15.3 us (27%)
  Pallas kernels  6.08 us (11%)
  local copies, waits for them, and re-layouts  5.43 us (10%)
  between operations  0.97 us (2%)
    ppermute x16, starting transfers between devices, swap(): lax.ppermute(array, axis, [(i, i ^ stride) for i in range(lax.axis_size(a...  23.8 us
    ppermute x16, waiting for transfers between devices, swap(): lax.ppermute(array, axis, [(i, i ^ stride) for i in range(lax.axis_size(a...  15.3 us
    pallas_call x4, Pallas kernels, call(): pl.pallas_call(body, name=name, out_shape=[jax.ShapeDtypeStruct(s, d) for...  6.08 us
    unnamed x13, local copies, waits for them, and re-layouts  3.55 us
    ppermute x4, starting transfers between devices, swap_across(): lax.ppermute(array, axis, [(i, j % size) for i, j in pairs if wrap or 0 <...  3.54 us
    reshape x2, local copies, waits for them, and re-layouts, channels_first(): return jnp.transpose(v.reshape(rows, cols, channels), (2, 0, 1))  1.56 us
  transfers between devices with their start and end apart: 20, of which 6 were waited for; matrix products, arithmetic and copies ran while one was open for 7% of the time, Pallas kernels for 11%

profile of v2, /device:TPU:0, one launch (start us, length us, event | category | flops | bytes accessed | tf_op | source)
XLA Modules:
  0.0 55.6 jit_solution(16528953261427063981)
XLA Ops:
  0.7 0.9 %copy.25 = bf16[256,2,128]{2,0,1:T(8,128)(2,1)S(1)} copy(bf16[256,2,128]{2,1,0:T(2,128)(2,1)} %param.6) | data formatting | bytes 262144 | tf_op args[0]
  1.8 3.0 %collective-permute-start.1 = (bf16[128,2,128]{0,2,1:T(8,128)(2,1)S(1)}, bf16[128,2,128]{0,2,1:T(8,128)(2,1)S(1)}, u32[]{:S(2)}, u32[]{:S(2)}) collective-permute-start(bf16[128,2,128]{0,2,1:T(8,128)(2,1)S(1)} %copy.26), channel_id=1, source_target_pairs={{0,4},{4,0},{8,12},{12,8},{16,20},{20,16},{24,28},{28,24},{1,5},{5... | collective-permute-start | bytes 196616 | tf_op jit(solution)/shard_map/ppermute | solution.py:192
  4.8 1.0 %copy.30 = bf16[256,2,128]{0,2,1:T(8,128)(2,1)S(1)} copy(bf16[256,2,128]{2,1,0:T(2,128)(2,1)} %param.11) | data formatting | bytes 262144 | tf_op args[5]
  5.9 0.9 %copy.34 = bf16[2,8,8,256]{3,2,1,0:T(8,128)(2,1)S(1)} copy(bf16[2,8,8,256]{3,1,2,0:T(8,128)(2,1)} %bitcast.43) | data formatting | bytes 131072
  6.8 3.1 %collective-permute-start = (bf16[9,8,256]{2,1,0:T(8,128)(2,1)S(1)}, bf16[9,8,256]{2,1,0:T(8,128)(2,1)S(1)}, u32[]{:S(2)}, u32[]{:S(2)}) collective-permute-start(bf16[9,8,256]{2,1,0:T(8,128)(2,1)S(1)} %slice.138), channel_id=1, source_target_pairs={{0,16},{4,20},{8,24},{12,28},{16,0},{20,4},{24,8},{28,12},{1,17},{... | collective-permute-start | bytes 110600 | tf_op jit(solution)/shard_map/ppermute | solution.py:192
  10.3 1.6 %collective-permute-done = bf16[9,8,256]{2,1,0:T(8,128)(2,1)S(1)} collective-permute-done((bf16[9,8,256]{2,1,0:T(8,128)(2,1)S(1)}, bf16[9,8,256]{2,1,0:T(8,128)(2,1)S(1)}, u32[]{:S(2)}, u32[]{:S(2)}) %collective-permute-start) | collective-permute-done | bytes 36896 | tf_op jit(solution)/shard_map/ppermute | solution.py:192
  11.9 1.9 %collective-permute-start.3 = (bf16[2,128,128]{2,1,0:T(8,128)(2,1)S(1)}, bf16[2,128,128]{2,1,0:T(8,128)(2,1)S(1)}, u32[]{:S(2)}, u32[]{:S(2)}) collective-permute-start(bf16[2,128,128]{2,1,0:T(8,128)(2,1)S(1)} %get-tuple-element.45), channel_id=1, source_target_pairs={{0,8},{4,12},{8,0},{12,4},{16,24},{20,28},{24,16},{28,20},{1,9},{5... | collective-permute-start | bytes 196616 | tf_op jit(solution)/shard_map/ppermute | solution.py:192
  14.5 4.7 %collective-permute-start.2 = (bf16[9,16,256]{2,1,0:T(8,128)(2,1)S(1)}, bf16[9,16,256]{2,1,0:T(8,128)(2,1)S(1)}, u32[]{:S(2)}, u32[]{:S(2)}) collective-permute-start(bf16[9,16,256]{2,1,0:T(8,128)(2,1)S(1)} %pad_maximum_fusion.2), channel_id=1, source_target_pairs={{0,8},{4,12},{8,0},{12,4},{16,24},{20,28},{24,16},{28,20},{1,9},{5... | collective-permute-start | bytes 221192 | tf_op jit(solution)/shard_map/ppermute | solution.py:192
  19.4 1.6 %collective-permute-start.7 = (bf16[8,16,128]{2,1,0:T(8,128)(2,1)S(1)}, bf16[8,16,128]{2,1,0:T(8,128)(2,1)S(1)}, u32[]{:S(2)}, u32[]{:S(2)}) collective-permute-start(bf16[8,16,128]{2,1,0:T(8,128)(2,1)S(1)} %get-tuple-element.49), channel_id=1, source_target_pairs={{0,3},{1,2},{2,1},{3,0},{4,7},{5,6},{6,5},{7,4},{8,11},{9,10},{10,... | collective-permute-start | bytes 98312 | tf_op jit(solution)/shard_map/ppermute | solution.py:198
  21.6 1.6 %collective-permute-start.5 = (bf16[9,32,256]{2,1,0:T(8,128)(2,1)S(1)}, bf16[9,32,256]{2,1,0:T(8,128)(2,1)S(1)}, u32[]{:S(2)}, u32[]{:S(2)}) collective-permute-start(bf16[9,32,256]{2,1,0:T(8,128)(2,1)S(1)} %pad_maximum_fusion.1), channel_id=1, source_target_pairs={{0,2},{1,3},{2,0},{3,1},{4,6},{5,7},{6,4},{7,5},{8,10},{9,11},{10,... | collective-permute-start | bytes 442376 | tf_op jit(solution)/shard_map/ppermute | solution.py:192
  23.2 1.5 %forward.1 = (bf16[9,512,128]{2,1,0:T(8,128)(2,1)S(1)}, f32[9,64,256]{2,1,0:T(8,128)S(1)}, f32[9,64,256]{2,1,0:T(8,128)S(1)}) custom-call(bf16[2,128,128]{2,1,0:T(8,128)(2,1)S(1)} %bitcast.30, bf16[2,128,128]{2,1,0:T(8,128)(2,1)S(1)} %bitcast.33, bf16[2,128,128]{2,1,0:T(8,128)(2,1)S(1)} %collective-permute-done.3.refs_2_, ...), custom_call_target="tpu_custom_call" | custom-call | tf_op jit(solution)/shard_map/forward/pallas_call | solution.py:22
  24.9 2.2 %collective-permute-start.13 = (bf16[2,128,256]{2,1,0:T(8,128)(2,1)S(1)}, bf16[2,128,256]{2,1,0:T(8,128)(2,1)S(1)}, u32[]{:S(2)}, u32[]{:S(2)}) collective-permute-start(bf16[2,128,256]{2,1,0:T(8,128)(2,1)S(1)} %get-tuple-element.34), channel_id=1, source_target_pairs={{0,8},{4,12},{8,0},{12,4},{16,24},{20,28},{24,16},{28,20},{1,9},{5... | collective-permute-start | bytes 393224 | tf_op jit(solution)/shard_map/ppermute | solution.py:192
  27.9 3.1 %collective-permute-done.13.refs_2_ = bf16[2,128,256]{2,1,0:T(8,128)(2,1)S(1)} collective-permute-done((bf16[2,128,256]{2,1,0:T(8,128)(2,1)S(1)}, bf16[2,128,256]{2,1,0:T(8,128)(2,1)S(1)}, u32[]{:S(2)}, u32[]{:S(2)}) %collective-permute-start.13) | collective-permute-done | bytes 131104 | tf_op jit(solution)/shard_map/ppermute | solution.py:192
  31.2 1.6 %collective-permute-start.12 = (f32[9,32,256]{2,1,0:T(8,128)S(1)}, f32[9,32,256]{2,1,0:T(8,128)S(1)}, u32[]{:S(2)}, u32[]{:S(2)}) collective-permute-start(f32[9,32,256]{2,1,0:T(8,128)S(1)} %get-tuple-element.30), channel_id=1, source_target_pairs={{0,2},{1,3},{2,0},{3,1},{4,6},{5,7},{6,4},{7,5},{8,10},{9,11},{10,... | collective-permute-start | bytes 884744 | tf_op jit(solution)/shard_map/ppermute | solution.py:192
  33.5 7.2 %collective-permute-done.12 = f32[9,32,256]{2,1,0:T(8,128)S(1)} collective-permute-done((f32[9,32,256]{2,1,0:T(8,128)S(1)}, f32[9,32,256]{2,1,0:T(8,128)S(1)}, u32[]{:S(2)}, u32[]{:S(2)}) %collective-permute-start.12) | collective-permute-done | bytes 294944 | tf_op jit(solution)/shard_map/ppermute | solution.py:192
  40.8 1.5 %collective-permute-start.18 = (f32[9,16,256]{2,1,0:T(8,128)S(1)}, f32[9,16,256]{2,1,0:T(8,128)S(1)}, u32[]{:S(2)}, u32[]{:S(2)}) collective-permute-start(f32[9,16,256]{2,1,0:T(8,128)S(1)} %get-tuple-element.32), channel_id=1, source_target_pairs={{0,8},{4,12},{8,0},{12,4},{16,24},{20,28},{24,16},{28,20},{1,9},{5... | collective-permute-start | bytes 442376 | tf_op jit(solution)/shard_map/ppermute | solution.py:192
  42.8 1.6 %collective-permute-start.10 = (f32[256,256]{1,0:T(8,128)S(1)}, f32[256,256]{1,0:T(8,128)S(1)}, u32[]{:S(2)}, u32[]{:S(2)}) collective-permute-start(f32[256,256]{1,0:T(8,128)S(1)} %get-tuple-element.22), channel_id=1, source_target_pairs={{0,4},{4,0},{8,12},{12,8},{16,20},{20,16},{24,28},{28,24},{1,5},{5... | collective-permute-start | bytes 786440 | tf_op jit(solution)/shard_map/ppermute | solution.py:192
  44.4 3.7 %backward.1 = (bf16[256,128]{1,0:T(8,128)(2,1)S(1)}, bf16[256,128]{1,0:T(8,128)(2,1)S(1)}) custom-call(bf16[2,128,256]{2,1,0:T(8,128)(2,1)S(1)} %bitcast.24, bf16[2,128,256]{2,1,0:T(8,128)(2,1)S(1)} %bitcast.28, bf16[2,128,256]{2,1,0:T(8,128)(2,1)S(1)} %collective-permute-done.13.refs_2_, bf16[2,128,256]{2,1,0:T(8,128)(2,1)S(1)} %collective-permute-done.14.refs_3_, ...), custom_call_target="tpu_custom_call" | custom-call | tf_op jit(solution)/shard_map/backward/pallas_call | solution.py:22
  48.7 1.5 %collective-permute-start.19 = (f32[9,8,256]{2,1,0:T(8,128)S(1)}, f32[9,8,256]{2,1,0:T(8,128)S(1)}, u32[]{:S(2)}, u32[]{:S(2)}) collective-permute-start(f32[9,8,256]{2,1,0:T(8,128)S(1)} %slice_add_fusion.4), channel_id=1, source_target_pairs={{0,16},{4,20},{8,24},{12,28},{16,0},{20,4},{24,8},{28,12},{1,17},{... | collective-permute-start | bytes 221192 | tf_op jit(solution)/shard_map/ppermute | solution.py:192
  50.3 0.8 %copy.32 = bf16[2,128,256]{1,0,2:T(2,128)(2,1)} copy(bf16[2,128,256]{2,1,0:T(8,128)(2,1)S(1)} %bitcast.34) | data formatting | bytes 262144 | tf_op jit(solution)/shard_map/reshape | solution.py:307
  51.1 1.4 %collective-permute-done.17.refs_1_ = bf16[256,128]{1,0:T(8,128)(2,1)S(1)} collective-permute-done((bf16[256,128]{1,0:T(8,128)(2,1)S(1)}, bf16[256,128]{1,0:T(8,128)(2,1)S(1)}, u32[]{:S(2)}, u32[]{:S(2)}) %collective-permute-start.17) | collective-permute-done | bytes 65568 | tf_op jit(solution)/shard_map/ppermute | solution.py:192
  52.8 0.8 %copy.33 = bf16[2,128,256]{1,0,2:T(2,128)(2,1)} copy(bf16[2,128,256]{2,1,0:T(8,128)(2,1)S(1)} %bitcast.31) | data formatting | bytes 262144 | tf_op jit(solution)/shard_map/reshape | solution.py:307
  53.5 1.3 %collective-permute-done.19 = f32[9,8,256]{2,1,0:T(8,128)S(1)} collective-permute-done((f32[9,8,256]{2,1,0:T(8,128)S(1)}, f32[9,8,256]{2,1,0:T(8,128)S(1)}, u32[]{:S(2)}, u32[]{:S(2)}) %collective-permute-start.19) | collective-permute-done | bytes 73760 | tf_op jit(solution)/shard_map/ppermute | solution.py:192
  54.9 0.7 %copy.35 = f32[2,8,8,256]{3,1,2,0:T(8,128)} copy(f32[2,8,8,256]{3,2,1,0:T(8,128)S(1)} %bitcast.36) | data formatting | bytes 262144
  (65 shorter events, 5.2 us)
Async XLA Ops:
  0.6 9.4 %copy-start.1 = (bf16[16,5,33]{2,0,1:T(8,128)(2,1)S(1)}, bf16[16,5,33]{2,0,1:T(8,128)(2,1)}, u32[]{:S(2)}) copy-start(bf16[16,5,33]{2,0,1:T(8,128)(2,1)} %param.8) | copy-start | bytes 15844
  0.6 9.5 %copy-start.2 = (s32[16]{0:T(128)S(1)}, s32[16]{0:T(128)}, u32[]{:S(2)}) copy-start(s32[16]{0:T(128)} %param.10) | copy-start | bytes 196
  0.7 9.5 %copy-start = (s32[16,5,33]{2,0,1:T(8,128)S(1)}, s32[16,5,33]{2,0,1:T(8,128)}, u32[]{:S(2)}) copy-start(s32[16,5,33]{2,0,1:T(8,128)} %param.9) | copy-start | bytes 31684
  1.8 10.1 %collective-permute-start.1 = (bf16[128,2,128]{0,2,1:T(8,128)(2,1)S(1)}, bf16[128,2,128]{0,2,1:T(8,128)(2,1)S(1)}, u32[]{:S(2)}, u32[]{:S(2)}) collective-permute-start(bf16[128,2,128]{0,2,1:T(8,128)(2,1)S(1)} %copy.26), channel_id=1, source_target_pairs={{0,4},{4,0},{8,12},{12,8},{16,20},{20,16},{24,28},{28,24},{1,5},{5... | collective-permute-start | bytes 196616 | tf_op jit(solution)/shard_map/ppermute | solution.py:192
  5.8 15.2 %collective-permute-start.8 = (bf16[256,2,128]{0,2,1:T(8,128)(2,1)S(1)}, bf16[256,2,128]{0,2,1:T(8,128)(2,1)S(1)}, u32[]{:S(2)}, u32[]{:S(2)}) collective-permute-start(bf16[256,2,128]{0,2,1:T(8,128)(2,1)S(1)} %copy.30), channel_id=1, source_target_pairs={{0,4},{4,0},{8,12},{12,8},{16,20},{20,16},{24,28},{28,24},{1,5},{5... | collective-permute-start | bytes 393224 | tf_op jit(solution)/shard_map/ppermute | solution.py:192
  6.8 5.1 %collective-permute-start = (bf16[9,8,256]{2,1,0:T(8,128)(2,1)S(1)}, bf16[9,8,256]{2,1,0:T(8,128)(2,1)S(1)}, u32[]{:S(2)}, u32[]{:S(2)}) collective-permute-start(bf16[9,8,256]{2,1,0:T(8,128)(2,1)S(1)} %slice.138), channel_id=1, source_target_pairs={{0,16},{4,20},{8,24},{12,28},{16,0},{20,4},{24,8},{28,12},{1,17},{... | collective-permute-start | bytes 110600 | tf_op jit(solution)/shard_map/ppermute | solution.py:192
  11.9 7.3 %collective-permute-start.3 = (bf16[2,128,128]{2,1,0:T(8,128)(2,1)S(1)}, bf16[2,128,128]{2,1,0:T(8,128)(2,1)S(1)}, u32[]{:S(2)}, u32[]{:S(2)}) collective-permute-start(bf16[2,128,128]{2,1,0:T(8,128)(2,1)S(1)} %get-tuple-element.45), channel_id=1, source_target_pairs={{0,8},{4,12},{8,0},{12,4},{16,24},{20,28},{24,16},{28,20},{1,9},{5... | collective-permute-start | bytes 196616 | tf_op jit(solution)/shard_map/ppermute | solution.py:192
  13.9 5.4 %collective-permute-start.4 = (bf16[2,128,128]{2,1,0:T(8,128)(2,1)S(1)}, bf16[2,128,128]{2,1,0:T(8,128)(2,1)S(1)}, u32[]{:S(2)}, u32[]{:S(2)}) collective-permute-start(bf16[2,128,128]{2,1,0:T(8,128)(2,1)S(1)} %get-tuple-element.46), channel_id=1, source_target_pairs={{8,16},{12,20},{16,8},{20,12},{9,17},{13,21},{17,9},{21,13},{10,18... | collective-permute-start | bytes 196616 | tf_op jit(solution)/shard_map/ppermute | solution.py:198
  14.5 7.1 %collective-permute-start.2 = (bf16[9,16,256]{2,1,0:T(8,128)(2,1)S(1)}, bf16[9,16,256]{2,1,0:T(8,128)(2,1)S(1)}, u32[]{:S(2)}, u32[]{:S(2)}) collective-permute-start(bf16[9,16,256]{2,1,0:T(8,128)(2,1)S(1)} %pad_maximum_fusion.2), channel_id=1, source_target_pairs={{0,8},{4,12},{8,0},{12,4},{16,24},{20,28},{24,16},{28,20},{1,9},{5... | collective-permute-start | bytes 221192 | tf_op jit(solution)/shard_map/ppermute | solution.py:192
  19.3 3.9 %collective-permute-start.6 = (bf16[8,16,128]{2,1,0:T(8,128)(2,1)S(1)}, bf16[8,16,128]{2,1,0:T(8,128)(2,1)S(1)}, u32[]{:S(2)}, u32[]{:S(2)}) collective-permute-start(bf16[8,16,128]{2,1,0:T(8,128)(2,1)S(1)} %get-tuple-element.50), channel_id=1, source_target_pairs={{0,1},{1,0},{2,3},{3,2},{4,5},{5,4},{6,7},{7,6},{8,9},{9,8},{10,11... | collective-permute-start | bytes 98312 | tf_op jit(solution)/shard_map/ppermute | solution.py:192
  19.4 3.8 %collective-permute-start.7 = (bf16[8,16,128]{2,1,0:T(8,128)(2,1)S(1)}, bf16[8,16,128]{2,1,0:T(8,128)(2,1)S(1)}, u32[]{:S(2)}, u32[]{:S(2)}) collective-permute-start(bf16[8,16,128]{2,1,0:T(8,128)(2,1)S(1)} %get-tuple-element.49), channel_id=1, source_target_pairs={{0,3},{1,2},{2,1},{3,0},{4,7},{5,6},{6,5},{7,4},{8,11},{9,10},{10,... | collective-permute-start | bytes 98312 | tf_op jit(solution)/shard_map/ppermute | solution.py:198
  21.6 6.1 %collective-permute-start.5 = (bf16[9,32,256]{2,1,0:T(8,128)(2,1)S(1)}, bf16[9,32,256]{2,1,0:T(8,128)(2,1)S(1)}, u32[]{:S(2)}, u32[]{:S(2)}) collective-permute-start(bf16[9,32,256]{2,1,0:T(8,128)(2,1)S(1)} %pad_maximum_fusion.1), channel_id=1, source_target_pairs={{0,2},{1,3},{2,0},{3,1},{4,6},{5,7},{6,4},{7,5},{8,10},{9,11},{10,... | collective-permute-start | bytes 442376 | tf_op jit(solution)/shard_map/ppermute | solution.py:192
  24.7 6.4 %collective-permute-start.11 = (f32[9,64,256]{2,1,0:T(8,128)S(1)}, f32[9,64,256]{2,1,0:T(8,128)S(1)}, u32[]{:S(2)}, u32[]{:S(2)}) collective-permute-start(f32[9,64,256]{2,1,0:T(8,128)S(1)} %get-tuple-element.18), channel_id=1, source_target_pairs={{0,1},{1,0},{2,3},{3,2},{4,5},{5,4},{6,7},{7,6},{8,9},{9,8},{10,11... | collective-permute-start | bytes 1769480 | tf_op jit(solution)/shard_map/ppermute | solution.py:192
  24.9 6.2 %collective-permute-start.13 = (bf16[2,128,256]{2,1,0:T(8,128)(2,1)S(1)}, bf16[2,128,256]{2,1,0:T(8,128)(2,1)S(1)}, u32[]{:S(2)}, u32[]{:S(2)}) collective-permute-start(bf16[2,128,256]{2,1,0:T(8,128)(2,1)S(1)} %get-tuple-element.34), channel_id=1, source_target_pairs={{0,8},{4,12},{8,0},{12,4},{16,24},{20,28},{24,16},{28,20},{1,9},{5... | collective-permute-start | bytes 393224 | tf_op jit(solution)/shard_map/ppermute | solution.py:192
  27.1 5.7 %collective-permute-start.14 = (bf16[2,128,256]{2,1,0:T(8,128)(2,1)S(1)}, bf16[2,128,256]{2,1,0:T(8,128)(2,1)S(1)}, u32[]{:S(2)}, u32[]{:S(2)}) collective-permute-start(bf16[2,128,256]{2,1,0:T(8,128)(2,1)S(1)} %get-tuple-element.33), channel_id=1, source_target_pairs={{8,16},{12,20},{16,8},{20,12},{9,17},{13,21},{17,9},{21,13},{10,18... | collective-permute-start | bytes 393224 | tf_op jit(solution)/shard_map/ppermute | solution.py:198
  27.8 14.5 %collective-permute-start.9 = (bf16[9,64,256]{2,1,0:T(8,128)(2,1)S(1)}, bf16[9,64,256]{2,1,0:T(8,128)(2,1)S(1)}, u32[]{:S(2)}, u32[]{:S(2)}) collective-permute-start(bf16[9,64,256]{2,1,0:T(8,128)(2,1)S(1)} %pad_maximum_fusion), channel_id=1, source_target_pairs={{0,1},{1,0},{2,3},{3,2},{4,5},{5,4},{6,7},{7,6},{8,9},{9,8},{10,11... | collective-permute-start | bytes 884744 | tf_op jit(solution)/shard_map/ppermute | solution.py:192
  31.2 9.5 %collective-permute-start.12 = (f32[9,32,256]{2,1,0:T(8,128)S(1)}, f32[9,32,256]{2,1,0:T(8,128)S(1)}, u32[]{:S(2)}, u32[]{:S(2)}) collective-permute-start(f32[9,32,256]{2,1,0:T(8,128)S(1)} %get-tuple-element.30), channel_id=1, source_target_pairs={{0,2},{1,3},{2,0},{3,1},{4,6},{5,7},{6,4},{7,5},{8,10},{9,11},{10,... | collective-permute-start | bytes 884744 | tf_op jit(solution)/shard_map/ppermute | solution.py:192
  32.8 11.6 %collective-permute-start.15 = (bf16[8,16,256]{2,1,0:T(8,128)(2,1)S(1)}, bf16[8,16,256]{2,1,0:T(8,128)(2,1)S(1)}, u32[]{:S(2)}, u32[]{:S(2)}) collective-permute-start(bf16[8,16,256]{2,1,0:T(8,128)(2,1)S(1)} %get-tuple-element.36), channel_id=1, source_target_pairs={{0,1},{1,0},{2,3},{3,2},{4,5},{5,4},{6,7},{7,6},{8,9},{9,8},{10,11... | collective-permute-start | bytes 196616 | tf_op jit(solution)/shard_map/ppermute | solution.py:192
  32.9 11.5 %collective-permute-start.16 = (bf16[8,16,256]{2,1,0:T(8,128)(2,1)S(1)}, bf16[8,16,256]{2,1,0:T(8,128)(2,1)S(1)}, u32[]{:S(2)}, u32[]{:S(2)}) collective-permute-start(bf16[8,16,256]{2,1,0:T(8,128)(2,1)S(1)} %get-tuple-element.35), channel_id=1, source_target_pairs={{0,3},{1,2},{2,1},{3,0},{4,7},{5,6},{6,5},{7,4},{8,11},{9,10},{10,... | collective-permute-start | bytes 196616 | tf_op jit(solution)/shard_map/ppermute | solution.py:198
  40.8 8.0 %collective-permute-start.18 = (f32[9,16,256]{2,1,0:T(8,128)S(1)}, f32[9,16,256]{2,1,0:T(8,128)S(1)}, u32[]{:S(2)}, u32[]{:S(2)}) collective-permute-start(f32[9,16,256]{2,1,0:T(8,128)S(1)} %get-tuple-element.32), channel_id=1, source_target_pairs={{0,8},{4,12},{8,0},{12,4},{16,24},{20,28},{24,16},{28,20},{1,9},{5... | collective-permute-start | bytes 442376 | tf_op jit(solution)/shard_map/ppermute | solution.py:192
  42.8 7.5 %collective-permute-start.10 = (f32[256,256]{1,0:T(8,128)S(1)}, f32[256,256]{1,0:T(8,128)S(1)}, u32[]{:S(2)}, u32[]{:S(2)}) collective-permute-start(f32[256,256]{1,0:T(8,128)S(1)} %get-tuple-element.22), channel_id=1, source_target_pairs={{0,4},{4,0},{8,12},{12,8},{16,20},{20,16},{24,28},{28,24},{1,5},{5... | collective-permute-start | bytes 786440 | tf_op jit(solution)/shard_map/ppermute | solution.py:192
  48.2 4.3 %collective-permute-start.17 = (bf16[256,128]{1,0:T(8,128)(2,1)S(1)}, bf16[256,128]{1,0:T(8,128)(2,1)S(1)}, u32[]{:S(2)}, u32[]{:S(2)}) collective-permute-start(bf16[256,128]{1,0:T(8,128)(2,1)S(1)} %get-tuple-element.28), channel_id=1, source_target_pairs={{0,4},{4,0},{8,12},{12,8},{16,20},{20,16},{24,28},{28,24},{1,5},{5... | collective-permute-start | bytes 196616 | tf_op jit(solution)/shard_map/ppermute | solution.py:192
  48.7 6.1 %collective-permute-start.19 = (f32[9,8,256]{2,1,0:T(8,128)S(1)}, f32[9,8,256]{2,1,0:T(8,128)S(1)}, u32[]{:S(2)}, u32[]{:S(2)}) collective-permute-start(f32[9,8,256]{2,1,0:T(8,128)S(1)} %slice_add_fusion.4), channel_id=1, source_target_pairs={{0,16},{4,20},{8,24},{12,28},{16,0},{20,4},{24,8},{28,12},{1,17},{... | collective-permute-start | bytes 221192 | tf_op jit(solution)/shard_map/ppermute | solution.py:192

commit v3 on v2

v3 whole, which is shorter than its diff:
```python
import jax
import jax.numpy as jnp
from jax import lax
from jax.experimental import pallas as pl
from jax.experimental.pallas import tpu as pltpu
from jax.sharding import PartitionSpec as P

TILE = 32
SLOT = 64
VMEM = 16 * 1024 * 1024
NT = (((1,), (1,)), ((), ()))
TN = (((0,), (0,)), ((), ()))
bf16, f32 = jnp.bfloat16, jnp.float32


def dot(a, b, dims=(((1,), (0,)), ((), ()))):
    return lax.dot_general(a, b, dims, preferred_element_type=f32)


def call(body, name, flops, outs, *args, scratch=()):
    in_vmem = pl.BlockSpec(memory_space=pltpu.VMEM)
    return pl.pallas_call(
        body,
        name=name,
        out_shape=[jax.ShapeDtypeStruct(s, d) for s, d in outs],
        in_specs=[in_vmem for _ in args],
        out_specs=[in_vmem for _ in outs],
        scratch_shapes=list(scratch),
        cost_estimate=pl.CostEstimate(
            flops=flops, transcendentals=0, bytes_accessed=sum(v.size * v.dtype.itemsize for v in args)
        ),
        compiler_params=pltpu.CompilerParams(vmem_limit_bytes=VMEM),
    )(*args)


def log2(size):
    return size.bit_length() - 1


class Layout:
    def __init__(self, channels, lats, lons):
        self.channels, self.lons = channels, lons
        devices = lats * lons
        self.parts = max(1, devices // channels)
        self.own = channels * self.parts // devices
        self.bits = [1 << b for b in range(devices.bit_length() - 1) if 1 << b != lons]
        self.merged = lats == 8 and lons == 4 and self.parts == 1
        if self.merged:
            steps = [("lon", 1), ("lat", 2), ("lon", 3), ("lat", 4)]
        else:
            steps = [("lon", 1 << b) for b in range(lons.bit_length() - 1)]
            steps += [("lat", 2 << b) for b in range(lats.bit_length() - 2)]
        steps = [(axis, flip, flip if axis == "lon" else flip * lons) for axis, flip in steps]
        self.split = [s for s in steps if s[2] < self.parts]
        self.steps = [s for s in steps if s[2] >= self.parts]
        self.pair = lons // self.parts * self.own

    def odd(self):
        return lax.axis_index("lat") & 1

    def places(self, shape, dim):
        place = lax.broadcasted_iota(jnp.int32, shape, dim)
        owner = lax.axis_index("lat") * self.lons + lax.axis_index("lon")
        for rank, (_, _, flip) in enumerate(self.steps):
            owner = owner ^ (((place >> log2(self.channels >> (rank + 2))) & 1) * flip)
        channel = place & (self.own - 1)
        for bit in self.bits:
            if bit >= self.parts:
                value = bit // self.parts * self.own
                value = value // 2 if value > self.pair else value
                channel = channel + (((owner >> log2(bit)) & 1) << log2(value))
        return channel

    def whole(self, channel, odd):
        low = log2(self.pair)
        return ((channel >> low) << (low + 1)) + (odd << low) + (channel & (self.pair - 1))


def bands(taps_ref, index_ref, row, basis_count, picked, offsets):
    taps, index = taps_ref[row], index_ref[row]

    def line(v, a, none):
        return v[a : a + 1] if 0 <= a < offsets else jnp.full((1, SLOT), none, v.dtype)

    def paired(v, none):
        return [
            jnp.concatenate([line(v, a, none), line(v, b, none)], axis=1)
            for a, b in zip(picked[::2], picked[1::2] + [-1] * (len(picked) % 2))
        ]

    taps, index = paired(taps, 0.0), paired(index, -1)
    parts = []
    for basis in range(basis_count):
        pieces = []
        for value, kind in zip(taps, index):
            piece = jnp.broadcast_to(jnp.where(kind == basis, value, 0.0), (TILE, 2 * SLOT))
            pieces.append(pltpu.roll(piece, 0, 1, stride=1, stride_axis=0))
        parts.append(jnp.concatenate(pieces, axis=1).astype(bf16))
    return jnp.concatenate(parts, axis=0)


def place_rows(scr, move, own_ref, pair_ref, near_ref, next_ref, core_ref, cross_ref):
    rows, cols, channels = own_ref.shape
    lat, lon = lax.axis_index("lat"), lax.axis_index("lon")
    odd, flip = lat & 1, (lat >> 1) & 1
    even_col = (lon & 1) == 0
    rim = (scr.shape[1] - cols) // 2
    wide = near_ref.shape[1] // channels

    def part(ref, first, row, length):
        low = (first + row // wide) * length
        return ref[low : low + length, row % wide * channels : (row % wide + 1) * channels]

    slots = ((1 - flip) * 3 * rows, (1 + odd) * rows, (2 - odd) * rows, flip * 3 * rows)
    for rank, slot in enumerate(slots):
        for row in range(rows):
            line = part((near_ref, next_ref)[rank // 3], 0, row, cols) if rank in (0, 3) else (own_ref, pair_ref)[rank - 1][row]
            core = part(core_ref, rank * (rows // wide), row, rim)
            cross = part(cross_ref, rank * (rows // wide), row, rim)
            scr[slot + row, rim : rim + cols, :] = move(line)
            scr[slot + row, :rim, :] = move(jnp.where(even_col, cross, core))
            scr[slot + row, rim + cols :, :] = move(jnp.where(even_col, core, cross))


def forward_body(lay, offsets, own_ref, pair_ref, near_ref, next_ref, core_ref, cross_ref, taps_ref, index_ref,
                 own_cot_ref, pair_cot_ref, out_ref, send_ref, keep_ref, ext_scr):
    rows, cols, channels = own_ref.shape
    basis_count = out_ref.shape[0]
    odd = lay.odd()
    shape = (channels, channels)
    pick = (lax.broadcasted_iota(jnp.int32, shape, 0) == lay.places(shape, 1)).astype(bf16)
    place_rows(ext_scr, lambda v: dot(v, pick).astype(bf16), own_ref, pair_ref, near_ref, next_ref, core_ref, cross_ref)
    first_row = (lax.axis_index("lat") - odd) * rows
    for line in range(2 * rows):
        low = (odd if line < rows else 1 - odd) * rows + line % rows
        picked = list(range(offsets))
        band = bands(taps_ref, index_ref, first_row + low + rows, basis_count, picked, offsets)[:, : offsets * SLOT]
        for first in range(0, cols, 2 * TILE):
            source = [
                jnp.concatenate([ext_scr[low + a, start : start + SLOT, :] for a in range(offsets)], axis=0)
                for start in (first, first + TILE)
            ]
            moved = dot(band, jnp.concatenate(source, axis=1)).astype(bf16)
            for basis in range(basis_count):
                for side in range(2):
                    start = line * cols + first + side * TILE
                    piece = moved[basis * TILE : (basis + 1) * TILE, side * channels : (side + 1) * channels]
                    out_ref[basis, start : start + TILE, :] = piece
    cot = jnp.concatenate([own_cot_ref[...], pair_cot_ref[...]], axis=0).reshape(2 * rows * cols, own_cot_ref.shape[2])
    half = channels // 2
    for basis in range(basis_count):
        terms = dot(out_ref[basis], cot, TN)
        send_ref[basis] = terms[half:].astype(send_ref.dtype)
        keep_ref[basis] = terms[:half]


def mix_body(weight_ref, basis_ref, own_ref, pair_ref):
    basis_count, channels, outs = weight_ref.shape
    cells = own_ref.shape[0]
    source = jnp.concatenate([basis_ref[basis] for basis in range(basis_count)], axis=1)
    total = dot(source, weight_ref[...].reshape(basis_count * channels, outs))
    own_ref[...] = total[:cells]
    pair_ref[...] = total[cells:].astype(pair_ref.dtype)


def backward_body(lay, offsets, own_ref, pair_ref, near_ref, next_ref, core_ref, cross_ref, taps_ref, index_ref,
                  weight_ref, own_grad_ref, pair_grad_ref, ext_scr, basis_scr, band_scr, sum_scr):
    rows, cols, _ = own_ref.shape
    basis_count, channels, outs = weight_ref.shape
    odd = lay.odd()
    place_rows(ext_scr, lambda v: v, own_ref, pair_ref, near_ref, next_ref, core_ref, cross_ref)
    weight = weight_ref[...].reshape(basis_count * channels, outs)
    first_row = (lax.axis_index("lat") - odd) * rows
    ext_rows, ext_cols, _ = ext_scr.shape
    blocks = ext_cols // TILE
    for row in range(ext_rows):
        basis_grad = dot(ext_scr[row], weight, NT).astype(bf16)
        low = row * basis_count * TILE
        for basis in range(basis_count):
            for block in range(blocks):
                piece = basis_grad[block * TILE : (block + 1) * TILE, basis * channels : (basis + 1) * channels]
                start = low + basis * TILE
                basis_scr[start : start + TILE, block * channels : (block + 1) * channels] = piece
        reached = [target + 2 * (offsets // 2) - row for target in range(2 * rows)]
        band_scr[low : low + basis_count * TILE, :] = bands(taps_ref, index_ref, first_row + row, basis_count, reached, offsets)
    sum_scr[...] = jnp.zeros(sum_scr.shape, f32)
    for block in range(0, blocks, 2):
        sides = min(2, blocks - block)
        spread = dot(band_scr[...], basis_scr[:, block * channels : (block + sides) * channels], TN)
        for target in range(2 * rows):
            for side in range(sides):
                start = (block + side) * TILE
                piece = spread[target * SLOT : (target + 1) * SLOT, side * channels : (side + 1) * channels]
                sum_scr[target, start : start + SLOT, :] = sum_scr[target, start : start + SLOT, :] + piece
    for row in range(rows):
        for ref, slot in ((own_grad_ref, odd * rows), (pair_grad_ref, (1 - odd) * rows)):
            ref[row * cols : (row + 1) * cols, :] = sum_scr[slot + row, TILE : TILE + cols, :].astype(bf16)


def finish_body(lay, own_ref, pair_ref, grad_ref):
    shape = (own_ref.shape[1], grad_ref.shape[1])
    place, column = lay.places(shape, 0), lax.broadcasted_iota(jnp.int32, shape, 1)
    odd = lay.odd()
    own = (column == lay.whole(place, odd)).astype(bf16)
    pair = (column == lay.whole(place, 1 - odd)).astype(bf16)
    grad_ref[...] = (dot(own_ref[...], own) + dot(pair_ref[...], pair)).astype(bf16)


def after(array, *others):
    return lax.optimization_barrier((array, *others))[0]


def swap(array, axis, stride):
    return lax.ppermute(array, axis, [(i, i ^ stride) for i in range(lax.axis_size(axis))])


def swap_across(array, axis, stride, wrap):
    size = lax.axis_size(axis)
    pairs = [(i, i + stride if i // stride % 2 else i - stride) for i in range(size)]
    return lax.ppermute(array, axis, [(i, j % size) for i, j in pairs if wrap or 0 <= j < size])


def flat(rows, width):
    wide = width // rows.shape[2]
    lines = [
        jnp.concatenate([rows[row + side] for side in range(wide)], axis=1) for row in range(0, rows.shape[0], wide)
    ]
    return jnp.concatenate(lines, axis=0)


def row_halo(own, pair, width, near_more):
    lat = lax.axis_index("lat")
    own_first = (lat & 1) != ((lat >> 1) & 1)
    to_near, to_far = jnp.where(own_first, own, pair), jnp.where(own_first, pair, own)
    near = swap(jnp.concatenate([flat(to_near, width), *near_more], axis=0), "lat", 2)
    return near, swap_across(flat(to_far, width), "lat", 2, False)


def edges(near, own, pair, far, rim, width):
    rows, cols, channels = own.shape
    lines = rows * channels // width

    def at(first):
        def halo(v):
            return [v[line * cols + first : line * cols + first + rim] for line in range(lines)]

        kept = [flat(v[:, first : first + rim], width) for v in (own, pair)]
        return jnp.concatenate([*halo(near), *kept, *halo(far)], axis=0)

    even = (lax.axis_index("lon") & 1) == 0
    left, right = at(0), at(cols - rim)
    return jnp.where(even, right, left), jnp.where(even, left, right)


def column_halo(lay, to_core, to_cross, cross_more):
    to_cross = jnp.concatenate([to_cross, *cross_more], axis=0)
    cross = swap(to_cross, "lon", 3) if lay.merged else swap_across(to_cross, "lon", 1, True)
    return swap(to_core, "lon", 1), cross


def local(features, weight, tap_values, basis_index, half_width, cotangent):
    channels, rows, cols = features.shape
    basis_count = weight.shape[0]
    _, offsets, window = tap_values.shape
    rim = (window - 1) // 2
    lay = Layout(channels, lax.axis_size("lat"), lax.axis_size("lon"))
    odd = lay.odd()
    half = channels // 2

    split = features.reshape(half // lay.pair, 2, lay.pair, rows, cols)
    to_pair = lax.dynamic_index_in_dim(split, 1 - odd, 1, False).reshape(half, rows, cols)
    to_keep = lax.dynamic_index_in_dim(split, odd, 1, False).reshape(half, rows, cols)
    feat_pair = jnp.transpose(swap(to_pair, "lat", 1), (1, 2, 0))
    feat_own = jnp.transpose(to_keep, (1, 2, 0))
    cot_pair = jnp.transpose(swap(cotangent, "lat", 1), (1, 2, 0))
    cot_own = jnp.transpose(cotangent, (1, 2, 0))

    far = jnp.abs(jnp.arange(window) - rim)
    index = jnp.where(far[None, None, :] <= half_width[:, None, None], basis_index, -1)
    fill = ((rows, rows), (0, offsets % 2), (0, SLOT - window))
    index = jnp.pad(index, fill, constant_values=-1)
    taps = jnp.pad(tap_values.astype(f32), fill)

    full = weight.reshape(basis_count, lay.own, channels // lay.parts)
    for axis, flip, _ in lay.split:
        other = swap(full, axis, flip)
        low = (lax.axis_index(axis) // flip) % 2 == 0
        full = jnp.where(low, jnp.concatenate([full, other], 2), jnp.concatenate([other, full], 2))
    gather = list(reversed(lay.steps))

    def widen(full, step):
        return jnp.concatenate([full, swap(full, step[0], step[1])], axis=1)

    lot = basis_count * lay.own

    def tail(array, count):
        return [array[array.shape[0] - (i + 1) * lot : array.shape[0] - i * lot] for i in reversed(range(count))]

    own, by_next = [], []
    if lay.merged:
        own = [after(weight, to_pair).reshape(lot, channels)]
        own = [lax.optimization_barrier(own[0])]
        by_next = [swap(own[0], "lat", 4)]
    near, far = row_halo(feat_own, feat_pair, channels, own)
    by_near = tail(near, len(own))
    to_core, to_cross = edges(near, feat_own, feat_pair, far, rim, channels)
    core, cross = column_halo(lay, to_core, to_cross, own + by_next + by_near)
    if not lay.merged:
        for step in gather[:-1]:
            full = widen(full, step)
    cot_near, cot_far = row_halo(after(cot_own, to_core, to_cross), cot_pair, channels, by_next)

    cells = rows * cols
    ext = (4 * rows, cols + 2 * rim)
    basis_out, send, keep = call(
        lambda *refs: forward_body(lay, offsets, *refs), "forward", 16 * basis_count * cells * half * channels,
        [((basis_count, 2 * cells, half), bf16), ((basis_count, half // 2, channels), f32),
         ((basis_count, half // 2, channels), f32)],
        feat_own, feat_pair, near, far, core, cross, taps, index, cot_own, cot_pair,
        scratch=[pltpu.VMEM((*ext, half), bf16)],
    )
    for rank, (axis, flip, _) in enumerate(lay.steps):
        terms = (keep, swap(send, axis, flip))
        if rank == 0:
            cot_near, cot_far = after(cot_near, send), after(cot_far, send)
        elif rank == 1:
            by_both = tail(cot_near, len(own))
            to_core, to_cross = edges(cot_near, cot_own, cot_pair, cot_far, rim, channels)
            to_core, to_cross = after(to_core, send), after(to_cross, send)
            cot_core, cot_cross = column_halo(lay, to_core, to_cross, by_both)
        elif rank == 2:
            cot_core, cot_cross = after(cot_core, send), after(cot_cross, send)
            cot_around = (cot_near, cot_far, cot_core, cot_cross)
            if lay.merged:
                here, there = own + by_next + by_near + by_both, tail(cross, 3) + tail(cot_cross, 1)
                held = here[:2] + there[:2] + here[2:] + there[2:]
                full = jnp.concatenate([v.reshape(basis_count, lay.own, channels) for v in held], axis=1)
            full = widen(full, gather[-1])
            own_out, pair_out = call(
                mix_body, "mix", 4 * basis_count * cells * half * channels, [((cells, channels), f32), ((cells, channels), bf16)], full, basis_out
            )
            cot_after = after(cot_own, pair_out)
            pair_out = swap(pair_out, "lat", 1)
            cot_around = (cot_near, cot_far, cot_core, cot_cross)
            own_grad, pair_grad = call(
                lambda *refs: backward_body(lay, offsets, *refs), "backward", 48 * basis_count * cells * half * channels,
                [((cells, half), bf16), ((cells, half), bf16)],
                cot_after, cot_pair, *cot_around, taps, index, full,
                scratch=[pltpu.VMEM((*ext, channels), bf16),
                         pltpu.VMEM((ext[0] * basis_count * TILE, ext[1] // TILE * half), bf16),
                         pltpu.VMEM((ext[0] * basis_count * TILE, 2 * rows * SLOT), bf16),
                         pltpu.VMEM((2 * rows, ext[1] + TILE, half), f32)],
            )
            pair_grad = swap(pair_grad, "lat", 1)
        if rank + 1 < len(lay.steps):
            size = keep.shape[1] // 2
            send = (terms[0][:, size:] + terms[1][:, size:]).astype(bf16 if rank < 2 else f32)
            keep = terms[0][:, :size] + terms[1][:, :size]
        if rank == 2:
            send = after(send, own_grad)
    grad = terms[0] + terms[1]
    for axis, flip, _ in reversed(lay.split):
        size = grad.shape[2] // 2
        odd_part = (lax.axis_index(axis) // flip) % 2
        other = swap(lax.dynamic_slice_in_dim(grad, (1 - odd_part) * size, size, 2), axis, flip)
        grad = lax.dynamic_slice_in_dim(grad, odd_part * size, size, 2) + other
    weight_grad = grad.reshape(basis_count, weight.shape[1])

    output = (own_out + pair_out).astype(bf16)
    (input_grad,) = call(
        lambda *refs: finish_body(lay, *refs), "finish", 4 * cells * half * channels, [((cells, channels), bf16)], own_grad, pair_grad
    )

    def channels_first(v):
        return jnp.transpose(v.reshape(rows, cols, channels), (2, 0, 1))

    return channels_first(output), channels_first(input_grad), weight_grad


def solution(mesh):
    field = P(None, "lat", "lon")
    flat = P(None, ("lat", "lon"))
    return jax.shard_map(
        local,
        mesh=mesh,
        in_specs=(field, flat, P(), P(), P(), field),
        out_specs=(field, field, flat),
        check_vma=False,
    )
```

time: 55.8 us -> 51.9 us (0.930)
  starting transfers between devices: 27.4 us -> 25 us
  Pallas kernels: 6.08 us -> 4.95 us
  waiting for transfers between devices: 15.3 us -> 14.7 us
    ppermute x4 -> x2, starting transfers between devices: 3.54 us -> 1.33 us  [swap_across(): lax.ppermute(array, axis, [(i, j % size) for i, j in pairs if wrap or 0 <...]
    pallas_call x4, Pallas kernels: 6.08 us -> 4.95 us  [call(): pl.pallas_call(body, name=name, out_shape=[jax.ShapeDtypeStruct(s, d) for...]
    reshape x1, local copies, waits for them, and re-layouts: 0.01 us -> 0.87 us  [local(): own = [after(weight, to_pair).reshape(lot, channels)]]
    unnamed x13 -> x25, local copies, waits for them, and re-layouts: 3.55 us -> 2.75 us
    ppermute x16, waiting for transfers between devices: 15.3 us -> 14.7 us  [swap(): lax.ppermute(array, axis, [(i, i ^ stride) for i in range(lax.axis_size(a...]
  transfers between devices with their start and end apart: 20 -> 18, of which waited for: 6 -> 8; matrix products, arithmetic and copies ran while one was open for 7% -> 8% of each run, Pallas kernels for 11% -> 4%
where the time goes in v3:
time: 51.9 us; the launch traced here: 51.7 us
  starting transfers between devices  25 us (48%)
  waiting for transfers between devices  14.7 us (28%)
  local copies, waits for them, and re-layouts  5.53 us (11%)
  Pallas kernels  4.95 us (10%)
  between operations  1.09 us (2%)
    ppermute x16, starting transfers between devices, swap(): lax.ppermute(array, axis, [(i, i ^ stride) for i in range(lax.axis_size(a...  23.7 us
    ppermute x16, waiting for transfers between devices, swap(): lax.ppermute(array, axis, [(i, i ^ stride) for i in range(lax.axis_size(a...  14.7 us
    pallas_call x4, Pallas kernels, call(): pl.pallas_call(body, name=name, out_shape=[jax.ShapeDtypeStruct(s, d) for...  4.95 us
    unnamed x25, local copies, waits for them, and re-layouts  2.75 us
    reshape x2, local copies, waits for them, and re-layouts, channels_first(): return jnp.transpose(v.reshape(rows, cols, channels), (2, 0, 1))  1.56 us
    ppermute x2, starting transfers between devices, swap_across(): lax.ppermute(array, axis, [(i, j % size) for i, j in pairs if wrap or 0 <...  1.33 us
  transfers between devices with their start and end apart: 18, of which 8 were waited for; matrix products, arithmetic and copies ran while one was open for 8% of the time, Pallas kernels for 4%

profile of v3, /device:TPU:0, one launch (start us, length us, event | category | flops | bytes accessed | tf_op | source)
XLA Modules:
  0.0 51.7 jit_solution(8894277085195103743)
XLA Ops:
  0.7 0.9 %copy.25 = bf16[256,2,128]{2,0,1:T(8,128)(2,1)S(1)} copy(bf16[256,2,128]{2,1,0:T(2,128)(2,1)} %param.6) | data formatting | bytes 262144 | tf_op args[0]
  1.8 3.0 %collective-permute-start.1 = (bf16[128,2,128]{0,2,1:T(8,128)(2,1)S(1)}, bf16[128,2,128]{0,2,1:T(8,128)(2,1)S(1)}, u32[]{:S(2)}, u32[]{:S(2)}) collective-permute-start(bf16[128,2,128]{0,2,1:T(8,128)(2,1)S(1)} %copy.27), channel_id=1, source_target_pairs={{0,4},{4,0},{8,12},{12,8},{16,20},{20,16},{24,28},{28,24},{1,5},{5... | collective-permute-start | bytes 196616 | tf_op jit(solution)/shard_map/ppermute | solution.py:214
  4.8 0.9 %reshape.89 = bf16[72,256]{1,0:T(8,128)(2,1)S(1)} reshape(bf16[9,2048]{1,0:T(8,128)(2,1)} %param.7) | data formatting | bytes 73728 | tf_op jit(solution)/shard_map/reshape | solution.py:301
  5.7 2.7 %collective-permute-start = (bf16[72,256]{1,0:T(8,128)(2,1)S(1)}, bf16[72,256]{1,0:T(8,128)(2,1)S(1)}, u32[]{:S(2)}, u32[]{:S(2)}) collective-permute-start(bf16[72,256]{1,0:T(8,128)(2,1)S(1)} %reshape.89), channel_id=1, source_target_pairs={{0,16},{4,20},{8,24},{12,28},{16,0},{20,4},{24,8},{28,12},{1,17},{... | collective-permute-start | bytes 110600 | tf_op jit(solution)/shard_map/ppermute | solution.py:214
  8.3 1.0 %copy.28 = bf16[256,2,128]{0,2,1:T(8,128)(2,1)S(1)} copy(bf16[256,2,128]{2,1,0:T(2,128)(2,1)} %param.11) | data formatting | bytes 262144 | tf_op args[5]
  11.4 4.5 %collective-permute-start.2 = (bf16[200,256]{1,0:T(8,128)(2,1)S(1)}, bf16[200,256]{1,0:T(8,128)(2,1)S(1)}, u32[]{:S(2)}, u32[]{:S(2)}) collective-permute-start(bf16[200,256]{1,0:T(8,128)(2,1)S(1)} %pad_maximum_fusion.3), channel_id=1, source_target_pairs={{0,8},{4,12},{8,0},{12,4},{16,24},{20,28},{24,16},{28,20},{1,9},{5... | collective-permute-start | bytes 307208 | tf_op jit(solution)/shard_map/ppermute | solution.py:214
  15.9 2.6 %collective-permute-done.2.refs_2_ = bf16[200,256]{1,0:T(8,128)(2,1)S(1)} collective-permute-done((bf16[200,256]{1,0:T(8,128)(2,1)S(1)}, bf16[200,256]{1,0:T(8,128)(2,1)S(1)}, u32[]{:S(2)}, u32[]{:S(2)}) %collective-permute-start.2) | collective-permute-done | bytes 102432 | tf_op jit(solution)/shard_map/ppermute | solution.py:214
  18.6 1.6 %collective-permute-start.4 = (bf16[280,256]{1,0:T(8,128)(2,1)S(1)}, bf16[280,256]{1,0:T(8,128)(2,1)S(1)}, u32[]{:S(2)}, u32[]{:S(2)}) collective-permute-start(bf16[280,256]{1,0:T(8,128)(2,1)S(1)} %pad_maximum_fusion.1), channel_id=1, source_target_pairs={{0,3},{1,2},{2,1},{3,0},{4,7},{5,6},{6,5},{7,4},{8,11},{9,10},{10,... | collective-permute-start | bytes 430088 | tf_op jit(solution)/shard_map/ppermute | solution.py:214
  20.3 0.7 %collective-permute-start.8 = (bf16[256,256]{1,0:T(8,128)(2,1)S(1)}, bf16[256,256]{1,0:T(8,128)(2,1)S(1)}, u32[]{:S(2)}, u32[]{:S(2)}) collective-permute-start(bf16[256,256]{1,0:T(8,128)(2,1)S(1)} %pad_maximum_fusion.2), channel_id=1, source_target_pairs={{8,16},{12,20},{16,8},{20,12},{9,17},{13,21},{17,9},{21,13},{10,18... | collective-permute-start | bytes 393224 | tf_op jit(solution)/shard_map/ppermute | solution.py:220
  21.1 3.7 %collective-permute-start.6 = (bf16[328,256]{1,0:T(8,128)(2,1)S(1)}, bf16[328,256]{1,0:T(8,128)(2,1)S(1)}, u32[]{:S(2)}, u32[]{:S(2)}) collective-permute-start(bf16[328,256]{1,0:T(8,128)(2,1)S(1)} %pad_maximum_fusion), channel_id=1, source_target_pairs={{0,8},{4,12},{8,0},{12,4},{16,24},{20,28},{24,16},{28,20},{1,9},{5... | collective-permute-start | bytes 503816 | tf_op jit(solution)/shard_map/ppermute | solution.py:214
  24.8 1.6 %forward.1 = (bf16[9,512,128]{2,1,0:T(8,128)(2,1)S(1)}, f32[9,64,256]{2,1,0:T(8,128)S(1)}, f32[9,64,256]{2,1,0:T(8,128)S(1)}) custom-call(bf16[2,128,128]{2,1,0:T(8,128)(2,1)S(1)} %bitcast.124, bf16[2,128,128]{2,1,0:T(8,128)(2,1)S(1)} %bitcast.130, bf16[200,256]{1,0:T(8,128)(2,1)S(1)} %collective-permute-done.2.refs_2_, ...), custom_call_target="tpu_custom_call" | custom-call | flops 1207959552 | bytes 798720 | tf_op jit(solution)/shard_map/forward/pallas_call | solution.py:22
  26.5 2.5 %collective-permute-done.6.refs_2_ = bf16[328,256]{1,0:T(8,128)(2,1)S(1)} collective-permute-done((bf16[328,256]{1,0:T(8,128)(2,1)S(1)}, bf16[328,256]{1,0:T(8,128)(2,1)S(1)}, u32[]{:S(2)}, u32[]{:S(2)}) %collective-permute-start.6) | collective-permute-done | bytes 167968 | tf_op jit(solution)/shard_map/ppermute | solution.py:214
  29.2 1.8 %collective-permute-start.11 = (bf16[9,32,256]{2,1,0:T(8,128)(2,1)S(1)}, bf16[9,32,256]{2,1,0:T(8,128)(2,1)S(1)}, u32[]{:S(2)}, u32[]{:S(2)}) collective-permute-start(bf16[9,32,256]{2,1,0:T(8,128)(2,1)S(1)} %get-tuple-element.38), channel_id=1, source_target_pairs={{0,8},{4,12},{8,0},{12,4},{16,24},{20,28},{24,16},{28,20},{1,9},{5... | collective-permute-start | bytes 442376 | tf_op jit(solution)/shard_map/ppermute | solution.py:214
  31.3 3.2 %collective-permute-done.11 = bf16[9,32,256]{2,1,0:T(8,128)(2,1)S(1)} collective-permute-done((bf16[9,32,256]{2,1,0:T(8,128)(2,1)S(1)}, bf16[9,32,256]{2,1,0:T(8,128)(2,1)S(1)}, u32[]{:S(2)}, u32[]{:S(2)}) %collective-permute-start.11) | collective-permute-done | bytes 147488 | tf_op jit(solution)/shard_map/ppermute | solution.py:214
  36.3 1.2 %collective-permute-done.14.refs_4_ = bf16[128,256]{1,0:T(8,128)(2,1)S(1)} collective-permute-done((bf16[128,256]{1,0:T(8,128)(2,1)S(1)}, bf16[128,256]{1,0:T(8,128)(2,1)S(1)}, u32[]{:S(2)}, u32[]{:S(2)}) %collective-permute-start.14) | collective-permute-done | bytes 65568 | tf_op jit(solution)/shard_map/ppermute | solution.py:214
  37.5 1.6 %collective-permute-done.16 = bf16[9,16,256]{2,1,0:T(8,128)(2,1)S(1)} collective-permute-done((bf16[9,16,256]{2,1,0:T(8,128)(2,1)S(1)}, bf16[9,16,256]{2,1,0:T(8,128)(2,1)S(1)}, u32[]{:S(2)}, u32[]{:S(2)}) %collective-permute-start.16) | collective-permute-done | bytes 73760 | tf_op jit(solution)/shard_map/ppermute | solution.py:214
  39.7 2.6 %backward.1 = (bf16[256,128]{1,0:T(8,128)(2,1)S(1)}, bf16[256,128]{1,0:T(8,128)(2,1)S(1)}) custom-call(bf16[2,128,256]{2,1,0:T(8,128)(2,1)S(1)} %bitcast.121, bf16[2,128,256]{2,1,0:T(8,128)(2,1)S(1)} %bitcast.128, bf16[328,256]{1,0:T(8,128)(2,1)S(1)} %collective-permute-done.6.refs_2_, bf16[256,256]{1,0:T(8,128)(2,1)S(1)} %collective-permute-done.8.refs_3_, ...), custom_call_target="tpu_custom_call" | custom-call | flops 3623878656 | bytes 1380352 | tf_op jit(solution)/shard_map/backward/pallas_call | solution.py:22
  42.3 2.0 %collective-permute-start.17 = (f32[9,8,256]{2,1,0:T(8,128)S(1)}, f32[9,8,256]{2,1,0:T(8,128)S(1)}, u32[]{:S(2)}, u32[]{:S(2)}) collective-permute-start(f32[9,8,256]{2,1,0:T(8,128)S(1)} %slice_add_fusion.4), channel_id=1, source_target_pairs={{0,16},{4,20},{8,24},{12,28},{16,0},{20,4},{24,8},{28,12},{1,17},{... | collective-permute-start | bytes 221192 | tf_op jit(solution)/shard_map/ppermute | solution.py:214
  44.3 0.8 %collective-permute-start.15 = (bf16[256,128]{1,0:T(8,128)(2,1)S(1)}, bf16[256,128]{1,0:T(8,128)(2,1)S(1)}, u32[]{:S(2)}, u32[]{:S(2)}) collective-permute-start(bf16[256,128]{1,0:T(8,128)(2,1)S(1)} %get-tuple-element.35), channel_id=1, source_target_pairs={{0,4},{4,0},{8,12},{12,8},{16,20},{20,16},{24,28},{28,24},{1,5},{5... | collective-permute-start | bytes 196616 | tf_op jit(solution)/shard_map/ppermute | solution.py:214
  45.2 1.2 %collective-permute-start.13 = (bf16[256,256]{1,0:T(8,128)(2,1)S(1)}, bf16[256,256]{1,0:T(8,128)(2,1)S(1)}, u32[]{:S(2)}, u32[]{:S(2)}) collective-permute-start(bf16[256,256]{1,0:T(8,128)(2,1)S(1)} %get-tuple-element.30), channel_id=1, source_target_pairs={{0,4},{4,0},{8,12},{12,8},{16,20},{20,16},{24,28},{28,24},{1,5},{5... | collective-permute-start | bytes 393224 | tf_op jit(solution)/shard_map/ppermute | solution.py:214
  46.4 2.7 %collective-permute-done.15.refs_1_ = bf16[256,128]{1,0:T(8,128)(2,1)S(1)} collective-permute-done((bf16[256,128]{1,0:T(8,128)(2,1)S(1)}, bf16[256,128]{1,0:T(8,128)(2,1)S(1)}, u32[]{:S(2)}, u32[]{:S(2)}) %collective-permute-start.15) | collective-permute-done | bytes 65568 | tf_op jit(solution)/shard_map/ppermute | solution.py:214
  49.3 0.8 %copy.33 = bf16[2,128,256]{1,0,2:T(2,128)(2,1)} copy(bf16[2,128,256]{2,1,0:T(8,128)(2,1)S(1)} %bitcast.122) | data formatting | bytes 262144 | tf_op jit(solution)/shard_map/reshape | solution.py:375
  50.2 0.7 %copy.34 = f32[2,8,8,256]{3,1,2,0:T(8,128)} copy(f32[2,8,8,256]{3,2,1,0:T(8,128)S(1)} %bitcast.132) | data formatting | bytes 262144
  50.9 0.8 %copy.32 = bf16[2,128,256]{1,0,2:T(2,128)(2,1)} copy(bf16[2,128,256]{2,1,0:T(8,128)(2,1)S(1)} %bitcast.133) | data formatting | bytes 262144 | tf_op jit(solution)/shard_map/reshape | solution.py:375
  (80 shorter events, 5.4 us)
Async XLA Ops:
  0.6 9.4 %copy-start.1 = (bf16[16,5,33]{2,0,1:T(8,128)(2,1)S(1)}, bf16[16,5,33]{2,0,1:T(8,128)(2,1)}, u32[]{:S(2)}) copy-start(bf16[16,5,33]{2,0,1:T(8,128)(2,1)} %param.8) | copy-start | bytes 15844
  0.6 9.5 %copy-start.2 = (s32[16]{0:T(128)S(1)}, s32[16]{0:T(128)}, u32[]{:S(2)}) copy-start(s32[16]{0:T(128)} %param.10) | copy-start | bytes 196
  0.7 9.5 %copy-start = (s32[16,5,33]{2,0,1:T(8,128)S(1)}, s32[16,5,33]{2,0,1:T(8,128)}, u32[]{:S(2)}) copy-start(s32[16,5,33]{2,0,1:T(8,128)} %param.9) | copy-start | bytes 31684
  1.8 8.8 %collective-permute-start.1 = (bf16[128,2,128]{0,2,1:T(8,128)(2,1)S(1)}, bf16[128,2,128]{0,2,1:T(8,128)(2,1)S(1)}, u32[]{:S(2)}, u32[]{:S(2)}) collective-permute-start(bf16[128,2,128]{0,2,1:T(8,128)(2,1)S(1)} %copy.27), channel_id=1, source_target_pairs={{0,4},{4,0},{8,12},{12,8},{16,20},{20,16},{24,28},{28,24},{1,5},{5... | collective-permute-start | bytes 196616 | tf_op jit(solution)/shard_map/ppermute | solution.py:214
  5.7 4.9 %collective-permute-start = (bf16[72,256]{1,0:T(8,128)(2,1)S(1)}, bf16[72,256]{1,0:T(8,128)(2,1)S(1)}, u32[]{:S(2)}, u32[]{:S(2)}) collective-permute-start(bf16[72,256]{1,0:T(8,128)(2,1)S(1)} %reshape.89), channel_id=1, source_target_pairs={{0,16},{4,20},{8,24},{12,28},{16,0},{20,4},{24,8},{28,12},{1,17},{... | collective-permute-start | bytes 110600 | tf_op jit(solution)/shard_map/ppermute | solution.py:214
  9.3 10.9 %collective-permute-start.5 = (bf16[256,2,128]{0,2,1:T(8,128)(2,1)S(1)}, bf16[256,2,128]{0,2,1:T(8,128)(2,1)S(1)}, u32[]{:S(2)}, u32[]{:S(2)}) collective-permute-start(bf16[256,2,128]{0,2,1:T(8,128)(2,1)S(1)} %copy.28), channel_id=1, source_target_pairs={{0,4},{4,0},{8,12},{12,8},{16,20},{20,16},{24,28},{28,24},{1,5},{5... | collective-permute-start | bytes 393224 | tf_op jit(solution)/shard_map/ppermute | solution.py:214
  10.7 5.2 %collective-permute-start.3 = (bf16[128,256]{1,0:T(8,128)(2,1)S(1)}, bf16[128,256]{1,0:T(8,128)(2,1)S(1)}, u32[]{:S(2)}, u32[]{:S(2)}) collective-permute-start(bf16[128,256]{1,0:T(8,128)(2,1)S(1)} %pad_maximum_fusion.5), channel_id=1, source_target_pairs={{8,16},{12,20},{16,8},{20,12},{9,17},{13,21},{17,9},{21,13},{10,18... | collective-permute-start | bytes 196616 | tf_op jit(solution)/shard_map/ppermute | solution.py:220
  11.4 7.1 %collective-permute-start.2 = (bf16[200,256]{1,0:T(8,128)(2,1)S(1)}, bf16[200,256]{1,0:T(8,128)(2,1)S(1)}, u32[]{:S(2)}, u32[]{:S(2)}) collective-permute-start(bf16[200,256]{1,0:T(8,128)(2,1)S(1)} %pad_maximum_fusion.3), channel_id=1, source_target_pairs={{0,8},{4,12},{8,0},{12,4},{16,24},{20,28},{24,16},{28,20},{1,9},{5... | collective-permute-start | bytes 307208 | tf_op jit(solution)/shard_map/ppermute | solution.py:214
  18.5 6.3 %collective-permute-start.7 = (bf16[64,256]{1,0:T(8,128)(2,1)S(1)}, bf16[64,256]{1,0:T(8,128)(2,1)S(1)}, u32[]{:S(2)}, u32[]{:S(2)}) collective-permute-start(bf16[64,256]{1,0:T(8,128)(2,1)S(1)} %broadcast_select_fusion.6), channel_id=1, source_target_pairs={{0,1},{1,0},{2,3},{3,2},{4,5},{5,4},{6,7},{7,6},{8,9},{9,8},{10,11... | collective-permute-start | bytes 98312 | tf_op jit(solution)/shard_map/ppermute | solution.py:214
  18.6 6.2 %collective-permute-start.4 = (bf16[280,256]{1,0:T(8,128)(2,1)S(1)}, bf16[280,256]{1,0:T(8,128)(2,1)S(1)}, u32[]{:S(2)}, u32[]{:S(2)}) collective-permute-start(bf16[280,256]{1,0:T(8,128)(2,1)S(1)} %pad_maximum_fusion.1), channel_id=1, source_target_pairs={{0,3},{1,2},{2,1},{3,0},{4,7},{5,6},{6,5},{7,4},{8,11},{9,10},{10,... | collective-permute-start | bytes 430088 | tf_op jit(solution)/shard_map/ppermute | solution.py:214
  20.3 6.1 %collective-permute-start.8 = (bf16[256,256]{1,0:T(8,128)(2,1)S(1)}, bf16[256,256]{1,0:T(8,128)(2,1)S(1)}, u32[]{:S(2)}, u32[]{:S(2)}) collective-permute-start(bf16[256,256]{1,0:T(8,128)(2,1)S(1)} %pad_maximum_fusion.2), channel_id=1, source_target_pairs={{8,16},{12,20},{16,8},{20,12},{9,17},{13,21},{17,9},{21,13},{10,18... | collective-permute-start | bytes 393224 | tf_op jit(solution)/shard_map/ppermute | solution.py:220
  21.1 7.9 %collective-permute-start.6 = (bf16[328,256]{1,0:T(8,128)(2,1)S(1)}, bf16[328,256]{1,0:T(8,128)(2,1)S(1)}, u32[]{:S(2)}, u32[]{:S(2)}) collective-permute-start(bf16[328,256]{1,0:T(8,128)(2,1)S(1)} %pad_maximum_fusion), channel_id=1, source_target_pairs={{0,8},{4,12},{8,0},{12,4},{16,24},{20,28},{24,16},{28,20},{1,9},{5... | collective-permute-start | bytes 503816 | tf_op jit(solution)/shard_map/ppermute | solution.py:214
  26.4 2.7 %collective-permute-start.9 = (f32[9,64,256]{2,1,0:T(8,128)S(1)}, f32[9,64,256]{2,1,0:T(8,128)S(1)}, u32[]{:S(2)}, u32[]{:S(2)}) collective-permute-start(f32[9,64,256]{2,1,0:T(8,128)S(1)} %get-tuple-element.22), channel_id=1, source_target_pairs={{0,1},{1,0},{2,3},{3,2},{4,5},{5,4},{6,7},{7,6},{8,9},{9,8},{10,11... | collective-permute-start | bytes 1769480 | tf_op jit(solution)/shard_map/ppermute | solution.py:214
  29.2 5.3 %collective-permute-start.11 = (bf16[9,32,256]{2,1,0:T(8,128)(2,1)S(1)}, bf16[9,32,256]{2,1,0:T(8,128)(2,1)S(1)}, u32[]{:S(2)}, u32[]{:S(2)}) collective-permute-start(bf16[9,32,256]{2,1,0:T(8,128)(2,1)S(1)} %get-tuple-element.38), channel_id=1, source_target_pairs={{0,8},{4,12},{8,0},{12,4},{16,24},{20,28},{24,16},{28,20},{1,9},{5... | collective-permute-start | bytes 442376 | tf_op jit(solution)/shard_map/ppermute | solution.py:214
  31.1 4.5 %collective-permute-start.10 = (bf16[200,256]{1,0:T(8,128)(2,1)S(1)}, bf16[200,256]{1,0:T(8,128)(2,1)S(1)}, u32[]{:S(2)}, u32[]{:S(2)}) collective-permute-start(bf16[200,256]{1,0:T(8,128)(2,1)S(1)} %pad_maximum_fusion.4), channel_id=1, source_target_pairs={{0,3},{1,2},{2,1},{3,0},{4,7},{5,6},{6,5},{7,4},{8,11},{9,10},{10,... | collective-permute-start | bytes 307208 | tf_op jit(solution)/shard_map/ppermute | solution.py:214
  34.5 4.6 %collective-permute-start.16 = (bf16[9,16,256]{2,1,0:T(8,128)(2,1)S(1)}, bf16[9,16,256]{2,1,0:T(8,128)(2,1)S(1)}, u32[]{:S(2)}, u32[]{:S(2)}) collective-permute-start(bf16[9,16,256]{2,1,0:T(8,128)(2,1)S(1)} %get-tuple-element.40), channel_id=1, source_target_pairs={{0,3},{1,2},{2,1},{3,0},{4,7},{5,6},{6,5},{7,4},{8,11},{9,10},{10,... | collective-permute-start | bytes 221192 | tf_op jit(solution)/shard_map/ppermute | solution.py:214
  35.6 3.6 %collective-permute-start.12 = (bf16[9,64,256]{2,1,0:T(8,128)(2,1)S(1)}, bf16[9,64,256]{2,1,0:T(8,128)(2,1)S(1)}, u32[]{:S(2)}, u32[]{:S(2)}) collective-permute-start(bf16[9,64,256]{2,1,0:T(8,128)(2,1)S(1)} %get-tuple-element.77), channel_id=1, source_target_pairs={{0,1},{1,0},{2,3},{3,2},{4,5},{5,4},{6,7},{7,6},{8,9},{9,8},{10,11... | collective-permute-start | bytes 884744 | tf_op jit(solution)/shard_map/ppermute | solution.py:214
  36.2 1.3 %collective-permute-start.14 = (bf16[128,256]{1,0:T(8,128)(2,1)S(1)}, bf16[128,256]{1,0:T(8,128)(2,1)S(1)}, u32[]{:S(2)}, u32[]{:S(2)}) collective-permute-start(bf16[128,256]{1,0:T(8,128)(2,1)S(1)} %get-tuple-element.32), channel_id=1, source_target_pairs={{0,1},{1,0},{2,3},{3,2},{4,5},{5,4},{6,7},{7,6},{8,9},{9,8},{10,11... | collective-permute-start | bytes 196616 | tf_op jit(solution)/shard_map/ppermute | solution.py:214
  42.3 7.8 %collective-permute-start.17 = (f32[9,8,256]{2,1,0:T(8,128)S(1)}, f32[9,8,256]{2,1,0:T(8,128)S(1)}, u32[]{:S(2)}, u32[]{:S(2)}) collective-permute-start(f32[9,8,256]{2,1,0:T(8,128)S(1)} %slice_add_fusion.4), channel_id=1, source_target_pairs={{0,16},{4,20},{8,24},{12,28},{16,0},{20,4},{24,8},{28,12},{1,17},{... | collective-permute-start | bytes 221192 | tf_op jit(solution)/shard_map/ppermute | solution.py:214
  44.3 4.7 %collective-permute-start.15 = (bf16[256,128]{1,0:T(8,128)(2,1)S(1)}, bf16[256,128]{1,0:T(8,128)(2,1)S(1)}, u32[]{:S(2)}, u32[]{:S(2)}) collective-permute-start(bf16[256,128]{1,0:T(8,128)(2,1)S(1)} %get-tuple-element.35), channel_id=1, source_target_pairs={{0,4},{4,0},{8,12},{12,8},{16,20},{20,16},{24,28},{28,24},{1,5},{5... | collective-permute-start | bytes 196616 | tf_op jit(solution)/shard_map/ppermute | solution.py:214
  45.2 5.7 %collective-permute-start.13 = (bf16[256,256]{1,0:T(8,128)(2,1)S(1)}, bf16[256,256]{1,0:T(8,128)(2,1)S(1)}, u32[]{:S(2)}, u32[]{:S(2)}) collective-permute-start(bf16[256,256]{1,0:T(8,128)(2,1)S(1)} %get-tuple-element.30), channel_id=1, source_target_pairs={{0,4},{4,0},{8,12},{12,8},{16,20},{20,16},{24,28},{28,24},{1,5},{5... | collective-permute-start | bytes 393224 | tf_op jit(solution)/shard_map/ppermute | solution.py:214

commit v4 on v3

--- a/solution.py
+++ b/solution.py
@@ -304,10 +304,11 @@
     near, far = row_halo(feat_own, feat_pair, channels, own)
     by_near = tail(near, len(own))
     to_core, to_cross = edges(near, feat_own, feat_pair, far, rim, channels)
-    core, cross = column_halo(lay, to_core, to_cross, own + by_next + by_near)
+    core, cross = column_halo(lay, to_core, to_cross, own + by_near)
     if not lay.merged:
         for step in gather[:-1]:
             full = widen(full, step)
+    by_next = [after(v, to_core, to_cross) for v in by_next]
     cot_near, cot_far = row_halo(after(cot_own, to_core, to_cross), cot_pair, channels, by_next)
 
     cells = rows * cols
@@ -327,13 +328,13 @@
             by_both = tail(cot_near, len(own))
             to_core, to_cross = edges(cot_near, cot_own, cot_pair, cot_far, rim, channels)
             to_core, to_cross = after(to_core, send), after(to_cross, send)
-            cot_core, cot_cross = column_halo(lay, to_core, to_cross, by_both)
+            cot_core, cot_cross = column_halo(lay, to_core, to_cross, by_next + by_both)
         elif rank == 2:
             cot_core, cot_cross = after(cot_core, send), after(cot_cross, send)
             cot_around = (cot_near, cot_far, cot_core, cot_cross)
             if lay.merged:
-                here, there = own + by_next + by_near + by_both, tail(cross, 3) + tail(cot_cross, 1)
-                held = here[:2] + there[:2] + here[2:] + there[2:]
+                crossed, crossed_last = tail(cross, 2), tail(cot_cross, 2)
+                held = own + by_next + crossed[:1] + crossed_last[:1] + by_near + by_both + crossed[1:] + crossed_last[1:]
                 full = jnp.concatenate([v.reshape(basis_count, lay.own, channels) for v in held], axis=1)
             full = widen(full, gather[-1])
             own_out, pair_out = call(
@@ -356,8 +357,6 @@
             size = keep.shape[1] // 2
             send = (terms[0][:, size:] + terms[1][:, size:]).astype(bf16 if rank < 2 else f32)
             keep = terms[0][:, :size] + terms[1][:, :size]
-        if rank == 2:
-            send = after(send, own_grad)
     grad = terms[0] + terms[1]
     for axis, flip, _ in reversed(lay.split):
         size = grad.shape[2] // 2

time: 51.9 us -> 50.4 us (0.971)
  starting transfers between devices: 25 us -> 23.7 us
    ppermute x16, starting transfers between devices: 23.7 us -> 22.4 us  [swap(): lax.ppermute(array, axis, [(i, i ^ stride) for i in range(lax.axis_size(a...]
  transfers between devices with their start and end apart: 18 -> 18, of which waited for: 8 -> 7; matrix products, arithmetic and copies ran while one was open for 8% -> 8% of each run, Pallas kernels for 4% -> 10%
where the time goes in v4:
time: 50.4 us; the launch traced here: 50.2 us
  starting transfers between devices  23.7 us (47%)
  waiting for transfers between devices  14.4 us (29%)
  local copies, waits for them, and re-layouts  5.53 us (11%)
  Pallas kernels  4.96 us (10%)
  between operations  1.15 us (2%)
    ppermute x16, starting transfers between devices, swap(): lax.ppermute(array, axis, [(i, i ^ stride) for i in range(lax.axis_size(a...  22.4 us
    ppermute x16, waiting for transfers between devices, swap(): lax.ppermute(array, axis, [(i, i ^ stride) for i in range(lax.axis_size(a...  14.4 us
    pallas_call x4, Pallas kernels, call(): pl.pallas_call(body, name=name, out_shape=[jax.ShapeDtypeStruct(s, d) for...  4.96 us
    unnamed x25, local copies, waits for them, and re-layouts  2.75 us
    reshape x2, local copies, waits for them, and re-layouts, channels_first(): return jnp.transpose(v.reshape(rows, cols, channels), (2, 0, 1))  1.56 us
    ppermute x2, starting transfers between devices, swap_across(): lax.ppermute(array, axis, [(i, j % size) for i, j in pairs if wrap or 0 <...  1.33 us
  transfers between devices with their start and end apart: 18, of which 7 were waited for; matrix products, arithmetic and copies ran while one was open for 8% of the time, Pallas kernels for 10%

profile of v4, /device:TPU:0, one launch (start us, length us, event | category | flops | bytes accessed | tf_op | source)
XLA Modules:
  0.0 50.2 jit_solution(16072510820120634929)
XLA Ops:
  0.7 0.9 %copy.25 = bf16[256,2,128]{2,0,1:T(8,128)(2,1)S(1)} copy(bf16[256,2,128]{2,1,0:T(2,128)(2,1)} %param.6) | data formatting | bytes 262144 | tf_op args[0]
  1.8 3.0 %collective-permute-start.1 = (bf16[128,2,128]{0,2,1:T(8,128)(2,1)S(1)}, bf16[128,2,128]{0,2,1:T(8,128)(2,1)S(1)}, u32[]{:S(2)}, u32[]{:S(2)}) collective-permute-start(bf16[128,2,128]{0,2,1:T(8,128)(2,1)S(1)} %copy.27), channel_id=1, source_target_pairs={{0,4},{4,0},{8,12},{12,8},{16,20},{20,16},{24,28},{28,24},{1,5},{5... | collective-permute-start | bytes 196616 | tf_op jit(solution)/shard_map/ppermute | solution.py:214
  4.8 1.0 %copy.28 = bf16[256,2,128]{0,2,1:T(8,128)(2,1)S(1)} copy(bf16[256,2,128]{2,1,0:T(2,128)(2,1)} %param.11) | data formatting | bytes 262144 | tf_op args[5]
  5.9 0.9 %reshape.89 = bf16[72,256]{1,0:T(8,128)(2,1)S(1)} reshape(bf16[9,2048]{1,0:T(8,128)(2,1)} %param.7) | data formatting | bytes 73728 | tf_op jit(solution)/shard_map/reshape | solution.py:301
  6.8 3.1 %collective-permute-start = (bf16[72,256]{1,0:T(8,128)(2,1)S(1)}, bf16[72,256]{1,0:T(8,128)(2,1)S(1)}, u32[]{:S(2)}, u32[]{:S(2)}) collective-permute-start(bf16[72,256]{1,0:T(8,128)(2,1)S(1)} %reshape.89), channel_id=1, source_target_pairs={{0,16},{4,20},{8,24},{12,28},{16,0},{20,4},{24,8},{28,12},{1,17},{... | collective-permute-start | bytes 110600 | tf_op jit(solution)/shard_map/ppermute | solution.py:214
  10.3 1.6 %collective-permute-start.2 = (bf16[200,256]{1,0:T(8,128)(2,1)S(1)}, bf16[200,256]{1,0:T(8,128)(2,1)S(1)}, u32[]{:S(2)}, u32[]{:S(2)}) collective-permute-start(bf16[200,256]{1,0:T(8,128)(2,1)S(1)} %pad_maximum_fusion.4), channel_id=1, source_target_pairs={{0,8},{4,12},{8,0},{12,4},{16,24},{20,28},{24,16},{28,20},{1,9},{5... | collective-permute-start | bytes 307208 | tf_op jit(solution)/shard_map/ppermute | solution.py:214
  12.0 0.7 %collective-permute-start.3 = (bf16[128,256]{1,0:T(8,128)(2,1)S(1)}, bf16[128,256]{1,0:T(8,128)(2,1)S(1)}, u32[]{:S(2)}, u32[]{:S(2)}) collective-permute-start(bf16[128,256]{1,0:T(8,128)(2,1)S(1)} %pad_maximum_fusion.5), channel_id=1, source_target_pairs={{8,16},{12,20},{16,8},{20,12},{9,17},{13,21},{17,9},{21,13},{10,18... | collective-permute-start | bytes 196616 | tf_op jit(solution)/shard_map/ppermute | solution.py:220
  12.7 2.4 %collective-permute-done.2.refs_2_ = bf16[200,256]{1,0:T(8,128)(2,1)S(1)} collective-permute-done((bf16[200,256]{1,0:T(8,128)(2,1)S(1)}, bf16[200,256]{1,0:T(8,128)(2,1)S(1)}, u32[]{:S(2)}, u32[]{:S(2)}) %collective-permute-start.2) | collective-permute-done | bytes 102432 | tf_op jit(solution)/shard_map/ppermute | solution.py:214
  15.2 1.6 %collective-permute-start.7 = (bf16[64,256]{1,0:T(8,128)(2,1)S(1)}, bf16[64,256]{1,0:T(8,128)(2,1)S(1)}, u32[]{:S(2)}, u32[]{:S(2)}) collective-permute-start(bf16[64,256]{1,0:T(8,128)(2,1)S(1)} %broadcast_select_fusion.7), channel_id=1, source_target_pairs={{0,1},{1,0},{2,3},{3,2},{4,5},{5,4},{6,7},{7,6},{8,9},{9,8},{10,11... | collective-permute-start | bytes 98312 | tf_op jit(solution)/shard_map/ppermute | solution.py:214
  16.9 0.7 %collective-permute-start.8 = (bf16[256,256]{1,0:T(8,128)(2,1)S(1)}, bf16[256,256]{1,0:T(8,128)(2,1)S(1)}, u32[]{:S(2)}, u32[]{:S(2)}) collective-permute-start(bf16[256,256]{1,0:T(8,128)(2,1)S(1)} %pad_maximum_fusion.2), channel_id=1, source_target_pairs={{8,16},{12,20},{16,8},{20,12},{9,17},{13,21},{17,9},{21,13},{10,18... | collective-permute-start | bytes 393224 | tf_op jit(solution)/shard_map/ppermute | solution.py:220
  17.7 5.3 %collective-permute-start.6 = (bf16[328,256]{1,0:T(8,128)(2,1)S(1)}, bf16[328,256]{1,0:T(8,128)(2,1)S(1)}, u32[]{:S(2)}, u32[]{:S(2)}) collective-permute-start(bf16[328,256]{1,0:T(8,128)(2,1)S(1)} %pad_maximum_fusion), channel_id=1, source_target_pairs={{0,8},{4,12},{8,0},{12,4},{16,24},{20,28},{24,16},{28,20},{1,9},{5... | collective-permute-start | bytes 503816 | tf_op jit(solution)/shard_map/ppermute | solution.py:214
  23.0 1.6 %forward.1 = (bf16[9,512,128]{2,1,0:T(8,128)(2,1)S(1)}, f32[9,64,256]{2,1,0:T(8,128)S(1)}, f32[9,64,256]{2,1,0:T(8,128)S(1)}) custom-call(bf16[2,128,128]{2,1,0:T(8,128)(2,1)S(1)} %bitcast.121, bf16[2,128,128]{2,1,0:T(8,128)(2,1)S(1)} %bitcast.127, bf16[200,256]{1,0:T(8,128)(2,1)S(1)} %collective-permute-done.2.refs_2_, ...), custom_call_target="tpu_custom_call" | custom-call | flops 1207959552 | bytes 761856 | tf_op jit(solution)/shard_map/forward/pallas_call | solution.py:22
  24.7 2.5 %collective-permute-done.6.refs_2_ = bf16[328,256]{1,0:T(8,128)(2,1)S(1)} collective-permute-done((bf16[328,256]{1,0:T(8,128)(2,1)S(1)}, bf16[328,256]{1,0:T(8,128)(2,1)S(1)}, u32[]{:S(2)}, u32[]{:S(2)}) %collective-permute-start.6) | collective-permute-done | bytes 167968 | tf_op jit(solution)/shard_map/ppermute | solution.py:214
  27.3 1.8 %collective-permute-start.11 = (bf16[9,32,256]{2,1,0:T(8,128)(2,1)S(1)}, bf16[9,32,256]{2,1,0:T(8,128)(2,1)S(1)}, u32[]{:S(2)}, u32[]{:S(2)}) collective-permute-start(bf16[9,32,256]{2,1,0:T(8,128)(2,1)S(1)} %get-tuple-element.38), channel_id=1, source_target_pairs={{0,8},{4,12},{8,0},{12,4},{16,24},{20,28},{24,16},{28,20},{1,9},{5... | collective-permute-start | bytes 442376 | tf_op jit(solution)/shard_map/ppermute | solution.py:214
  29.3 3.4 %collective-permute-done.11 = bf16[9,32,256]{2,1,0:T(8,128)(2,1)S(1)} collective-permute-done((bf16[9,32,256]{2,1,0:T(8,128)(2,1)S(1)}, bf16[9,32,256]{2,1,0:T(8,128)(2,1)S(1)}, u32[]{:S(2)}, u32[]{:S(2)}) %collective-permute-start.11) | collective-permute-done | bytes 147488 | tf_op jit(solution)/shard_map/ppermute | solution.py:214
  32.8 1.5 %collective-permute-done.10.refs_5_ = bf16[272,256]{1,0:T(8,128)(2,1)S(1)} collective-permute-done((bf16[272,256]{1,0:T(8,128)(2,1)S(1)}, bf16[272,256]{1,0:T(8,128)(2,1)S(1)}, u32[]{:S(2)}, u32[]{:S(2)}) %collective-permute-start.10) | collective-permute-done | bytes 139296 | tf_op jit(solution)/shard_map/ppermute | solution.py:214
  35.0 1.2 %collective-permute-done.14.refs_4_ = bf16[128,256]{1,0:T(8,128)(2,1)S(1)} collective-permute-done((bf16[128,256]{1,0:T(8,128)(2,1)S(1)}, bf16[128,256]{1,0:T(8,128)(2,1)S(1)}, u32[]{:S(2)}, u32[]{:S(2)}) %collective-permute-start.14) | collective-permute-done | bytes 65568 | tf_op jit(solution)/shard_map/ppermute | solution.py:214
  36.6 2.7 %collective-permute-start.17 = (f32[9,8,256]{2,1,0:T(8,128)S(1)}, f32[9,8,256]{2,1,0:T(8,128)S(1)}, u32[]{:S(2)}, u32[]{:S(2)}) collective-permute-start(f32[9,8,256]{2,1,0:T(8,128)S(1)} %slice_add_fusion.4), channel_id=1, source_target_pairs={{0,16},{4,20},{8,24},{12,28},{16,0},{20,4},{24,8},{28,12},{1,17},{... | collective-permute-start | bytes 221192 | tf_op jit(solution)/shard_map/ppermute | solution.py:214
  39.8 1.6 %collective-permute-start.13 = (bf16[256,256]{1,0:T(8,128)(2,1)S(1)}, bf16[256,256]{1,0:T(8,128)(2,1)S(1)}, u32[]{:S(2)}, u32[]{:S(2)}) collective-permute-start(bf16[256,256]{1,0:T(8,128)(2,1)S(1)} %get-tuple-element.31), channel_id=1, source_target_pairs={{0,4},{4,0},{8,12},{12,8},{16,20},{20,16},{24,28},{28,24},{1,5},{5... | collective-permute-start | bytes 393224 | tf_op jit(solution)/shard_map/ppermute | solution.py:214
  41.4 2.6 %backward.1 = (bf16[256,128]{1,0:T(8,128)(2,1)S(1)}, bf16[256,128]{1,0:T(8,128)(2,1)S(1)}) custom-call(bf16[2,128,256]{2,1,0:T(8,128)(2,1)S(1)} %bitcast.118, bf16[2,128,256]{2,1,0:T(8,128)(2,1)S(1)} %bitcast.125, bf16[328,256]{1,0:T(8,128)(2,1)S(1)} %collective-permute-done.6.refs_2_, bf16[256,256]{1,0:T(8,128)(2,1)S(1)} %collective-permute-done.8.refs_3_, ...), custom_call_target="tpu_custom_call" | custom-call | flops 3623878656 | bytes 1417216 | tf_op jit(solution)/shard_map/backward/pallas_call | solution.py:22
  44.6 0.7 %copy.34 = f32[2,8,8,256]{3,1,2,0:T(8,128)} copy(f32[2,8,8,256]{3,2,1,0:T(8,128)S(1)} %bitcast.129) | data formatting | bytes 262144
  45.3 3.0 %collective-permute-done.15.refs_1_ = bf16[256,128]{1,0:T(8,128)(2,1)S(1)} collective-permute-done((bf16[256,128]{1,0:T(8,128)(2,1)S(1)}, bf16[256,128]{1,0:T(8,128)(2,1)S(1)}, u32[]{:S(2)}, u32[]{:S(2)}) %collective-permute-start.15) | collective-permute-done | bytes 65568 | tf_op jit(solution)/shard_map/ppermute | solution.py:214
  48.6 0.8 %copy.33 = bf16[2,128,256]{1,0,2:T(2,128)(2,1)} copy(bf16[2,128,256]{2,1,0:T(8,128)(2,1)S(1)} %bitcast.119) | data formatting | bytes 262144 | tf_op jit(solution)/shard_map/reshape | solution.py:374
  49.4 0.8 %copy.32 = bf16[2,128,256]{1,0,2:T(2,128)(2,1)} copy(bf16[2,128,256]{2,1,0:T(8,128)(2,1)S(1)} %bitcast.130) | data formatting | bytes 262144 | tf_op jit(solution)/shard_map/reshape | solution.py:374
  (80 shorter events, 3.7 us)
Async XLA Ops:
  0.6 9.4 %copy-start.1 = (bf16[16,5,33]{2,0,1:T(8,128)(2,1)S(1)}, bf16[16,5,33]{2,0,1:T(8,128)(2,1)}, u32[]{:S(2)}) copy-start(bf16[16,5,33]{2,0,1:T(8,128)(2,1)} %param.8) | copy-start | bytes 15844
  0.6 9.5 %copy-start.2 = (s32[16]{0:T(128)S(1)}, s32[16]{0:T(128)}, u32[]{:S(2)}) copy-start(s32[16]{0:T(128)} %param.10) | copy-start | bytes 196
  0.7 9.5 %copy-start = (s32[16,5,33]{2,0,1:T(8,128)S(1)}, s32[16,5,33]{2,0,1:T(8,128)}, u32[]{:S(2)}) copy-start(s32[16,5,33]{2,0,1:T(8,128)} %param.9) | copy-start | bytes 31684
  1.8 8.5 %collective-permute-start.1 = (bf16[128,2,128]{0,2,1:T(8,128)(2,1)S(1)}, bf16[128,2,128]{0,2,1:T(8,128)(2,1)S(1)}, u32[]{:S(2)}, u32[]{:S(2)}) collective-permute-start(bf16[128,2,128]{0,2,1:T(8,128)(2,1)S(1)} %copy.27), channel_id=1, source_target_pairs={{0,4},{4,0},{8,12},{12,8},{16,20},{20,16},{24,28},{28,24},{1,5},{5... | collective-permute-start | bytes 196616 | tf_op jit(solution)/shard_map/ppermute | solution.py:214
  5.8 11.1 %collective-permute-start.5 = (bf16[256,2,128]{0,2,1:T(8,128)(2,1)S(1)}, bf16[256,2,128]{0,2,1:T(8,128)(2,1)S(1)}, u32[]{:S(2)}, u32[]{:S(2)}) collective-permute-start(bf16[256,2,128]{0,2,1:T(8,128)(2,1)S(1)} %copy.28), channel_id=1, source_target_pairs={{0,4},{4,0},{8,12},{12,8},{16,20},{20,16},{24,28},{28,24},{1,5},{5... | collective-permute-start | bytes 393224 | tf_op jit(solution)/shard_map/ppermute | solution.py:214
  6.8 10.9 %collective-permute-start = (bf16[72,256]{1,0:T(8,128)(2,1)S(1)}, bf16[72,256]{1,0:T(8,128)(2,1)S(1)}, u32[]{:S(2)}, u32[]{:S(2)}) collective-permute-start(bf16[72,256]{1,0:T(8,128)(2,1)S(1)} %reshape.89), channel_id=1, source_target_pairs={{0,16},{4,20},{8,24},{12,28},{16,0},{20,4},{24,8},{28,12},{1,17},{... | collective-permute-start | bytes 110600 | tf_op jit(solution)/shard_map/ppermute | solution.py:214
  10.3 4.7 %collective-permute-start.2 = (bf16[200,256]{1,0:T(8,128)(2,1)S(1)}, bf16[200,256]{1,0:T(8,128)(2,1)S(1)}, u32[]{:S(2)}, u32[]{:S(2)}) collective-permute-start(bf16[200,256]{1,0:T(8,128)(2,1)S(1)} %pad_maximum_fusion.4), channel_id=1, source_target_pairs={{0,8},{4,12},{8,0},{12,4},{16,24},{20,28},{24,16},{28,20},{1,9},{5... | collective-permute-start | bytes 307208 | tf_op jit(solution)/shard_map/ppermute | solution.py:214
  12.0 0.7 %collective-permute-start.3 = (bf16[128,256]{1,0:T(8,128)(2,1)S(1)}, bf16[128,256]{1,0:T(8,128)(2,1)S(1)}, u32[]{:S(2)}, u32[]{:S(2)}) collective-permute-start(bf16[128,256]{1,0:T(8,128)(2,1)S(1)} %pad_maximum_fusion.5), channel_id=1, source_target_pairs={{8,16},{12,20},{16,8},{20,12},{9,17},{13,21},{17,9},{21,13},{10,18... | collective-permute-start | bytes 196616 | tf_op jit(solution)/shard_map/ppermute | solution.py:220
  15.1 7.9 %collective-permute-start.4 = (bf16[208,256]{1,0:T(8,128)(2,1)S(1)}, bf16[208,256]{1,0:T(8,128)(2,1)S(1)}, u32[]{:S(2)}, u32[]{:S(2)}) collective-permute-start(bf16[208,256]{1,0:T(8,128)(2,1)S(1)} %pad_maximum_fusion.3), channel_id=1, source_target_pairs={{0,3},{1,2},{2,1},{3,0},{4,7},{5,6},{6,5},{7,4},{8,11},{9,10},{10,... | collective-permute-start | bytes 319496 | tf_op jit(solution)/shard_map/ppermute | solution.py:214
  15.2 7.8 %collective-permute-start.7 = (bf16[64,256]{1,0:T(8,128)(2,1)S(1)}, bf16[64,256]{1,0:T(8,128)(2,1)S(1)}, u32[]{:S(2)}, u32[]{:S(2)}) collective-permute-start(bf16[64,256]{1,0:T(8,128)(2,1)S(1)} %broadcast_select_fusion.7), channel_id=1, source_target_pairs={{0,1},{1,0},{2,3},{3,2},{4,5},{5,4},{6,7},{7,6},{8,9},{9,8},{10,11... | collective-permute-start | bytes 98312 | tf_op jit(solution)/shard_map/ppermute | solution.py:214
  16.9 7.7 %collective-permute-start.8 = (bf16[256,256]{1,0:T(8,128)(2,1)S(1)}, bf16[256,256]{1,0:T(8,128)(2,1)S(1)}, u32[]{:S(2)}, u32[]{:S(2)}) collective-permute-start(bf16[256,256]{1,0:T(8,128)(2,1)S(1)} %pad_maximum_fusion.2), channel_id=1, source_target_pairs={{8,16},{12,20},{16,8},{20,12},{9,17},{13,21},{17,9},{21,13},{10,18... | collective-permute-start | bytes 393224 | tf_op jit(solution)/shard_map/ppermute | solution.py:220
  17.7 9.5 %collective-permute-start.6 = (bf16[328,256]{1,0:T(8,128)(2,1)S(1)}, bf16[328,256]{1,0:T(8,128)(2,1)S(1)}, u32[]{:S(2)}, u32[]{:S(2)}) collective-permute-start(bf16[328,256]{1,0:T(8,128)(2,1)S(1)} %pad_maximum_fusion), channel_id=1, source_target_pairs={{0,8},{4,12},{8,0},{12,4},{16,24},{20,28},{24,16},{28,20},{1,9},{5... | collective-permute-start | bytes 503816 | tf_op jit(solution)/shard_map/ppermute | solution.py:214
  24.6 2.7 %collective-permute-start.9 = (f32[9,64,256]{2,1,0:T(8,128)S(1)}, f32[9,64,256]{2,1,0:T(8,128)S(1)}, u32[]{:S(2)}, u32[]{:S(2)}) collective-permute-start(f32[9,64,256]{2,1,0:T(8,128)S(1)} %get-tuple-element.23), channel_id=1, source_target_pairs={{0,1},{1,0},{2,3},{3,2},{4,5},{5,4},{6,7},{7,6},{8,9},{9,8},{10,11... | collective-permute-start | bytes 1769480 | tf_op jit(solution)/shard_map/ppermute | solution.py:214
  27.3 5.3 %collective-permute-start.11 = (bf16[9,32,256]{2,1,0:T(8,128)(2,1)S(1)}, bf16[9,32,256]{2,1,0:T(8,128)(2,1)S(1)}, u32[]{:S(2)}, u32[]{:S(2)}) collective-permute-start(bf16[9,32,256]{2,1,0:T(8,128)(2,1)S(1)} %get-tuple-element.38), channel_id=1, source_target_pairs={{0,8},{4,12},{8,0},{12,4},{16,24},{20,28},{24,16},{28,20},{1,9},{5... | collective-permute-start | bytes 442376 | tf_op jit(solution)/shard_map/ppermute | solution.py:214
  29.2 5.1 %collective-permute-start.10 = (bf16[272,256]{1,0:T(8,128)(2,1)S(1)}, bf16[272,256]{1,0:T(8,128)(2,1)S(1)}, u32[]{:S(2)}, u32[]{:S(2)}) collective-permute-start(bf16[272,256]{1,0:T(8,128)(2,1)S(1)} %pad_maximum_fusion.1), channel_id=1, source_target_pairs={{0,3},{1,2},{2,1},{3,0},{4,7},{5,6},{6,5},{7,4},{8,11},{9,10},{10,... | collective-permute-start | bytes 417800 | tf_op jit(solution)/shard_map/ppermute | solution.py:214
  32.7 3.8 %collective-permute-start.16 = (bf16[9,16,256]{2,1,0:T(8,128)(2,1)S(1)}, bf16[9,16,256]{2,1,0:T(8,128)(2,1)S(1)}, u32[]{:S(2)}, u32[]{:S(2)}) collective-permute-start(bf16[9,16,256]{2,1,0:T(8,128)(2,1)S(1)} %get-tuple-element.40), channel_id=1, source_target_pairs={{0,3},{1,2},{2,1},{3,0},{4,7},{5,6},{6,5},{7,4},{8,11},{9,10},{10,... | collective-permute-start | bytes 221192 | tf_op jit(solution)/shard_map/ppermute | solution.py:214
  34.4 4.9 %collective-permute-start.12 = (bf16[9,64,256]{2,1,0:T(8,128)(2,1)S(1)}, bf16[9,64,256]{2,1,0:T(8,128)(2,1)S(1)}, u32[]{:S(2)}, u32[]{:S(2)}) collective-permute-start(bf16[9,64,256]{2,1,0:T(8,128)(2,1)S(1)} %get-tuple-element.49), channel_id=1, source_target_pairs={{0,1},{1,0},{2,3},{3,2},{4,5},{5,4},{6,7},{7,6},{8,9},{9,8},{10,11... | collective-permute-start | bytes 884744 | tf_op jit(solution)/shard_map/ppermute | solution.py:214
  34.5 1.7 %collective-permute-start.14 = (bf16[128,256]{1,0:T(8,128)(2,1)S(1)}, bf16[128,256]{1,0:T(8,128)(2,1)S(1)}, u32[]{:S(2)}, u32[]{:S(2)}) collective-permute-start(bf16[128,256]{1,0:T(8,128)(2,1)S(1)} %get-tuple-element.33), channel_id=1, source_target_pairs={{0,1},{1,0},{2,3},{3,2},{4,5},{5,4},{6,7},{7,6},{8,9},{9,8},{10,11... | collective-permute-start | bytes 196616 | tf_op jit(solution)/shard_map/ppermute | solution.py:214
  36.6 8.0 %collective-permute-start.17 = (f32[9,8,256]{2,1,0:T(8,128)S(1)}, f32[9,8,256]{2,1,0:T(8,128)S(1)}, u32[]{:S(2)}, u32[]{:S(2)}) collective-permute-start(f32[9,8,256]{2,1,0:T(8,128)S(1)} %slice_add_fusion.4), channel_id=1, source_target_pairs={{0,16},{4,20},{8,24},{12,28},{16,0},{20,4},{24,8},{28,12},{1,17},{... | collective-permute-start | bytes 221192 | tf_op jit(solution)/shard_map/ppermute | solution.py:214
  39.8 9.6 %collective-permute-start.13 = (bf16[256,256]{1,0:T(8,128)(2,1)S(1)}, bf16[256,256]{1,0:T(8,128)(2,1)S(1)}, u32[]{:S(2)}, u32[]{:S(2)}) collective-permute-start(bf16[256,256]{1,0:T(8,128)(2,1)S(1)} %get-tuple-element.31), channel_id=1, source_target_pairs={{0,4},{4,0},{8,12},{12,8},{16,20},{20,16},{24,28},{28,24},{1,5},{5... | collective-permute-start | bytes 393224 | tf_op jit(solution)/shard_map/ppermute | solution.py:214
  44.0 4.3 %collective-permute-start.15 = (bf16[256,128]{1,0:T(8,128)(2,1)S(1)}, bf16[256,128]{1,0:T(8,128)(2,1)S(1)}, u32[]{:S(2)}, u32[]{:S(2)}) collective-permute-start(bf16[256,128]{1,0:T(8,128)(2,1)S(1)} %get-tuple-element.36), channel_id=1, source_target_pairs={{0,4},{4,0},{8,12},{12,8},{16,20},{20,16},{24,28},{28,24},{1,5},{5... | collective-permute-start | bytes 196616 | tf_op jit(solution)/shard_map/ppermute | solution.py:214

commit v5 on v4

--- a/solution.py
+++ b/solution.py
@@ -99,8 +99,9 @@
     return jnp.concatenate(parts, axis=0)
 
 
-def place_rows(scr, move, own_ref, pair_ref, near_ref, next_ref, core_ref, cross_ref):
-    rows, cols, channels = own_ref.shape
+def place_rows(scr, move, own_ref, pair_ref, near_ref, next_ref, core_ref, cross_ref, base, rim_base):
+    rows, cols, _ = own_ref.shape
+    channels = scr.shape[2]
     lat, lon = lax.axis_index("lat"), lax.axis_index("lon")
     odd, flip = lat & 1, (lat >> 1) & 1
     even_col = (lon & 1) == 0
@@ -108,15 +109,18 @@
     wide = near_ref.shape[1] // channels
 
     def part(ref, first, row, length):
-        low = (first + row // wide) * length
+        low = first + row // wide * length
         return ref[low : low + length, row % wide * channels : (row % wide + 1) * channels]
 
     slots = ((1 - flip) * 3 * rows, (1 + odd) * rows, (2 - odd) * rows, flip * 3 * rows)
     for rank, slot in enumerate(slots):
         for row in range(rows):
-            line = part((near_ref, next_ref)[rank // 3], 0, row, cols) if rank in (0, 3) else (own_ref, pair_ref)[rank - 1][row]
-            core = part(core_ref, rank * (rows // wide), row, rim)
-            cross = part(cross_ref, rank * (rows // wide), row, rim)
+            if rank in (0, 3):
+                line = part((near_ref, next_ref)[rank // 3], base, row, cols)
+            else:
+                line = (own_ref, pair_ref)[rank - 1][row]
+            first = rim_base + rank * (rows // wide) * rim
+            core, cross = part(core_ref, first, row, rim), part(cross_ref, first, row, rim)
             scr[slot + row, rim : rim + cols, :] = move(line)
             scr[slot + row, :rim, :] = move(jnp.where(even_col, cross, core))
             scr[slot + row, rim + cols :, :] = move(jnp.where(even_col, core, cross))
@@ -124,12 +128,15 @@
 
 def forward_body(lay, offsets, own_ref, pair_ref, near_ref, next_ref, core_ref, cross_ref, taps_ref, index_ref,
                  own_cot_ref, pair_cot_ref, out_ref, send_ref, keep_ref, ext_scr):
-    rows, cols, channels = own_ref.shape
-    basis_count = out_ref.shape[0]
+    rows, cols, _ = own_ref.shape
+    basis_count, _, channels = out_ref.shape
     odd = lay.odd()
     shape = (channels, channels)
     pick = (lax.broadcasted_iota(jnp.int32, shape, 0) == lay.places(shape, 1)).astype(bf16)
-    place_rows(ext_scr, lambda v: dot(v, pick).astype(bf16), own_ref, pair_ref, near_ref, next_ref, core_ref, cross_ref)
+    place_rows(
+        ext_scr, lambda v: dot(v, pick).astype(bf16),
+        own_ref, pair_ref, near_ref, next_ref, core_ref, cross_ref, 0, 0,
+    )
     first_row = (lax.axis_index("lat") - odd) * rows
     for line in range(2 * rows):
         low = (odd if line < rows else 1 - odd) * rows + line % rows
@@ -168,7 +175,12 @@
     rows, cols, _ = own_ref.shape
     basis_count, channels, outs = weight_ref.shape
     odd = lay.odd()
-    place_rows(ext_scr, lambda v: v, own_ref, pair_ref, near_ref, next_ref, core_ref, cross_ref)
+    rim = (ext_scr.shape[1] - cols) // 2
+    beside = outs // channels
+    place_rows(
+        ext_scr, lambda v: v, own_ref, pair_ref, near_ref, next_ref, core_ref, cross_ref,
+        rows // beside * cols, 4 * (rows // beside) * rim,
+    )
     weight = weight_ref[...].reshape(basis_count * channels, outs)
     first_row = (lax.axis_index("lat") - odd) * rows
     ext_rows, ext_cols, _ = ext_scr.shape
@@ -228,32 +240,35 @@
     return jnp.concatenate(lines, axis=0)
 
 
-def row_halo(own, pair, width, near_more):
+def row_halo(own, pair, near_more):
     lat = lax.axis_index("lat")
     own_first = (lat & 1) != ((lat >> 1) & 1)
-    to_near, to_far = jnp.where(own_first, own, pair), jnp.where(own_first, pair, own)
-    near = swap(jnp.concatenate([flat(to_near, width), *near_more], axis=0), "lat", 2)
-    return near, swap_across(flat(to_far, width), "lat", 2, False)
-
-
-def edges(near, own, pair, far, rim, width):
-    rows, cols, channels = own.shape
-    lines = rows * channels // width
+    width = own[1].shape[2]
+    to_near = [flat(jnp.where(own_first, a, b), width) for a, b in zip(own, pair)]
+    to_far = [flat(jnp.where(own_first, b, a), width) for a, b in zip(own, pair)]
+    near = swap(jnp.concatenate([*to_near, *near_more], axis=0), "lat", 2)
+    return near, swap_across(jnp.concatenate(to_far, axis=0), "lat", 2, False)
+
+
+def edges(near, own, pair, far, rim):
+    rows, cols, width = own[1].shape
 
     def at(first):
-        def halo(v):
-            return [v[line * cols + first : line * cols + first + rim] for line in range(lines)]
-
-        kept = [flat(v[:, first : first + rim], width) for v in (own, pair)]
-        return jnp.concatenate([*halo(near), *kept, *halo(far)], axis=0)
+        fields, base = [], 0
+        for a, b in zip(own, pair):
+            lines = rows * a.shape[2] // width
+            starts = [base + line * cols + first for line in range(lines)]
+            kept = [flat(v[:, first : first + rim], width) for v in (a, b)]
+            fields += [near[start : start + rim] for start in starts] + kept + [far[start : start + rim] for start in starts]
+            base += lines * cols
+        return jnp.concatenate(fields, axis=0)
 
     even = (lax.axis_index("lon") & 1) == 0
     left, right = at(0), at(cols - rim)
     return jnp.where(even, right, left), jnp.where(even, left, right)
 
 
-def column_halo(lay, to_core, to_cross, cross_more):
-    to_cross = jnp.concatenate([to_cross, *cross_more], axis=0)
+def column_halo(lay, to_core, to_cross):
     cross = swap(to_cross, "lon", 3) if lay.merged else swap_across(to_cross, "lon", 1, True)
     return swap(to_core, "lon", 1), cross
 
@@ -270,10 +285,11 @@
     split = features.reshape(half // lay.pair, 2, lay.pair, rows, cols)
     to_pair = lax.dynamic_index_in_dim(split, 1 - odd, 1, False).reshape(half, rows, cols)
     to_keep = lax.dynamic_index_in_dim(split, odd, 1, False).reshape(half, rows, cols)
-    feat_pair = jnp.transpose(swap(to_pair, "lat", 1), (1, 2, 0))
-    feat_own = jnp.transpose(to_keep, (1, 2, 0))
-    cot_pair = jnp.transpose(swap(cotangent, "lat", 1), (1, 2, 0))
-    cot_own = jnp.transpose(cotangent, (1, 2, 0))
+    def channels_last(v):
+        return jnp.transpose(v, (1, 2, 0))
+
+    pair = channels_last(swap(to_pair, "lat", 1)), channels_last(swap(cotangent, "lat", 1))
+    mine = channels_last(to_keep), channels_last(cotangent)
 
     far = jnp.abs(jnp.arange(window) - rim)
     index = jnp.where(far[None, None, :] <= half_width[:, None, None], basis_index, -1)
@@ -296,20 +312,17 @@
     def tail(array, count):
         return [array[array.shape[0] - (i + 1) * lot : array.shape[0] - i * lot] for i in reversed(range(count))]
 
-    own, by_next = [], []
+    own = [lax.optimization_barrier(weight.reshape(lot, channels))] if lay.merged else []
+    near, far = row_halo(mine, pair, own)
+    by_near = tail(near, len(own))
+    to_core, to_cross = edges(near, mine, pair, far, rim)
+    core, cross = column_halo(lay, to_core, to_cross)
     if lay.merged:
-        own = [after(weight, to_pair).reshape(lot, channels)]
-        own = [lax.optimization_barrier(own[0])]
-        by_next = [swap(own[0], "lat", 4)]
-    near, far = row_halo(feat_own, feat_pair, channels, own)
-    by_near = tail(near, len(own))
-    to_core, to_cross = edges(near, feat_own, feat_pair, far, rim, channels)
-    core, cross = column_halo(lay, to_core, to_cross, own + by_near)
-    if not lay.merged:
+        held = jnp.concatenate(own + by_near, axis=0)
+        held = [held, swap(after(held, to_core, to_cross), "lat", 4)]
+    else:
         for step in gather[:-1]:
             full = widen(full, step)
-    by_next = [after(v, to_core, to_cross) for v in by_next]
-    cot_near, cot_far = row_halo(after(cot_own, to_core, to_cross), cot_pair, channels, by_next)
 
     cells = rows * cols
     ext = (4 * rows, cols + 2 * rim)
@@ -317,36 +330,35 @@
         lambda *refs: forward_body(lay, offsets, *refs), "forward", 16 * basis_count * cells * half * channels,
         [((basis_count, 2 * cells, half), bf16), ((basis_count, half // 2, channels), f32),
          ((basis_count, half // 2, channels), f32)],
-        feat_own, feat_pair, near, far, core, cross, taps, index, cot_own, cot_pair,
+        mine[0], pair[0], near, far, core, cross, taps, index, mine[1], pair[1],
         scratch=[pltpu.VMEM((*ext, half), bf16)],
     )
     for rank, (axis, flip, _) in enumerate(lay.steps):
         terms = (keep, swap(send, axis, flip))
-        if rank == 0:
-            cot_near, cot_far = after(cot_near, send), after(cot_far, send)
+        if rank == 2:
+            terms = (keep, after(terms[1], own_grad))
+        elif rank == 0:
+            if lay.merged:
+                held = [after(v, send) for v in held]
+                (first, third), (second, fourth) = ((v[:lot], v[lot:]) for v in held)
+                held = jnp.concatenate([first, second, third, fourth], axis=0)
+                other = swap(held, "lon", 3)
         elif rank == 1:
-            by_both = tail(cot_near, len(own))
-            to_core, to_cross = edges(cot_near, cot_own, cot_pair, cot_far, rim, channels)
-            to_core, to_cross = after(to_core, send), after(to_cross, send)
-            cot_core, cot_cross = column_halo(lay, to_core, to_cross, by_next + by_both)
-        elif rank == 2:
-            cot_core, cot_cross = after(cot_core, send), after(cot_cross, send)
-            cot_around = (cot_near, cot_far, cot_core, cot_cross)
             if lay.merged:
-                crossed, crossed_last = tail(cross, 2), tail(cot_cross, 2)
-                held = own + by_next + crossed[:1] + crossed_last[:1] + by_near + by_both + crossed[1:] + crossed_last[1:]
-                full = jnp.concatenate([v.reshape(basis_count, lay.own, channels) for v in held], axis=1)
+                other = after(other, send)
+                blocks = [v[i * lot : (i + 1) * lot] for v, i in ((held, 0), (held, 1), (other, 0), (other, 1),
+                                                                  (held, 2), (held, 3), (other, 2), (other, 3))]
+                full = jnp.concatenate([v.reshape(basis_count, lay.own, channels) for v in blocks], axis=1)
             full = widen(full, gather[-1])
             own_out, pair_out = call(
                 mix_body, "mix", 4 * basis_count * cells * half * channels, [((cells, channels), f32), ((cells, channels), bf16)], full, basis_out
             )
-            cot_after = after(cot_own, pair_out)
+            mine_after = after(mine[1], pair_out)
             pair_out = swap(pair_out, "lat", 1)
-            cot_around = (cot_near, cot_far, cot_core, cot_cross)
             own_grad, pair_grad = call(
                 lambda *refs: backward_body(lay, offsets, *refs), "backward", 48 * basis_count * cells * half * channels,
                 [((cells, half), bf16), ((cells, half), bf16)],
-                cot_after, cot_pair, *cot_around, taps, index, full,
+                mine_after, pair[1], near, far, core, cross, taps, index, full,
                 scratch=[pltpu.VMEM((*ext, channels), bf16),
                          pltpu.VMEM((ext[0] * basis_count * TILE, ext[1] // TILE * half), bf16),
                          pltpu.VMEM((ext[0] * basis_count * TILE, 2 * rows * SLOT), bf16),
@@ -355,9 +367,18 @@
             pair_grad = swap(pair_grad, "lat", 1)
         if rank + 1 < len(lay.steps):
             size = keep.shape[1] // 2
-            send = (terms[0][:, size:] + terms[1][:, size:]).astype(bf16 if rank < 2 else f32)
+            send = (terms[0][:, size:] + terms[1][:, size:]).astype(bf16 if rank < 3 else f32)
             keep = terms[0][:, :size] + terms[1][:, :size]
-    grad = terms[0] + terms[1]
+    output = (own_out + pair_out).astype(bf16)
+    (input_grad,) = call(
+        lambda *refs: finish_body(lay, *refs), "finish", 4 * cells * half * channels, [((cells, channels), bf16)], own_grad, pair_grad
+    )
+
+    def channels_first(v):
+        return jnp.transpose(v.reshape(rows, cols, channels), (2, 0, 1))
+
+    output, input_grad = channels_first(output), channels_first(input_grad)
+    grad = terms[0] + after(terms[1], output, input_grad)
     for axis, flip, _ in reversed(lay.split):
         size = grad.shape[2] // 2
         odd_part = (lax.axis_index(axis) // flip) % 2
@@ -365,15 +386,7 @@
         grad = lax.dynamic_slice_in_dim(grad, odd_part * size, size, 2) + other
     weight_grad = grad.reshape(basis_count, weight.shape[1])
 
-    output = (own_out + pair_out).astype(bf16)
-    (input_grad,) = call(
-        lambda *refs: finish_body(lay, *refs), "finish", 4 * cells * half * channels, [((cells, channels), bf16)], own_grad, pair_grad
-    )
-
-    def channels_first(v):
-        return jnp.transpose(v.reshape(rows, cols, channels), (2, 0, 1))
-
-    return channels_first(output), channels_first(input_grad), weight_grad
+    return output, input_grad, weight_grad
 
 
 def solution(mesh):

time: 50.4 us -> 47.7 us (0.946)
  starting transfers between devices: 23.7 us -> 19.1 us
  waiting for transfers between devices: 14.4 us -> 15.6 us
  local copies, waits for them, and re-layouts: 5.53 us -> 6.29 us
    ppermute x16 -> x14, starting transfers between devices: 22.4 us -> 18.4 us  [swap(): lax.ppermute(array, axis, [(i, i ^ stride) for i in range(lax.axis_size(a...]
    ppermute x16 -> x14, waiting for transfers between devices: 14.4 us -> 15.6 us  [swap(): lax.ppermute(array, axis, [(i, i ^ stride) for i in range(lax.axis_size(a...]
    unnamed x25 -> x30, local copies, waits for them, and re-layouts: 2.75 us -> 3.5 us
    ppermute x2 -> x1, starting transfers between devices: 1.33 us -> 0.67 us  [swap_across(): lax.ppermute(array, axis, [(i, j % size) for i, j in pairs if wrap or 0 <...]
  transfers between devices with their start and end apart: 18 -> 15, of which waited for: 7 -> 7; matrix products, arithmetic and copies ran while one was open for 8% -> 10% of each run, Pallas kernels for 10% -> 10%
where the time goes in v5:
time: 47.7 us; the launch traced here: 47.5 us
  starting transfers between devices  19.1 us (40%)
  waiting for transfers between devices  15.6 us (33%)
  local copies, waits for them, and re-layouts  6.29 us (13%)
  Pallas kernels  4.97 us (10%)
  between operations  1.12 us (2%)
    ppermute x14, starting transfers between devices, swap(): lax.ppermute(array, axis, [(i, i ^ stride) for i in range(lax.axis_size(a...  18.4 us
    ppermute x14, waiting for transfers between devices, swap(): lax.ppermute(array, axis, [(i, i ^ stride) for i in range(lax.axis_size(a...  15.6 us
    pallas_call x4, Pallas kernels, call(): pl.pallas_call(body, name=name, out_shape=[jax.ShapeDtypeStruct(s, d) for...  4.97 us
    unnamed x30, local copies, waits for them, and re-layouts  3.5 us
    reshape x2, local copies, waits for them, and re-layouts, channels_first(): return jnp.transpose(v.reshape(rows, cols, channels), (2, 0, 1))  1.56 us
  transfers between devices with their start and end apart: 15, of which 7 were waited for; matrix products, arithmetic and copies ran while one was open for 10% of the time, Pallas kernels for 10%

profile of v5, /device:TPU:0, one launch (start us, length us, event | category | flops | bytes accessed | tf_op | source)
XLA Modules:
  0.0 47.5 jit_solution(15184634411112620123)
XLA Ops:
  0.7 0.9 %copy.25 = bf16[256,2,128]{2,0,1:T(8,128)(2,1)S(1)} copy(bf16[256,2,128]{2,1,0:T(2,128)(2,1)} %param.6) | data formatting | bytes 262144 | tf_op args[0]
  1.7 3.0 %collective-permute-start = (bf16[128,2,128]{0,2,1:T(8,128)(2,1)S(1)}, bf16[128,2,128]{0,2,1:T(8,128)(2,1)S(1)}, u32[]{:S(2)}, u32[]{:S(2)}) collective-permute-start(bf16[128,2,128]{0,2,1:T(8,128)(2,1)S(1)} %copy.27), channel_id=1, source_target_pairs={{0,4},{4,0},{8,12},{12,8},{16,20},{20,16},{24,28},{28,24},{1,5},{5... | collective-permute-start | bytes 196616 | tf_op jit(solution)/shard_map/ppermute | solution.py:226
  4.8 1.0 %copy.28 = bf16[256,2,128]{0,2,1:T(8,128)(2,1)S(1)} copy(bf16[256,2,128]{2,1,0:T(2,128)(2,1)} %param.11) | data formatting | bytes 262144 | tf_op args[5]
  5.9 0.7 %copy.30 = bf16[16,5,33]{2,1,0:T(8,128)(2,1)S(1)} copy(bf16[16,5,33]{2,0,1:T(8,128)(2,1)} %param.8) | data formatting | bytes 10560 | tf_op args[2]
  6.6 0.9 %reshape.87 = bf16[72,256]{1,0:T(8,128)(2,1)S(1)} reshape(bf16[9,2048]{1,0:T(8,128)(2,1)} %param.7) | data formatting | bytes 73728 | tf_op jit(solution)/shard_map/reshape | solution.py:315
  7.9 3.0 %collective-permute-done.1 = bf16[256,2,128]{0,2,1:T(8,128)(2,1)S(1)} collective-permute-done((bf16[256,2,128]{0,2,1:T(8,128)(2,1)S(1)}, bf16[256,2,128]{0,2,1:T(8,128)(2,1)S(1)}, u32[]{:S(2)}, u32[]{:S(2)}) %collective-permute-start.1) | collective-permute-done | bytes 131104 | tf_op jit(solution)/shard_map/ppermute | solution.py:226
  10.9 1.6 %collective-permute-start.2 = (bf16[456,256]{1,0:T(8,128)(2,1)S(1)}, bf16[456,256]{1,0:T(8,128)(2,1)S(1)}, u32[]{:S(2)}, u32[]{:S(2)}) collective-permute-start(bf16[456,256]{1,0:T(8,128)(2,1)S(1)} %pad_maximum_fusion), channel_id=1, source_target_pairs={{0,8},{4,12},{8,0},{12,4},{16,24},{20,28},{24,16},{28,20},{1,9},{5... | collective-permute-start | bytes 700424 | tf_op jit(solution)/shard_map/ppermute | solution.py:226
  12.6 0.7 %collective-permute-start.3 = (bf16[384,256]{1,0:T(8,128)(2,1)S(1)}, bf16[384,256]{1,0:T(8,128)(2,1)S(1)}, u32[]{:S(2)}, u32[]{:S(2)}) collective-permute-start(bf16[384,256]{1,0:T(8,128)(2,1)S(1)} %pad_maximum_fusion.1), channel_id=1, source_target_pairs={{8,16},{12,20},{16,8},{20,12},{9,17},{13,21},{17,9},{21,13},{10,18... | collective-permute-start | bytes 589832 | tf_op jit(solution)/shard_map/ppermute | solution.py:232
  13.3 3.8 %collective-permute-done.2.refs_2_ = bf16[456,256]{1,0:T(8,128)(2,1)S(1)} collective-permute-done((bf16[456,256]{1,0:T(8,128)(2,1)S(1)}, bf16[456,256]{1,0:T(8,128)(2,1)S(1)}, u32[]{:S(2)}, u32[]{:S(2)}) %collective-permute-start.2) | collective-permute-done | bytes 233504 | tf_op jit(solution)/shard_map/ppermute | solution.py:226
  17.3 1.6 %collective-permute-start.4 = (bf16[192,256]{1,0:T(8,128)(2,1)S(1)}, bf16[192,256]{1,0:T(8,128)(2,1)S(1)}, u32[]{:S(2)}, u32[]{:S(2)}) collective-permute-start(bf16[192,256]{1,0:T(8,128)(2,1)S(1)} %get-tuple-element.44), channel_id=1, source_target_pairs={{0,1},{1,0},{2,3},{3,2},{4,5},{5,4},{6,7},{7,6},{8,9},{9,8},{10,11... | collective-permute-start | bytes 294920 | tf_op jit(solution)/shard_map/ppermute | solution.py:226
  18.9 5.7 %collective-permute-start.6 = (bf16[144,256]{1,0:T(8,128)(2,1)S(1)}, bf16[144,256]{1,0:T(8,128)(2,1)S(1)}, u32[]{:S(2)}, u32[]{:S(2)}) collective-permute-start(bf16[144,256]{1,0:T(8,128)(2,1)S(1)} %pad_maximum_fusion.3), channel_id=1, source_target_pairs={{0,16},{4,20},{8,24},{12,28},{16,0},{20,4},{24,8},{28,12},{1,17},{... | collective-permute-start | bytes 221192 | tf_op jit(solution)/shard_map/ppermute | solution.py:226
  24.6 1.6 %forward.1 = (bf16[9,512,128]{2,1,0:T(8,128)(2,1)S(1)}, f32[9,64,256]{2,1,0:T(8,128)S(1)}, f32[9,64,256]{2,1,0:T(8,128)S(1)}) custom-call(bf16[2,128,128]{2,1,0:T(8,128)(2,1)S(1)} %bitcast.116, bf16[2,128,128]{2,1,0:T(8,128)(2,1)S(1)} %bitcast.122, bf16[456,256]{1,0:T(8,128)(2,1)S(1)} %collective-permute-done.2.refs_2_, ...), custom_call_target="tpu_custom_call" | custom-call | flops 1207959552 | bytes 1081344 | tf_op jit(solution)/shard_map/forward/pallas_call | solution.py:22
  26.3 2.4 %collective-permute-done.6 = bf16[144,256]{1,0:T(8,128)(2,1)S(1)} collective-permute-done((bf16[144,256]{1,0:T(8,128)(2,1)S(1)}, bf16[144,256]{1,0:T(8,128)(2,1)S(1)}, u32[]{:S(2)}, u32[]{:S(2)}) %collective-permute-start.6) | collective-permute-done | bytes 73760 | tf_op jit(solution)/shard_map/ppermute | solution.py:226
  28.9 1.4 %collective-permute-start.12 = (bf16[9,32,256]{2,1,0:T(8,128)(2,1)S(1)}, bf16[9,32,256]{2,1,0:T(8,128)(2,1)S(1)}, u32[]{:S(2)}, u32[]{:S(2)}) collective-permute-start(bf16[9,32,256]{2,1,0:T(8,128)(2,1)S(1)} %get-tuple-element.32), channel_id=1, source_target_pairs={{0,8},{4,12},{8,0},{12,4},{16,24},{20,28},{24,16},{28,20},{1,9},{5... | collective-permute-start | bytes 442376 | tf_op jit(solution)/shard_map/ppermute | solution.py:226
  30.3 4.2 %collective-permute-done.7 = bf16[288,256]{1,0:T(8,128)(2,1)S(1)} collective-permute-done((bf16[288,256]{1,0:T(8,128)(2,1)S(1)}, bf16[288,256]{1,0:T(8,128)(2,1)S(1)}, u32[]{:S(2)}, u32[]{:S(2)}) %collective-permute-start.7) | collective-permute-done | bytes 147488 | tf_op jit(solution)/shard_map/ppermute | solution.py:226
  34.7 0.6 %collective-permute-done.12 = bf16[9,32,256]{2,1,0:T(8,128)(2,1)S(1)} collective-permute-done((bf16[9,32,256]{2,1,0:T(8,128)(2,1)S(1)}, bf16[9,32,256]{2,1,0:T(8,128)(2,1)S(1)}, u32[]{:S(2)}, u32[]{:S(2)}) %collective-permute-start.12) | collective-permute-done | bytes 147488 | tf_op jit(solution)/shard_map/ppermute | solution.py:226
  35.3 1.1 %collective-permute-start.13 = (bf16[9,16,256]{2,1,0:T(8,128)(2,1)S(1)}, bf16[9,16,256]{2,1,0:T(8,128)(2,1)S(1)}, u32[]{:S(2)}, u32[]{:S(2)}) collective-permute-start(bf16[9,16,256]{2,1,0:T(8,128)(2,1)S(1)} %get-tuple-element.33), channel_id=1, source_target_pairs={{0,3},{1,2},{2,1},{3,0},{4,7},{5,6},{6,5},{7,4},{8,11},{9,10},{10,... | collective-permute-start | bytes 221192 | tf_op jit(solution)/shard_map/ppermute | solution.py:226
  37.4 2.6 %backward.1 = (bf16[256,128]{1,0:T(8,128)(2,1)S(1)}, bf16[256,128]{1,0:T(8,128)(2,1)S(1)}) custom-call(bf16[2,128,256]{2,1,0:T(8,128)(2,1)S(1)} %bitcast.113, bf16[2,128,256]{2,1,0:T(8,128)(2,1)S(1)} %bitcast.120, bf16[456,256]{1,0:T(8,128)(2,1)S(1)} %collective-permute-done.2.refs_2_, bf16[384,256]{1,0:T(8,128)(2,1)S(1)} %collective-permute-done.3.refs_3_, ...), custom_call_target="tpu_custom_call" | custom-call | flops 3623878656 | bytes 1540096 | tf_op jit(solution)/shard_map/backward/pallas_call | solution.py:22
  40.0 1.8 %collective-permute-start.11 = (bf16[256,128]{1,0:T(8,128)(2,1)S(1)}, bf16[256,128]{1,0:T(8,128)(2,1)S(1)}, u32[]{:S(2)}, u32[]{:S(2)}) collective-permute-start(bf16[256,128]{1,0:T(8,128)(2,1)S(1)} %get-tuple-element.28), channel_id=1, source_target_pairs={{0,4},{4,0},{8,12},{12,8},{16,20},{20,16},{24,28},{28,24},{1,5},{5... | collective-permute-start | bytes 196616 | tf_op jit(solution)/shard_map/ppermute | solution.py:226
  41.8 1.4 %collective-permute-start.14 = (bf16[9,8,256]{2,1,0:T(8,128)(2,1)S(1)}, bf16[9,8,256]{2,1,0:T(8,128)(2,1)S(1)}, u32[]{:S(2)}, u32[]{:S(2)}) collective-permute-start(bf16[9,8,256]{2,1,0:T(8,128)(2,1)S(1)} %fusion.2), channel_id=1, source_target_pairs={{0,16},{4,20},{8,24},{12,28},{16,0},{20,4},{24,8},{28,12},{1,17},{... | collective-permute-start | bytes 110600 | tf_op jit(solution)/shard_map/ppermute | solution.py:226
  43.2 1.2 %collective-permute-done.11.refs_1_ = bf16[256,128]{1,0:T(8,128)(2,1)S(1)} collective-permute-done((bf16[256,128]{1,0:T(8,128)(2,1)S(1)}, bf16[256,128]{1,0:T(8,128)(2,1)S(1)}, u32[]{:S(2)}, u32[]{:S(2)}) %collective-permute-start.11) | collective-permute-done | bytes 65568 | tf_op jit(solution)/shard_map/ppermute | solution.py:226
  44.7 0.8 %copy.33 = bf16[2,128,256]{1,0,2:T(2,128)(2,1)} copy(bf16[2,128,256]{2,1,0:T(8,128)(2,1)S(1)} %bitcast.114) | data formatting | bytes 262144 | tf_op jit(solution)/shard_map/reshape | solution.py:378
  45.5 0.8 %copy.32 = bf16[2,128,256]{1,0,2:T(2,128)(2,1)} copy(bf16[2,128,256]{2,1,0:T(8,128)(2,1)S(1)} %bitcast.125) | data formatting | bytes 262144 | tf_op jit(solution)/shard_map/reshape | solution.py:378
  46.8 0.7 %copy.34 = f32[2,8,8,256]{3,1,2,0:T(8,128)} copy(f32[2,8,8,256]{3,2,1,0:T(8,128)S(1)} %bitcast.124) | data formatting | bytes 262144
  (77 shorter events, 3.0 us)
Async XLA Ops:
  0.6 7.0 %copy-start.1 = (s32[16]{0:T(128)S(1)}, s32[16]{0:T(128)}, u32[]{:S(2)}) copy-start(s32[16]{0:T(128)} %param.10) | copy-start | bytes 196
  0.6 7.1 %copy-start = (s32[16,5,33]{2,0,1:T(8,128)S(1)}, s32[16,5,33]{2,0,1:T(8,128)}, u32[]{:S(2)}) copy-start(s32[16,5,33]{2,0,1:T(8,128)} %param.9) | copy-start | bytes 31684
  1.7 6.1 %collective-permute-start = (bf16[128,2,128]{0,2,1:T(8,128)(2,1)S(1)}, bf16[128,2,128]{0,2,1:T(8,128)(2,1)S(1)}, u32[]{:S(2)}, u32[]{:S(2)}) collective-permute-start(bf16[128,2,128]{0,2,1:T(8,128)(2,1)S(1)} %copy.27), channel_id=1, source_target_pairs={{0,4},{4,0},{8,12},{12,8},{16,20},{20,16},{24,28},{28,24},{1,5},{5... | collective-permute-start | bytes 196616 | tf_op jit(solution)/shard_map/ppermute | solution.py:226
  5.8 5.0 %collective-permute-start.1 = (bf16[256,2,128]{0,2,1:T(8,128)(2,1)S(1)}, bf16[256,2,128]{0,2,1:T(8,128)(2,1)S(1)}, u32[]{:S(2)}, u32[]{:S(2)}) collective-permute-start(bf16[256,2,128]{0,2,1:T(8,128)(2,1)S(1)} %copy.28), channel_id=1, source_target_pairs={{0,4},{4,0},{8,12},{12,8},{16,20},{20,16},{24,28},{28,24},{1,5},{5... | collective-permute-start | bytes 393224 | tf_op jit(solution)/shard_map/ppermute | solution.py:226
  10.9 6.1 %collective-permute-start.2 = (bf16[456,256]{1,0:T(8,128)(2,1)S(1)}, bf16[456,256]{1,0:T(8,128)(2,1)S(1)}, u32[]{:S(2)}, u32[]{:S(2)}) collective-permute-start(bf16[456,256]{1,0:T(8,128)(2,1)S(1)} %pad_maximum_fusion), channel_id=1, source_target_pairs={{0,8},{4,12},{8,0},{12,4},{16,24},{20,28},{24,16},{28,20},{1,9},{5... | collective-permute-start | bytes 700424 | tf_op jit(solution)/shard_map/ppermute | solution.py:226
  12.6 4.5 %collective-permute-start.3 = (bf16[384,256]{1,0:T(8,128)(2,1)S(1)}, bf16[384,256]{1,0:T(8,128)(2,1)S(1)}, u32[]{:S(2)}, u32[]{:S(2)}) collective-permute-start(bf16[384,256]{1,0:T(8,128)(2,1)S(1)} %pad_maximum_fusion.1), channel_id=1, source_target_pairs={{8,16},{12,20},{16,8},{20,12},{9,17},{13,21},{17,9},{21,13},{10,18... | collective-permute-start | bytes 589832 | tf_op jit(solution)/shard_map/ppermute | solution.py:232
  17.2 7.4 %collective-permute-start.5 = (bf16[192,256]{1,0:T(8,128)(2,1)S(1)}, bf16[192,256]{1,0:T(8,128)(2,1)S(1)}, u32[]{:S(2)}, u32[]{:S(2)}) collective-permute-start(bf16[192,256]{1,0:T(8,128)(2,1)S(1)} %get-tuple-element.43), channel_id=1, source_target_pairs={{0,3},{1,2},{2,1},{3,0},{4,7},{5,6},{6,5},{7,4},{8,11},{9,10},{10,... | collective-permute-start | bytes 294920 | tf_op jit(solution)/shard_map/ppermute | solution.py:226
  17.3 7.3 %collective-permute-start.4 = (bf16[192,256]{1,0:T(8,128)(2,1)S(1)}, bf16[192,256]{1,0:T(8,128)(2,1)S(1)}, u32[]{:S(2)}, u32[]{:S(2)}) collective-permute-start(bf16[192,256]{1,0:T(8,128)(2,1)S(1)} %get-tuple-element.44), channel_id=1, source_target_pairs={{0,1},{1,0},{2,3},{3,2},{4,5},{5,4},{6,7},{7,6},{8,9},{9,8},{10,11... | collective-permute-start | bytes 294920 | tf_op jit(solution)/shard_map/ppermute | solution.py:226
  18.9 9.7 %collective-permute-start.6 = (bf16[144,256]{1,0:T(8,128)(2,1)S(1)}, bf16[144,256]{1,0:T(8,128)(2,1)S(1)}, u32[]{:S(2)}, u32[]{:S(2)}) collective-permute-start(bf16[144,256]{1,0:T(8,128)(2,1)S(1)} %pad_maximum_fusion.3), channel_id=1, source_target_pairs={{0,16},{4,20},{8,24},{12,28},{16,0},{20,4},{24,8},{28,12},{1,17},{... | collective-permute-start | bytes 221192 | tf_op jit(solution)/shard_map/ppermute | solution.py:226
  26.2 2.6 %collective-permute-start.8 = (f32[9,64,256]{2,1,0:T(8,128)S(1)}, f32[9,64,256]{2,1,0:T(8,128)S(1)}, u32[]{:S(2)}, u32[]{:S(2)}) collective-permute-start(f32[9,64,256]{2,1,0:T(8,128)S(1)} %get-tuple-element.17), channel_id=1, source_target_pairs={{0,1},{1,0},{2,3},{3,2},{4,5},{5,4},{6,7},{7,6},{8,9},{9,8},{10,11... | collective-permute-start | bytes 1769480 | tf_op jit(solution)/shard_map/ppermute | solution.py:226
  28.6 5.9 %collective-permute-start.7 = (bf16[288,256]{1,0:T(8,128)(2,1)S(1)}, bf16[288,256]{1,0:T(8,128)(2,1)S(1)}, u32[]{:S(2)}, u32[]{:S(2)}) collective-permute-start(bf16[288,256]{1,0:T(8,128)(2,1)S(1)} %pad_maximum_fusion.2), channel_id=1, source_target_pairs={{0,3},{1,2},{2,1},{3,0},{4,7},{5,6},{6,5},{7,4},{8,11},{9,10},{10,... | collective-permute-start | bytes 442376 | tf_op jit(solution)/shard_map/ppermute | solution.py:226
  28.9 6.4 %collective-permute-start.12 = (bf16[9,32,256]{2,1,0:T(8,128)(2,1)S(1)}, bf16[9,32,256]{2,1,0:T(8,128)(2,1)S(1)}, u32[]{:S(2)}, u32[]{:S(2)}) collective-permute-start(bf16[9,32,256]{2,1,0:T(8,128)(2,1)S(1)} %get-tuple-element.32), channel_id=1, source_target_pairs={{0,8},{4,12},{8,0},{12,4},{16,24},{20,28},{24,16},{28,20},{1,9},{5... | collective-permute-start | bytes 442376 | tf_op jit(solution)/shard_map/ppermute | solution.py:226
  34.6 1.9 %collective-permute-start.9 = (bf16[9,64,256]{2,1,0:T(8,128)(2,1)S(1)}, bf16[9,64,256]{2,1,0:T(8,128)(2,1)S(1)}, u32[]{:S(2)}, u32[]{:S(2)}) collective-permute-start(bf16[9,64,256]{2,1,0:T(8,128)(2,1)S(1)} %get-tuple-element.51), channel_id=1, source_target_pairs={{0,1},{1,0},{2,3},{3,2},{4,5},{5,4},{6,7},{7,6},{8,9},{9,8},{10,11... | collective-permute-start | bytes 884744 | tf_op jit(solution)/shard_map/ppermute | solution.py:226
  35.3 4.7 %collective-permute-start.13 = (bf16[9,16,256]{2,1,0:T(8,128)(2,1)S(1)}, bf16[9,16,256]{2,1,0:T(8,128)(2,1)S(1)}, u32[]{:S(2)}, u32[]{:S(2)}) collective-permute-start(bf16[9,16,256]{2,1,0:T(8,128)(2,1)S(1)} %get-tuple-element.33), channel_id=1, source_target_pairs={{0,3},{1,2},{2,1},{3,0},{4,7},{5,6},{6,5},{7,4},{8,11},{9,10},{10,... | collective-permute-start | bytes 221192 | tf_op jit(solution)/shard_map/ppermute | solution.py:226
  37.0 8.4 %collective-permute-start.10 = (bf16[256,256]{1,0:T(8,128)(2,1)S(1)}, bf16[256,256]{1,0:T(8,128)(2,1)S(1)}, u32[]{:S(2)}, u32[]{:S(2)}) collective-permute-start(bf16[256,256]{1,0:T(8,128)(2,1)S(1)} %get-tuple-element.25), channel_id=1, source_target_pairs={{0,4},{4,0},{8,12},{12,8},{16,20},{20,16},{24,28},{28,24},{1,5},{5... | collective-permute-start | bytes 393224 | tf_op jit(solution)/shard_map/ppermute | solution.py:226
  40.0 4.3 %collective-permute-start.11 = (bf16[256,128]{1,0:T(8,128)(2,1)S(1)}, bf16[256,128]{1,0:T(8,128)(2,1)S(1)}, u32[]{:S(2)}, u32[]{:S(2)}) collective-permute-start(bf16[256,128]{1,0:T(8,128)(2,1)S(1)} %get-tuple-element.28), channel_id=1, source_target_pairs={{0,4},{4,0},{8,12},{12,8},{16,20},{20,16},{24,28},{28,24},{1,5},{5... | collective-permute-start | bytes 196616 | tf_op jit(solution)/shard_map/ppermute | solution.py:226
  41.8 4.9 %collective-permute-start.14 = (bf16[9,8,256]{2,1,0:T(8,128)(2,1)S(1)}, bf16[9,8,256]{2,1,0:T(8,128)(2,1)S(1)}, u32[]{:S(2)}, u32[]{:S(2)}) collective-permute-start(bf16[9,8,256]{2,1,0:T(8,128)(2,1)S(1)} %fusion.2), channel_id=1, source_target_pairs={{0,16},{4,20},{8,24},{12,28},{16,0},{20,4},{24,8},{28,12},{1,17},{... | collective-permute-start | bytes 110600 | tf_op jit(solution)/shard_map/ppermute | solution.py:226

commit v6 on v5

--- a/solution.py
+++ b/solution.py
@@ -282,13 +282,18 @@
     odd = lay.odd()
     half = channels // 2
 
-    split = features.reshape(half // lay.pair, 2, lay.pair, rows, cols)
-    to_pair = lax.dynamic_index_in_dim(split, 1 - odd, 1, False).reshape(half, rows, cols)
+    split = features.reshape(half // lay.pair, 2, lay.pair * rows, cols)
+    to_pair = lax.dynamic_index_in_dim(split, 1 - odd, 1, False).reshape(half * rows, cols)
     to_keep = lax.dynamic_index_in_dim(split, odd, 1, False).reshape(half, rows, cols)
+
     def channels_last(v):
         return jnp.transpose(v, (1, 2, 0))
 
-    pair = channels_last(swap(to_pair, "lat", 1)), channels_last(swap(cotangent, "lat", 1))
+    def from_pair(v):
+        return channels_last(swap(v.reshape(-1, cols), "lat", 1).reshape(-1, rows, cols))
+
+    pair_cot = from_pair(cotangent)
+    pair = from_pair(to_pair), pair_cot
     mine = channels_last(to_keep), channels_last(cotangent)
 
     far = jnp.abs(jnp.arange(window) - rim)

time: 47.7 us -> 47 us (0.985)
  waiting for transfers between devices: 15.6 us -> 13.1 us
  other arithmetic: 0.42 us -> 1.86 us
    ppermute x14, waiting for transfers between devices: 15.6 us -> 13.1 us  [swap(): lax.ppermute(array, axis, [(i, i ^ stride) for i in range(lax.axis_size(a...]
    unnamed x30 -> x25, local copies, waits for them, and re-layouts: 3.5 us -> 2.59 us
    dynamic_slice x1, local copies, waits for them, and re-layouts: 0.02 us -> 0.89 us  [local(): lax.dynamic_index_in_dim(split, odd, 1, False).reshape(half, rows, cols)]
    select_n x1, other arithmetic: 0.02 us -> 0.8 us  [local(): jnp.where(far[None, None, :] <= half_width[:, None, None], basis_index, -1)]
    le x1, other arithmetic: 0.07 us -> 0.73 us  [local(): far[None, None, :] <= half_width[:, None, None]]
  transfers between devices with their start and end apart: 15 -> 15, of which waited for: 7 -> 6; matrix products, arithmetic and copies ran while one was open for 10% -> 14% of each run, Pallas kernels for 10% -> 11%
where the time goes in v6:
time: 47 us; the launch traced here: 46.6 us
  starting transfers between devices  19.2 us (41%)
  waiting for transfers between devices  13.1 us (28%)
  local copies, waits for them, and re-layouts  6.36 us (14%)
  Pallas kernels  4.97 us (11%)
  other arithmetic  1.86 us (4%)
  between operations  1.09 us (2%)
    ppermute x14, starting transfers between devices, swap(): lax.ppermute(array, axis, [(i, i ^ stride) for i in range(lax.axis_size(a...  18.6 us
    ppermute x14, waiting for transfers between devices, swap(): lax.ppermute(array, axis, [(i, i ^ stride) for i in range(lax.axis_size(a...  13.1 us
    pallas_call x4, Pallas kernels, call(): pl.pallas_call(body, name=name, out_shape=[jax.ShapeDtypeStruct(s, d) for...  4.97 us
    unnamed x25, local copies, waits for them, and re-layouts  2.59 us
    reshape x2, local copies, waits for them, and re-layouts, channels_first(): return jnp.transpose(v.reshape(rows, cols, channels), (2, 0, 1))  1.56 us
  transfers between devices with their start and end apart: 15, of which 6 were waited for; matrix products, arithmetic and copies ran while one was open for 14% of the time, Pallas kernels for 11%

profile of v6, /device:TPU:0, one launch (start us, length us, event | category | flops | bytes accessed | tf_op | source)
XLA Modules:
  0.0 46.6 jit_solution(7158277679270769839)
XLA Ops:
  0.6 0.9 %constant_dynamic-slice_fusion.1 = (bf16[4,1,64,128]{3,2,1,0:T(8,128)(2,1)S(1)}, bf16[4,1,64,128]{3,2,1,0:T(8,128)(2,1)S(1)}) fusion(bf16[4,2,64,128]{3,2,1,0:T(8,128)(2,1)} %bitcast.129, s32[]{:T(128)S(6)} %select_n.48, s32[]{:T(128)S(6)} %select_n.49), kind=kLoop, calls=%fused_computation.91 | loop fusion | bytes 262152 | tf_op jit(solution)/shard_map/jit(dynamic_index_in_dim)/dynamic_slice | solution.py:287
  1.5 3.0 %collective-permute-start = (bf16[256,128]{1,0:T(8,128)(2,1)S(1)}, bf16[256,128]{1,0:T(8,128)(2,1)S(1)}, u32[]{:S(2)}, u32[]{:S(2)}) collective-permute-start(bf16[256,128]{1,0:T(8,128)(2,1)S(1)} %bitcast.136), channel_id=1, source_target_pairs={{0,4},{4,0},{8,12},{12,8},{16,20},{20,16},{24,28},{28,24},{1,5},{5... | collective-permute-start | bytes 196616 | tf_op jit(solution)/shard_map/ppermute | solution.py:226
  4.7 1.0 %copy.24 = bf16[256,2,128]{0,2,1:T(8,128)(2,1)S(1)} copy(bf16[256,2,128]{2,1,0:T(2,128)(2,1)} %param.11) | data formatting | bytes 262144 | tf_op args[5]
  5.7 0.7 %copy.26 = bf16[16,5,33]{2,1,0:T(8,128)(2,1)S(1)} copy(bf16[16,5,33]{2,0,1:T(8,128)(2,1)} %param.8) | data formatting | bytes 10560 | tf_op args[2]
  6.5 0.9 %reshape.96 = bf16[72,256]{1,0:T(8,128)(2,1)S(1)} reshape(bf16[9,2048]{1,0:T(8,128)(2,1)} %param.7) | data formatting | bytes 73728 | tf_op jit(solution)/shard_map/reshape | solution.py:320
  7.5 0.7 %broadcast_compare_fusion = pred[16,33]{1,0:T(8,128)(4,1)S(1)} fusion(s32[33]{0:T(128)S(1)} %add_abs_fusion, s32[16]{0:T(128)} %param.10), kind=kLoop, calls=%fused_computation.88 | loop fusion | flops 528 | bytes 724 | tf_op jit(solution)/shard_map/le | solution.py:300
  8.2 0.8 %copy_select_fusion = s32[16,5,33]{2,1,0:T(8,128)S(1)} fusion(s32[16,5,33]{2,0,1:T(8,128)} %param.9, pred[16,33]{1,0:T(8,128)(4,1)S(1)} %broadcast_compare_fusion), kind=kLoop, calls=%fused_computation.64 | loop fusion | flops 2640 | bytes 21648 | tf_op jit(solution)/shard_map/jit(_where)/select_n | solution.py:300
  9.9 2.0 %collective-permute-start.2 = (bf16[456,256]{1,0:T(8,128)(2,1)S(1)}, bf16[456,256]{1,0:T(8,128)(2,1)S(1)}, u32[]{:S(2)}, u32[]{:S(2)}) collective-permute-start(bf16[456,256]{1,0:T(8,128)(2,1)S(1)} %pad_maximum_fusion), channel_id=1, source_target_pairs={{0,8},{4,12},{8,0},{12,4},{16,24},{20,28},{24,16},{28,20},{1,9},{5... | collective-permute-start | bytes 700424 | tf_op jit(solution)/shard_map/ppermute | solution.py:226
  12.7 4.2 %collective-permute-done.2.refs_2_ = bf16[456,256]{1,0:T(8,128)(2,1)S(1)} collective-permute-done((bf16[456,256]{1,0:T(8,128)(2,1)S(1)}, bf16[456,256]{1,0:T(8,128)(2,1)S(1)}, u32[]{:S(2)}, u32[]{:S(2)}) %collective-permute-start.2) | collective-permute-done | bytes 233504 | tf_op jit(solution)/shard_map/ppermute | solution.py:226
  17.1 1.8 %collective-permute-start.4 = (bf16[192,256]{1,0:T(8,128)(2,1)S(1)}, bf16[192,256]{1,0:T(8,128)(2,1)S(1)}, u32[]{:S(2)}, u32[]{:S(2)}) collective-permute-start(bf16[192,256]{1,0:T(8,128)(2,1)S(1)} %get-tuple-element.44), channel_id=1, source_target_pairs={{0,1},{1,0},{2,3},{3,2},{4,5},{5,4},{6,7},{7,6},{8,9},{9,8},{10,11... | collective-permute-start | bytes 294920 | tf_op jit(solution)/shard_map/ppermute | solution.py:226
  18.9 5.1 %collective-permute-start.6 = (bf16[144,256]{1,0:T(8,128)(2,1)S(1)}, bf16[144,256]{1,0:T(8,128)(2,1)S(1)}, u32[]{:S(2)}, u32[]{:S(2)}) collective-permute-start(bf16[144,256]{1,0:T(8,128)(2,1)S(1)} %pad_maximum_fusion.3), channel_id=1, source_target_pairs={{0,16},{4,20},{8,24},{12,28},{16,0},{20,4},{24,8},{28,12},{1,17},{... | collective-permute-start | bytes 221192 | tf_op jit(solution)/shard_map/ppermute | solution.py:226
  24.0 1.6 %forward.1 = (bf16[9,512,128]{2,1,0:T(8,128)(2,1)S(1)}, f32[9,64,256]{2,1,0:T(8,128)S(1)}, f32[9,64,256]{2,1,0:T(8,128)S(1)}) custom-call(bf16[2,128,128]{2,1,0:T(8,128)(2,1)S(1)} %bitcast.123, bf16[2,128,128]{2,1,0:T(8,128)(2,1)S(1)} %bitcast.125, bf16[456,256]{1,0:T(8,128)(2,1)S(1)} %collective-permute-done.2.refs_2_, ...), custom_call_target="tpu_custom_call" | custom-call | flops 1207959552 | bytes 1081344 | tf_op jit(solution)/shard_map/forward/pallas_call | solution.py:22
  25.7 2.4 %collective-permute-done.6 = bf16[144,256]{1,0:T(8,128)(2,1)S(1)} collective-permute-done((bf16[144,256]{1,0:T(8,128)(2,1)S(1)}, bf16[144,256]{1,0:T(8,128)(2,1)S(1)}, u32[]{:S(2)}, u32[]{:S(2)}) %collective-permute-start.6) | collective-permute-done | bytes 73760 | tf_op jit(solution)/shard_map/ppermute | solution.py:226
  28.3 1.6 %collective-permute-start.12 = (bf16[9,32,256]{2,1,0:T(8,128)(2,1)S(1)}, bf16[9,32,256]{2,1,0:T(8,128)(2,1)S(1)}, u32[]{:S(2)}, u32[]{:S(2)}) collective-permute-start(bf16[9,32,256]{2,1,0:T(8,128)(2,1)S(1)} %get-tuple-element.32), channel_id=1, source_target_pairs={{0,8},{4,12},{8,0},{12,4},{16,24},{20,28},{24,16},{28,20},{1,9},{5... | collective-permute-start | bytes 442376 | tf_op jit(solution)/shard_map/ppermute | solution.py:226
  29.9 3.5 %collective-permute-done.7 = bf16[288,256]{1,0:T(8,128)(2,1)S(1)} collective-permute-done((bf16[288,256]{1,0:T(8,128)(2,1)S(1)}, bf16[288,256]{1,0:T(8,128)(2,1)S(1)}, u32[]{:S(2)}, u32[]{:S(2)}) %collective-permute-start.7) | collective-permute-done | bytes 147488 | tf_op jit(solution)/shard_map/ppermute | solution.py:226
  33.6 1.1 %collective-permute-done.12 = bf16[9,32,256]{2,1,0:T(8,128)(2,1)S(1)} collective-permute-done((bf16[9,32,256]{2,1,0:T(8,128)(2,1)S(1)}, bf16[9,32,256]{2,1,0:T(8,128)(2,1)S(1)}, u32[]{:S(2)}, u32[]{:S(2)}) %collective-permute-start.12) | collective-permute-done | bytes 147488 | tf_op jit(solution)/shard_map/ppermute | solution.py:226
  35.7 1.3 %collective-permute-start.10 = (bf16[256,256]{1,0:T(8,128)(2,1)S(1)}, bf16[256,256]{1,0:T(8,128)(2,1)S(1)}, u32[]{:S(2)}, u32[]{:S(2)}) collective-permute-start(bf16[256,256]{1,0:T(8,128)(2,1)S(1)} %get-tuple-element.25), channel_id=1, source_target_pairs={{0,4},{4,0},{8,12},{12,8},{16,20},{20,16},{24,28},{28,24},{1,5},{5... | collective-permute-start | bytes 393224 | tf_op jit(solution)/shard_map/ppermute | solution.py:226
  37.0 2.6 %backward.1 = (bf16[256,128]{1,0:T(8,128)(2,1)S(1)}, bf16[256,128]{1,0:T(8,128)(2,1)S(1)}) custom-call(bf16[2,128,256]{2,1,0:T(8,128)(2,1)S(1)} %bitcast.116, bf16[2,128,256]{2,1,0:T(8,128)(2,1)S(1)} %bitcast.120, bf16[456,256]{1,0:T(8,128)(2,1)S(1)} %collective-permute-done.2.refs_2_, bf16[384,256]{1,0:T(8,128)(2,1)S(1)} %collective-permute-done.3.refs_3_, ...), custom_call_target="tpu_custom_call" | custom-call | flops 3623878656 | bytes 1540096 | tf_op jit(solution)/shard_map/backward/pallas_call | solution.py:22
  39.6 0.9 %collective-permute-start.11 = (bf16[256,128]{1,0:T(8,128)(2,1)S(1)}, bf16[256,128]{1,0:T(8,128)(2,1)S(1)}, u32[]{:S(2)}, u32[]{:S(2)}) collective-permute-start(bf16[256,128]{1,0:T(8,128)(2,1)S(1)} %get-tuple-element.28), channel_id=1, source_target_pairs={{0,4},{4,0},{8,12},{12,8},{16,20},{20,16},{24,28},{28,24},{1,5},{5... | collective-permute-start | bytes 196616 | tf_op jit(solution)/shard_map/ppermute | solution.py:226
  40.5 2.0 %collective-permute-start.14 = (bf16[9,8,256]{2,1,0:T(8,128)(2,1)S(1)}, bf16[9,8,256]{2,1,0:T(8,128)(2,1)S(1)}, u32[]{:S(2)}, u32[]{:S(2)}) collective-permute-start(bf16[9,8,256]{2,1,0:T(8,128)(2,1)S(1)} %fusion.2), channel_id=1, source_target_pairs={{0,16},{4,20},{8,24},{12,28},{16,0},{20,4},{24,8},{28,12},{1,17},{... | collective-permute-start | bytes 110600 | tf_op jit(solution)/shard_map/ppermute | solution.py:226
  42.6 1.3 %collective-permute-done.11.refs_1_ = bf16[256,128]{1,0:T(8,128)(2,1)S(1)} collective-permute-done((bf16[256,128]{1,0:T(8,128)(2,1)S(1)}, bf16[256,128]{1,0:T(8,128)(2,1)S(1)}, u32[]{:S(2)}, u32[]{:S(2)}) %collective-permute-start.11) | collective-permute-done | bytes 65568 | tf_op jit(solution)/shard_map/ppermute | solution.py:226
  44.2 0.8 %copy.29 = bf16[2,128,256]{1,0,2:T(2,128)(2,1)} copy(bf16[2,128,256]{2,1,0:T(8,128)(2,1)S(1)} %bitcast.121) | data formatting | bytes 262144 | tf_op jit(solution)/shard_map/reshape | solution.py:383
  45.0 0.8 %copy.28 = bf16[2,128,256]{1,0,2:T(2,128)(2,1)} copy(bf16[2,128,256]{2,1,0:T(8,128)(2,1)S(1)} %bitcast.127) | data formatting | bytes 262144 | tf_op jit(solution)/shard_map/reshape | solution.py:383
  45.9 0.7 %copy.30 = f32[2,8,8,256]{3,1,2,0:T(8,128)} copy(f32[2,8,8,256]{3,2,1,0:T(8,128)S(1)} %bitcast.126) | data formatting | bytes 262144
  (73 shorter events, 3.8 us)
Async XLA Ops:
  1.5 7.5 %collective-permute-start = (bf16[256,128]{1,0:T(8,128)(2,1)S(1)}, bf16[256,128]{1,0:T(8,128)(2,1)S(1)}, u32[]{:S(2)}, u32[]{:S(2)}) collective-permute-start(bf16[256,128]{1,0:T(8,128)(2,1)S(1)} %bitcast.136), channel_id=1, source_target_pairs={{0,4},{4,0},{8,12},{12,8},{16,20},{20,16},{24,28},{28,24},{1,5},{5... | collective-permute-start | bytes 196616 | tf_op jit(solution)/shard_map/ppermute | solution.py:226
  4.6 5.2 %collective-permute-start.1 = (bf16[512,128]{1,0:T(8,128)(2,1)}, bf16[512,128]{1,0:T(8,128)(2,1)S(1)}, u32[]{:S(2)}, u32[]{:S(2)}) collective-permute-start(bf16[512,128]{1,0:T(8,128)(2,1)} %bitcast.130), channel_id=1, source_target_pairs={{0,4},{4,0},{8,12},{12,8},{16,20},{20,16},{24,28},{28,24},{1,5},{5... | collective-permute-start | bytes 393224 | tf_op jit(solution)/shard_map/ppermute | solution.py:226
  9.9 6.9 %collective-permute-start.2 = (bf16[456,256]{1,0:T(8,128)(2,1)S(1)}, bf16[456,256]{1,0:T(8,128)(2,1)S(1)}, u32[]{:S(2)}, u32[]{:S(2)}) collective-permute-start(bf16[456,256]{1,0:T(8,128)(2,1)S(1)} %pad_maximum_fusion), channel_id=1, source_target_pairs={{0,8},{4,12},{8,0},{12,4},{16,24},{20,28},{24,16},{28,20},{1,9},{5... | collective-permute-start | bytes 700424 | tf_op jit(solution)/shard_map/ppermute | solution.py:226
  12.0 4.9 %collective-permute-start.3 = (bf16[384,256]{1,0:T(8,128)(2,1)S(1)}, bf16[384,256]{1,0:T(8,128)(2,1)S(1)}, u32[]{:S(2)}, u32[]{:S(2)}) collective-permute-start(bf16[384,256]{1,0:T(8,128)(2,1)S(1)} %pad_maximum_fusion.1), channel_id=1, source_target_pairs={{8,16},{12,20},{16,8},{20,12},{9,17},{13,21},{17,9},{21,13},{10,18... | collective-permute-start | bytes 589832 | tf_op jit(solution)/shard_map/ppermute | solution.py:232
  17.0 7.0 %collective-permute-start.5 = (bf16[192,256]{1,0:T(8,128)(2,1)S(1)}, bf16[192,256]{1,0:T(8,128)(2,1)S(1)}, u32[]{:S(2)}, u32[]{:S(2)}) collective-permute-start(bf16[192,256]{1,0:T(8,128)(2,1)S(1)} %get-tuple-element.43), channel_id=1, source_target_pairs={{0,3},{1,2},{2,1},{3,0},{4,7},{5,6},{6,5},{7,4},{8,11},{9,10},{10,... | collective-permute-start | bytes 294920 | tf_op jit(solution)/shard_map/ppermute | solution.py:226
  17.1 6.9 %collective-permute-start.4 = (bf16[192,256]{1,0:T(8,128)(2,1)S(1)}, bf16[192,256]{1,0:T(8,128)(2,1)S(1)}, u32[]{:S(2)}, u32[]{:S(2)}) collective-permute-start(bf16[192,256]{1,0:T(8,128)(2,1)S(1)} %get-tuple-element.44), channel_id=1, source_target_pairs={{0,1},{1,0},{2,3},{3,2},{4,5},{5,4},{6,7},{7,6},{8,9},{9,8},{10,11... | collective-permute-start | bytes 294920 | tf_op jit(solution)/shard_map/ppermute | solution.py:226
  18.9 9.1 %collective-permute-start.6 = (bf16[144,256]{1,0:T(8,128)(2,1)S(1)}, bf16[144,256]{1,0:T(8,128)(2,1)S(1)}, u32[]{:S(2)}, u32[]{:S(2)}) collective-permute-start(bf16[144,256]{1,0:T(8,128)(2,1)S(1)} %pad_maximum_fusion.3), channel_id=1, source_target_pairs={{0,16},{4,20},{8,24},{12,28},{16,0},{20,4},{24,8},{28,12},{1,17},{... | collective-permute-start | bytes 221192 | tf_op jit(solution)/shard_map/ppermute | solution.py:226
  25.6 2.6 %collective-permute-start.8 = (f32[9,64,256]{2,1,0:T(8,128)S(1)}, f32[9,64,256]{2,1,0:T(8,128)S(1)}, u32[]{:S(2)}, u32[]{:S(2)}) collective-permute-start(f32[9,64,256]{2,1,0:T(8,128)S(1)} %get-tuple-element.17), channel_id=1, source_target_pairs={{0,1},{1,0},{2,3},{3,2},{4,5},{5,4},{6,7},{7,6},{8,9},{9,8},{10,11... | collective-permute-start | bytes 1769480 | tf_op jit(solution)/shard_map/ppermute | solution.py:226
  28.1 5.3 %collective-permute-start.7 = (bf16[288,256]{1,0:T(8,128)(2,1)S(1)}, bf16[288,256]{1,0:T(8,128)(2,1)S(1)}, u32[]{:S(2)}, u32[]{:S(2)}) collective-permute-start(bf16[288,256]{1,0:T(8,128)(2,1)S(1)} %pad_maximum_fusion.2), channel_id=1, source_target_pairs={{0,3},{1,2},{2,1},{3,0},{4,7},{5,6},{6,5},{7,4},{8,11},{9,10},{10,... | collective-permute-start | bytes 442376 | tf_op jit(solution)/shard_map/ppermute | solution.py:226
  28.3 6.4 %collective-permute-start.12 = (bf16[9,32,256]{2,1,0:T(8,128)(2,1)S(1)}, bf16[9,32,256]{2,1,0:T(8,128)(2,1)S(1)}, u32[]{:S(2)}, u32[]{:S(2)}) collective-permute-start(bf16[9,32,256]{2,1,0:T(8,128)(2,1)S(1)} %get-tuple-element.32), channel_id=1, source_target_pairs={{0,8},{4,12},{8,0},{12,4},{16,24},{20,28},{24,16},{28,20},{1,9},{5... | collective-permute-start | bytes 442376 | tf_op jit(solution)/shard_map/ppermute | solution.py:226
  33.4 1.8 %collective-permute-start.9 = (bf16[9,64,256]{2,1,0:T(8,128)(2,1)S(1)}, bf16[9,64,256]{2,1,0:T(8,128)(2,1)S(1)}, u32[]{:S(2)}, u32[]{:S(2)}) collective-permute-start(bf16[9,64,256]{2,1,0:T(8,128)(2,1)S(1)} %get-tuple-element.51), channel_id=1, source_target_pairs={{0,1},{1,0},{2,3},{3,2},{4,5},{5,4},{6,7},{7,6},{8,9},{9,8},{10,11... | collective-permute-start | bytes 884744 | tf_op jit(solution)/shard_map/ppermute | solution.py:226
  34.8 4.8 %collective-permute-start.13 = (bf16[9,16,256]{2,1,0:T(8,128)(2,1)S(1)}, bf16[9,16,256]{2,1,0:T(8,128)(2,1)S(1)}, u32[]{:S(2)}, u32[]{:S(2)}) collective-permute-start(bf16[9,16,256]{2,1,0:T(8,128)(2,1)S(1)} %get-tuple-element.33), channel_id=1, source_target_pairs={{0,3},{1,2},{2,1},{3,0},{4,7},{5,6},{6,5},{7,4},{8,11},{9,10},{10,... | collective-permute-start | bytes 221192 | tf_op jit(solution)/shard_map/ppermute | solution.py:226
  35.7 9.3 %collective-permute-start.10 = (bf16[256,256]{1,0:T(8,128)(2,1)S(1)}, bf16[256,256]{1,0:T(8,128)(2,1)S(1)}, u32[]{:S(2)}, u32[]{:S(2)}) collective-permute-start(bf16[256,256]{1,0:T(8,128)(2,1)S(1)} %get-tuple-element.25), channel_id=1, source_target_pairs={{0,4},{4,0},{8,12},{12,8},{16,20},{20,16},{24,28},{28,24},{1,5},{5... | collective-permute-start | bytes 393224 | tf_op jit(solution)/shard_map/ppermute | solution.py:226
  39.6 4.3 %collective-permute-start.11 = (bf16[256,128]{1,0:T(8,128)(2,1)S(1)}, bf16[256,128]{1,0:T(8,128)(2,1)S(1)}, u32[]{:S(2)}, u32[]{:S(2)}) collective-permute-start(bf16[256,128]{1,0:T(8,128)(2,1)S(1)} %get-tuple-element.28), channel_id=1, source_target_pairs={{0,4},{4,0},{8,12},{12,8},{16,20},{20,16},{24,28},{28,24},{1,5},{5... | collective-permute-start | bytes 196616 | tf_op jit(solution)/shard_map/ppermute | solution.py:226
  40.5 5.3 %collective-permute-start.14 = (bf16[9,8,256]{2,1,0:T(8,128)(2,1)S(1)}, bf16[9,8,256]{2,1,0:T(8,128)(2,1)S(1)}, u32[]{:S(2)}, u32[]{:S(2)}) collective-permute-start(bf16[9,8,256]{2,1,0:T(8,128)(2,1)S(1)} %fusion.2), channel_id=1, source_target_pairs={{0,16},{4,20},{8,24},{12,28},{16,0},{20,4},{24,8},{28,12},{1,17},{... | collective-permute-start | bytes 110600 | tf_op jit(solution)/shard_map/ppermute | solution.py:226

commit v7 on v6

--- a/solution.py
+++ b/solution.py
@@ -17,7 +17,7 @@
     return lax.dot_general(a, b, dims, preferred_element_type=f32)
 
 
-def call(body, name, flops, outs, *args, scratch=()):
+def call(body, name, outs, *args, scratch=()):
     in_vmem = pl.BlockSpec(memory_space=pltpu.VMEM)
     return pl.pallas_call(
         body,
@@ -26,9 +26,6 @@
         in_specs=[in_vmem for _ in args],
         out_specs=[in_vmem for _ in outs],
         scratch_shapes=list(scratch),
-        cost_estimate=pl.CostEstimate(
-            flops=flops, transcendentals=0, bytes_accessed=sum(v.size * v.dtype.itemsize for v in args)
-        ),
         compiler_params=pltpu.CompilerParams(vmem_limit_bytes=VMEM),
     )(*args)
 
@@ -332,7 +329,7 @@
     cells = rows * cols
     ext = (4 * rows, cols + 2 * rim)
     basis_out, send, keep = call(
-        lambda *refs: forward_body(lay, offsets, *refs), "forward", 16 * basis_count * cells * half * channels,
+        lambda *refs: forward_body(lay, offsets, *refs), "forward",
         [((basis_count, 2 * cells, half), bf16), ((basis_count, half // 2, channels), f32),
          ((basis_count, half // 2, channels), f32)],
         mine[0], pair[0], near, far, core, cross, taps, index, mine[1], pair[1],
@@ -356,12 +353,12 @@
                 full = jnp.concatenate([v.reshape(basis_count, lay.own, channels) for v in blocks], axis=1)
             full = widen(full, gather[-1])
             own_out, pair_out = call(
-                mix_body, "mix", 4 * basis_count * cells * half * channels, [((cells, channels), f32), ((cells, channels), bf16)], full, basis_out
+                mix_body, "mix", [((cells, channels), f32), ((cells, channels), bf16)], full, basis_out
             )
             mine_after = after(mine[1], pair_out)
             pair_out = swap(pair_out, "lat", 1)
             own_grad, pair_grad = call(
-                lambda *refs: backward_body(lay, offsets, *refs), "backward", 48 * basis_count * cells * half * channels,
+                lambda *refs: backward_body(lay, offsets, *refs), "backward",
                 [((cells, half), bf16), ((cells, half), bf16)],
                 mine_after, pair[1], near, far, core, cross, taps, index, full,
                 scratch=[pltpu.VMEM((*ext, channels), bf16),
@@ -376,7 +373,7 @@
             keep = terms[0][:, :size] + terms[1][:, :size]
     output = (own_out + pair_out).astype(bf16)
     (input_grad,) = call(
-        lambda *refs: finish_body(lay, *refs), "finish", 4 * cells * half * channels, [((cells, channels), bf16)], own_grad, pair_grad
+        lambda *refs: finish_body(lay, *refs), "finish", [((cells, channels), bf16)], own_grad, pair_grad
     )
 
     def channels_first(v):

time: 47 us -> 46.8 us (level)
  no operation moved by 1% of the time
where the time goes in v7:
time: 46.8 us; the launch traced here: 46.5 us
  starting transfers between devices  19.3 us (41%)
  waiting for transfers between devices  12.9 us (28%)
  local copies, waits for them, and re-layouts  6.33 us (14%)
  Pallas kernels  4.98 us (11%)
  other arithmetic  1.86 us (4%)
  between operations  1.12 us (2%)
    ppermute x14, starting transfers between devices, swap(): lax.ppermute(array, axis, [(i, i ^ stride) for i in range(lax.axis_size(a...  18.6 us
    ppermute x14, waiting for transfers between devices, swap(): lax.ppermute(array, axis, [(i, i ^ stride) for i in range(lax.axis_size(a...  12.9 us
    pallas_call x4, Pallas kernels, call(): pl.pallas_call(body, name=name, out_shape=[jax.ShapeDtypeStruct(s, d) for...  4.98 us
    unnamed x25, local copies, waits for them, and re-layouts  2.56 us
    reshape x2, local copies, waits for them, and re-layouts, channels_first(): return jnp.transpose(v.reshape(rows, cols, channels), (2, 0, 1))  1.56 us
  transfers between devices with their start and end apart: 15, of which 6 were waited for; matrix products, arithmetic and copies ran while one was open for 14% of the time, Pallas kernels for 11%

profile of v7, /device:TPU:0, one launch (start us, length us, event | category | flops | bytes accessed | tf_op | source)
XLA Modules:
  0.0 46.5 jit_solution(6633122822286529120)
XLA Ops:
  0.6 0.9 %constant_dynamic-slice_fusion.1 = (bf16[4,1,64,128]{3,2,1,0:T(8,128)(2,1)S(1)}, bf16[4,1,64,128]{3,2,1,0:T(8,128)(2,1)S(1)}) fusion(bf16[4,2,64,128]{3,2,1,0:T(8,128)(2,1)} %bitcast.129, s32[]{:T(128)S(6)} %select_n.48, s32[]{:T(128)S(6)} %select_n.49), kind=kLoop, calls=%fused_computation.91 | loop fusion | bytes 262152 | tf_op jit(solution)/shard_map/jit(dynamic_index_in_dim)/dynamic_slice | solution.py:284
  1.5 3.0 %collective-permute-start = (bf16[256,128]{1,0:T(8,128)(2,1)S(1)}, bf16[256,128]{1,0:T(8,128)(2,1)S(1)}, u32[]{:S(2)}, u32[]{:S(2)}) collective-permute-start(bf16[256,128]{1,0:T(8,128)(2,1)S(1)} %bitcast.136), channel_id=1, source_target_pairs={{0,4},{4,0},{8,12},{12,8},{16,20},{20,16},{24,28},{28,24},{1,5},{5... | collective-permute-start | bytes 196616 | tf_op jit(solution)/shard_map/ppermute | solution.py:223
  4.8 0.7 %broadcast_compare_fusion = pred[16,33]{1,0:T(8,128)(4,1)S(1)} fusion(s32[33]{0:T(128)S(1)} %add_abs_fusion, s32[16]{0:T(128)} %param.10), kind=kLoop, calls=%fused_computation.88 | loop fusion | flops 528 | bytes 724 | tf_op jit(solution)/shard_map/le | solution.py:297
  5.5 0.8 %copy_select_fusion = s32[16,5,33]{2,1,0:T(8,128)S(1)} fusion(s32[16,5,33]{2,0,1:T(8,128)} %param.9, pred[16,33]{1,0:T(8,128)(4,1)S(1)} %broadcast_compare_fusion), kind=kLoop, calls=%fused_computation.64 | loop fusion | flops 2640 | bytes 21648 | tf_op jit(solution)/shard_map/jit(_where)/select_n | solution.py:297
  6.3 1.0 %copy.24 = bf16[256,2,128]{0,2,1:T(8,128)(2,1)S(1)} copy(bf16[256,2,128]{2,1,0:T(2,128)(2,1)} %param.11) | data formatting | bytes 262144 | tf_op args[5]
  7.4 0.7 %copy.26 = bf16[16,5,33]{2,1,0:T(8,128)(2,1)S(1)} copy(bf16[16,5,33]{2,0,1:T(8,128)(2,1)} %param.8) | data formatting | bytes 10560 | tf_op args[2]
  8.1 0.9 %reshape.96 = bf16[72,256]{1,0:T(8,128)(2,1)S(1)} reshape(bf16[9,2048]{1,0:T(8,128)(2,1)} %param.7) | data formatting | bytes 73728 | tf_op jit(solution)/shard_map/reshape | solution.py:317
  10.0 2.0 %collective-permute-start.2 = (bf16[456,256]{1,0:T(8,128)(2,1)S(1)}, bf16[456,256]{1,0:T(8,128)(2,1)S(1)}, u32[]{:S(2)}, u32[]{:S(2)}) collective-permute-start(bf16[456,256]{1,0:T(8,128)(2,1)S(1)} %pad_maximum_fusion), channel_id=1, source_target_pairs={{0,8},{4,12},{8,0},{12,4},{16,24},{20,28},{24,16},{28,20},{1,9},{5... | collective-permute-start | bytes 700424 | tf_op jit(solution)/shard_map/ppermute | solution.py:223
  12.7 4.2 %collective-permute-done.2.refs_2_ = bf16[456,256]{1,0:T(8,128)(2,1)S(1)} collective-permute-done((bf16[456,256]{1,0:T(8,128)(2,1)S(1)}, bf16[456,256]{1,0:T(8,128)(2,1)S(1)}, u32[]{:S(2)}, u32[]{:S(2)}) %collective-permute-start.2) | collective-permute-done | bytes 233504 | tf_op jit(solution)/shard_map/ppermute | solution.py:223
  17.1 1.8 %collective-permute-start.4 = (bf16[192,256]{1,0:T(8,128)(2,1)S(1)}, bf16[192,256]{1,0:T(8,128)(2,1)S(1)}, u32[]{:S(2)}, u32[]{:S(2)}) collective-permute-start(bf16[192,256]{1,0:T(8,128)(2,1)S(1)} %get-tuple-element.44), channel_id=1, source_target_pairs={{0,1},{1,0},{2,3},{3,2},{4,5},{5,4},{6,7},{7,6},{8,9},{9,8},{10,11... | collective-permute-start | bytes 294920 | tf_op jit(solution)/shard_map/ppermute | solution.py:223
  18.9 5.0 %collective-permute-start.6 = (bf16[144,256]{1,0:T(8,128)(2,1)S(1)}, bf16[144,256]{1,0:T(8,128)(2,1)S(1)}, u32[]{:S(2)}, u32[]{:S(2)}) collective-permute-start(bf16[144,256]{1,0:T(8,128)(2,1)S(1)} %pad_maximum_fusion.3), channel_id=1, source_target_pairs={{0,16},{4,20},{8,24},{12,28},{16,0},{20,4},{24,8},{28,12},{1,17},{... | collective-permute-start | bytes 221192 | tf_op jit(solution)/shard_map/ppermute | solution.py:223
  24.0 1.6 %forward.1 = (bf16[9,512,128]{2,1,0:T(8,128)(2,1)S(1)}, f32[9,64,256]{2,1,0:T(8,128)S(1)}, f32[9,64,256]{2,1,0:T(8,128)S(1)}) custom-call(bf16[2,128,128]{2,1,0:T(8,128)(2,1)S(1)} %bitcast.122, bf16[2,128,128]{2,1,0:T(8,128)(2,1)S(1)} %bitcast.124, bf16[456,256]{1,0:T(8,128)(2,1)S(1)} %collective-permute-done.2.refs_2_, ...), custom_call_target="tpu_custom_call" | custom-call | tf_op jit(solution)/shard_map/forward/pallas_call | solution.py:22
  25.6 2.3 %collective-permute-done.6 = bf16[144,256]{1,0:T(8,128)(2,1)S(1)} collective-permute-done((bf16[144,256]{1,0:T(8,128)(2,1)S(1)}, bf16[144,256]{1,0:T(8,128)(2,1)S(1)}, u32[]{:S(2)}, u32[]{:S(2)}) %collective-permute-start.6) | collective-permute-done | bytes 73760 | tf_op jit(solution)/shard_map/ppermute | solution.py:223
  28.2 1.7 %collective-permute-start.12 = (bf16[9,32,256]{2,1,0:T(8,128)(2,1)S(1)}, bf16[9,32,256]{2,1,0:T(8,128)(2,1)S(1)}, u32[]{:S(2)}, u32[]{:S(2)}) collective-permute-start(bf16[9,32,256]{2,1,0:T(8,128)(2,1)S(1)} %get-tuple-element.32), channel_id=1, source_target_pairs={{0,8},{4,12},{8,0},{12,4},{16,24},{20,28},{24,16},{28,20},{1,9},{5... | collective-permute-start | bytes 442376 | tf_op jit(solution)/shard_map/ppermute | solution.py:223
  29.9 3.4 %collective-permute-done.7 = bf16[288,256]{1,0:T(8,128)(2,1)S(1)} collective-permute-done((bf16[288,256]{1,0:T(8,128)(2,1)S(1)}, bf16[288,256]{1,0:T(8,128)(2,1)S(1)}, u32[]{:S(2)}, u32[]{:S(2)}) %collective-permute-start.7) | collective-permute-done | bytes 147488 | tf_op jit(solution)/shard_map/ppermute | solution.py:223
  33.5 1.1 %collective-permute-done.12 = bf16[9,32,256]{2,1,0:T(8,128)(2,1)S(1)} collective-permute-done((bf16[9,32,256]{2,1,0:T(8,128)(2,1)S(1)}, bf16[9,32,256]{2,1,0:T(8,128)(2,1)S(1)}, u32[]{:S(2)}, u32[]{:S(2)}) %collective-permute-start.12) | collective-permute-done | bytes 147488 | tf_op jit(solution)/shard_map/ppermute | solution.py:223
  35.7 1.2 %collective-permute-start.10 = (bf16[256,256]{1,0:T(8,128)(2,1)S(1)}, bf16[256,256]{1,0:T(8,128)(2,1)S(1)}, u32[]{:S(2)}, u32[]{:S(2)}) collective-permute-start(bf16[256,256]{1,0:T(8,128)(2,1)S(1)} %get-tuple-element.25), channel_id=1, source_target_pairs={{0,4},{4,0},{8,12},{12,8},{16,20},{20,16},{24,28},{28,24},{1,5},{5... | collective-permute-start | bytes 393224 | tf_op jit(solution)/shard_map/ppermute | solution.py:223
  36.9 2.6 %backward.1 = (bf16[256,128]{1,0:T(8,128)(2,1)S(1)}, bf16[256,128]{1,0:T(8,128)(2,1)S(1)}) custom-call(bf16[2,128,256]{2,1,0:T(8,128)(2,1)S(1)} %bitcast.116, bf16[2,128,256]{2,1,0:T(8,128)(2,1)S(1)} %bitcast.120, bf16[456,256]{1,0:T(8,128)(2,1)S(1)} %collective-permute-done.2.refs_2_, bf16[384,256]{1,0:T(8,128)(2,1)S(1)} %collective-permute-done.3.refs_3_, ...), custom_call_target="tpu_custom_call" | custom-call | tf_op jit(solution)/shard_map/backward/pallas_call | solution.py:22
  39.5 0.9 %collective-permute-start.11 = (bf16[256,128]{1,0:T(8,128)(2,1)S(1)}, bf16[256,128]{1,0:T(8,128)(2,1)S(1)}, u32[]{:S(2)}, u32[]{:S(2)}) collective-permute-start(bf16[256,128]{1,0:T(8,128)(2,1)S(1)} %get-tuple-element.28), channel_id=1, source_target_pairs={{0,4},{4,0},{8,12},{12,8},{16,20},{20,16},{24,28},{28,24},{1,5},{5... | collective-permute-start | bytes 196616 | tf_op jit(solution)/shard_map/ppermute | solution.py:223
  40.4 2.1 %collective-permute-start.14 = (bf16[9,8,256]{2,1,0:T(8,128)(2,1)S(1)}, bf16[9,8,256]{2,1,0:T(8,128)(2,1)S(1)}, u32[]{:S(2)}, u32[]{:S(2)}) collective-permute-start(bf16[9,8,256]{2,1,0:T(8,128)(2,1)S(1)} %fusion.2), channel_id=1, source_target_pairs={{0,16},{4,20},{8,24},{12,28},{16,0},{20,4},{24,8},{28,12},{1,17},{... | collective-permute-start | bytes 110600 | tf_op jit(solution)/shard_map/ppermute | solution.py:223
  42.6 1.2 %collective-permute-done.11.refs_1_ = bf16[256,128]{1,0:T(8,128)(2,1)S(1)} collective-permute-done((bf16[256,128]{1,0:T(8,128)(2,1)S(1)}, bf16[256,128]{1,0:T(8,128)(2,1)S(1)}, u32[]{:S(2)}, u32[]{:S(2)}) %collective-permute-start.11) | collective-permute-done | bytes 65568 | tf_op jit(solution)/shard_map/ppermute | solution.py:223
  44.1 0.8 %copy.29 = bf16[2,128,256]{1,0,2:T(2,128)(2,1)} copy(bf16[2,128,256]{2,1,0:T(8,128)(2,1)S(1)} %bitcast.125) | data formatting | bytes 262144 | tf_op jit(solution)/shard_map/reshape | solution.py:380
  44.9 0.8 %copy.28 = bf16[2,128,256]{1,0,2:T(2,128)(2,1)} copy(bf16[2,128,256]{2,1,0:T(8,128)(2,1)S(1)} %bitcast.127) | data formatting | bytes 262144 | tf_op jit(solution)/shard_map/reshape | solution.py:380
  45.8 0.7 %copy.30 = f32[2,8,8,256]{3,1,2,0:T(8,128)} copy(f32[2,8,8,256]{3,2,1,0:T(8,128)S(1)} %bitcast.126) | data formatting | bytes 262144
  (73 shorter events, 3.8 us)
Async XLA Ops:
  1.5 7.5 %collective-permute-start = (bf16[256,128]{1,0:T(8,128)(2,1)S(1)}, bf16[256,128]{1,0:T(8,128)(2,1)S(1)}, u32[]{:S(2)}, u32[]{:S(2)}) collective-permute-start(bf16[256,128]{1,0:T(8,128)(2,1)S(1)} %bitcast.136), channel_id=1, source_target_pairs={{0,4},{4,0},{8,12},{12,8},{16,20},{20,16},{24,28},{28,24},{1,5},{5... | collective-permute-start | bytes 196616 | tf_op jit(solution)/shard_map/ppermute | solution.py:223
  4.6 5.2 %collective-permute-start.1 = (bf16[512,128]{1,0:T(8,128)(2,1)}, bf16[512,128]{1,0:T(8,128)(2,1)S(1)}, u32[]{:S(2)}, u32[]{:S(2)}) collective-permute-start(bf16[512,128]{1,0:T(8,128)(2,1)} %bitcast.130), channel_id=1, source_target_pairs={{0,4},{4,0},{8,12},{12,8},{16,20},{20,16},{24,28},{28,24},{1,5},{5... | collective-permute-start | bytes 393224 | tf_op jit(solution)/shard_map/ppermute | solution.py:223
  10.0 6.9 %collective-permute-start.2 = (bf16[456,256]{1,0:T(8,128)(2,1)S(1)}, bf16[456,256]{1,0:T(8,128)(2,1)S(1)}, u32[]{:S(2)}, u32[]{:S(2)}) collective-permute-start(bf16[456,256]{1,0:T(8,128)(2,1)S(1)} %pad_maximum_fusion), channel_id=1, source_target_pairs={{0,8},{4,12},{8,0},{12,4},{16,24},{20,28},{24,16},{28,20},{1,9},{5... | collective-permute-start | bytes 700424 | tf_op jit(solution)/shard_map/ppermute | solution.py:223
  12.0 4.9 %collective-permute-start.3 = (bf16[384,256]{1,0:T(8,128)(2,1)S(1)}, bf16[384,256]{1,0:T(8,128)(2,1)S(1)}, u32[]{:S(2)}, u32[]{:S(2)}) collective-permute-start(bf16[384,256]{1,0:T(8,128)(2,1)S(1)} %pad_maximum_fusion.1), channel_id=1, source_target_pairs={{8,16},{12,20},{16,8},{20,12},{9,17},{13,21},{17,9},{21,13},{10,18... | collective-permute-start | bytes 589832 | tf_op jit(solution)/shard_map/ppermute | solution.py:229
  17.1 6.9 %collective-permute-start.5 = (bf16[192,256]{1,0:T(8,128)(2,1)S(1)}, bf16[192,256]{1,0:T(8,128)(2,1)S(1)}, u32[]{:S(2)}, u32[]{:S(2)}) collective-permute-start(bf16[192,256]{1,0:T(8,128)(2,1)S(1)} %get-tuple-element.43), channel_id=1, source_target_pairs={{0,3},{1,2},{2,1},{3,0},{4,7},{5,6},{6,5},{7,4},{8,11},{9,10},{10,... | collective-permute-start | bytes 294920 | tf_op jit(solution)/shard_map/ppermute | solution.py:223
  17.1 6.8 %collective-permute-start.4 = (bf16[192,256]{1,0:T(8,128)(2,1)S(1)}, bf16[192,256]{1,0:T(8,128)(2,1)S(1)}, u32[]{:S(2)}, u32[]{:S(2)}) collective-permute-start(bf16[192,256]{1,0:T(8,128)(2,1)S(1)} %get-tuple-element.44), channel_id=1, source_target_pairs={{0,1},{1,0},{2,3},{3,2},{4,5},{5,4},{6,7},{7,6},{8,9},{9,8},{10,11... | collective-permute-start | bytes 294920 | tf_op jit(solution)/shard_map/ppermute | solution.py:223
  18.9 9.0 %collective-permute-start.6 = (bf16[144,256]{1,0:T(8,128)(2,1)S(1)}, bf16[144,256]{1,0:T(8,128)(2,1)S(1)}, u32[]{:S(2)}, u32[]{:S(2)}) collective-permute-start(bf16[144,256]{1,0:T(8,128)(2,1)S(1)} %pad_maximum_fusion.3), channel_id=1, source_target_pairs={{0,16},{4,20},{8,24},{12,28},{16,0},{20,4},{24,8},{28,12},{1,17},{... | collective-permute-start | bytes 221192 | tf_op jit(solution)/shard_map/ppermute | solution.py:223
  25.5 2.5 %collective-permute-start.8 = (f32[9,64,256]{2,1,0:T(8,128)S(1)}, f32[9,64,256]{2,1,0:T(8,128)S(1)}, u32[]{:S(2)}, u32[]{:S(2)}) collective-permute-start(f32[9,64,256]{2,1,0:T(8,128)S(1)} %get-tuple-element.17), channel_id=1, source_target_pairs={{0,1},{1,0},{2,3},{3,2},{4,5},{5,4},{6,7},{7,6},{8,9},{9,8},{10,11... | collective-permute-start | bytes 1769480 | tf_op jit(solution)/shard_map/ppermute | solution.py:223
  28.0 5.3 %collective-permute-start.7 = (bf16[288,256]{1,0:T(8,128)(2,1)S(1)}, bf16[288,256]{1,0:T(8,128)(2,1)S(1)}, u32[]{:S(2)}, u32[]{:S(2)}) collective-permute-start(bf16[288,256]{1,0:T(8,128)(2,1)S(1)} %pad_maximum_fusion.2), channel_id=1, source_target_pairs={{0,3},{1,2},{2,1},{3,0},{4,7},{5,6},{6,5},{7,4},{8,11},{9,10},{10,... | collective-permute-start | bytes 442376 | tf_op jit(solution)/shard_map/ppermute | solution.py:223
  28.2 6.4 %collective-permute-start.12 = (bf16[9,32,256]{2,1,0:T(8,128)(2,1)S(1)}, bf16[9,32,256]{2,1,0:T(8,128)(2,1)S(1)}, u32[]{:S(2)}, u32[]{:S(2)}) collective-permute-start(bf16[9,32,256]{2,1,0:T(8,128)(2,1)S(1)} %get-tuple-element.32), channel_id=1, source_target_pairs={{0,8},{4,12},{8,0},{12,4},{16,24},{20,28},{24,16},{28,20},{1,9},{5... | collective-permute-start | bytes 442376 | tf_op jit(solution)/shard_map/ppermute | solution.py:223
  33.4 1.7 %collective-permute-start.9 = (bf16[9,64,256]{2,1,0:T(8,128)(2,1)S(1)}, bf16[9,64,256]{2,1,0:T(8,128)(2,1)S(1)}, u32[]{:S(2)}, u32[]{:S(2)}) collective-permute-start(bf16[9,64,256]{2,1,0:T(8,128)(2,1)S(1)} %get-tuple-element.51), channel_id=1, source_target_pairs={{0,1},{1,0},{2,3},{3,2},{4,5},{5,4},{6,7},{7,6},{8,9},{9,8},{10,11... | collective-permute-start | bytes 884744 | tf_op jit(solution)/shard_map/ppermute | solution.py:223
  34.7 4.8 %collective-permute-start.13 = (bf16[9,16,256]{2,1,0:T(8,128)(2,1)S(1)}, bf16[9,16,256]{2,1,0:T(8,128)(2,1)S(1)}, u32[]{:S(2)}, u32[]{:S(2)}) collective-permute-start(bf16[9,16,256]{2,1,0:T(8,128)(2,1)S(1)} %get-tuple-element.33), channel_id=1, source_target_pairs={{0,3},{1,2},{2,1},{3,0},{4,7},{5,6},{6,5},{7,4},{8,11},{9,10},{10,... | collective-permute-start | bytes 221192 | tf_op jit(solution)/shard_map/ppermute | solution.py:223
  35.7 9.2 %collective-permute-start.10 = (bf16[256,256]{1,0:T(8,128)(2,1)S(1)}, bf16[256,256]{1,0:T(8,128)(2,1)S(1)}, u32[]{:S(2)}, u32[]{:S(2)}) collective-permute-start(bf16[256,256]{1,0:T(8,128)(2,1)S(1)} %get-tuple-element.25), channel_id=1, source_target_pairs={{0,4},{4,0},{8,12},{12,8},{16,20},{20,16},{24,28},{28,24},{1,5},{5... | collective-permute-start | bytes 393224 | tf_op jit(solution)/shard_map/ppermute | solution.py:223
  39.5 4.3 %collective-permute-start.11 = (bf16[256,128]{1,0:T(8,128)(2,1)S(1)}, bf16[256,128]{1,0:T(8,128)(2,1)S(1)}, u32[]{:S(2)}, u32[]{:S(2)}) collective-permute-start(bf16[256,128]{1,0:T(8,128)(2,1)S(1)} %get-tuple-element.28), channel_id=1, source_target_pairs={{0,4},{4,0},{8,12},{12,8},{16,20},{20,16},{24,28},{28,24},{1,5},{5... | collective-permute-start | bytes 196616 | tf_op jit(solution)/shard_map/ppermute | solution.py:223
  40.4 5.3 %collective-permute-start.14 = (bf16[9,8,256]{2,1,0:T(8,128)(2,1)S(1)}, bf16[9,8,256]{2,1,0:T(8,128)(2,1)S(1)}, u32[]{:S(2)}, u32[]{:S(2)}) collective-permute-start(bf16[9,8,256]{2,1,0:T(8,128)(2,1)S(1)} %fusion.2), channel_id=1, source_target_pairs={{0,16},{4,20},{8,24},{12,28},{16,0},{20,4},{24,8},{28,12},{1,17},{... | collective-permute-start | bytes 110600 | tf_op jit(solution)/shard_map/ppermute | solution.py:223
